TPU v7x, 256 devices: a whole 4x4x8 slice. The times are simulated.
256 devices in a mesh: dp: 16 (over y, x), expert: 16 (over z, core).
Axes of the slice: x: 4, y: 4, z: 8, core: 2. Of those that a mesh axis runs over, the one named last changes fastest.
Arguments:
- tokens: bfloat16 [16384, 2048], P(('dp', 'expert')), may hold values from -6 to 6
- expert_ids: int32 [16384, 8], P(('dp', 'expert')), may hold values from 0 to 127, all different within a row; in each aligned block of 32 rows (0 to 31, 32 to 63, ...) at most 3 rows name the same one
- gate_fixed: int32 [16384, 8], P(('dp', 'expert')), may hold values from 1 to 65535
- w_gate: bfloat16 [256, 2048, 384], P(('dp', 'expert')), may hold values from -0.125 to 0.125
- w_up: bfloat16 [256, 2048, 384], P(('dp', 'expert')), may hold values from -0.125 to 0.125
- w_down: bfloat16 [256, 384, 2048], P(('dp', 'expert')), may hold values from -0.21875 to 0.21875
Outputs:
- mixed: float32 [16384, 2048], P(('dp', 'expert'))
Inputs may be any that keep to these rules, and one draw needn't show every extreme that they name: `expert_ids`: each row names 8 different experts. In each aligned block of 32 rows (the first or the second half of one device's rows) no expert is named by more than 3 rows, a bound that some block reaches.
All inputs are finite; a program needn't handle non-finite values.
Results may differ from a plain program's by a relative error of at most 0.0041.
Values may be sent and summed in bfloat16 or wider, within the bound.
No kernel may reach another device: no remote copies, remote signals or barrier semaphores. Data moves between devices by JAX's collectives and lax.ppermute only.
A program may use at most 64 MiB of HBM per device.

v0:
```python
import functools

import jax
import jax.numpy as jnp
from jax import lax
from jax.experimental import pallas as pl
from jax.experimental.pallas import tpu as pltpu
from jax.sharding import PartitionSpec as P

F32 = jnp.float32
BF16 = jnp.bfloat16
EXTRA = 128
VMEM = pl.BlockSpec(memory_space=pltpu.VMEM)
SMEM = pl.BlockSpec(memory_space=pltpu.SMEM)
HBM = pl.BlockSpec(memory_space=pltpu.HBM)
PIECE = 128
PARAMS = pltpu.CompilerParams(vmem_limit_bytes=24 << 20)


def on_chip(x):
    return pltpu.with_memory_space_constraint(x, pltpu.VMEM)


def off_chip(x):
    return pltpu.with_memory_space_constraint(x, pltpu.HBM)


def after(x, *others):
    return lax.optimization_barrier((x,) + others)[0]


def kernel_call(
    body, name, outs, arrays, scalars=(), keep=(), specs=None, out_specs=None, scratch=()
):
    keep = list(keep) + [jax.ShapeDtypeStruct] * (len(outs) - len(keep))
    return pl.pallas_call(
        body,
        out_shape=[where(*out) for where, out in zip(keep, outs)],
        in_specs=[SMEM] * len(scalars) + (specs or [VMEM] * len(arrays)),
        out_specs=out_specs or [VMEM] * len(outs),
        scratch_shapes=list(scratch),
        compiler_params=PARAMS,
        name=name,
    )(*scalars, *arrays)


def slot_of(index, slots):
    group = jnp.zeros_like(index)
    for d in range(1, 16):
        group = group + (index >= d * slots).astype(jnp.int32)
    return group, index - group * slots


def pack_kernel(tokens_ref, ids_ref, gates_ref, out_ref):
    rows, width = tokens_ref.shape
    gates = gates_ref[...]
    columns = [ids_ref[...], gates >> 8, gates & 255]
    top = jnp.concatenate(columns, axis=0).astype(F32)
    top = jnp.concatenate([top, jnp.zeros((top.shape[0], EXTRA - rows), F32)], axis=1)
    extra = jnp.concatenate([top, jnp.zeros((EXTRA - top.shape[0], EXTRA), F32)], axis=0).T
    out_ref[:, :width] = tokens_ref[...]
    out_ref[:, width:] = extra[:rows, :].astype(BF16)


def dispatch_kernel(slots, planes, z_ref, *refs):
    refs, (out_ref, extra_ref, piece_ref, sems) = refs[:-4], refs[-4:]
    width = out_ref.shape[1]
    groups = out_ref.shape[0] // slots
    extra = jnp.concatenate([x[:, width:] for x in refs], axis=0)
    extra_ref[...] = extra
    extra = extra.astype(F32).T
    tokens = extra.shape[1]
    dest = planes * lax.broadcasted_iota(jnp.int32, (groups, 1), 0) + z_ref[0]
    dest = dest.astype(F32)
    match = jnp.zeros((groups, tokens), F32)
    for k in range(8):
        match = match + (extra[k : k + 1, :] == dest).astype(F32)
    upper = lax.broadcasted_iota(jnp.int32, (tokens, tokens), 0) <= lax.broadcasted_iota(
        jnp.int32, (tokens, tokens), 1
    )
    upper = upper.astype(F32).astype(BF16)
    order = jnp.dot(match.astype(BF16), upper, preferred_element_type=F32) * match
    row = lax.broadcasted_iota(jnp.int32, (groups * slots, 1), 0)
    group, place = slot_of(row, slots)
    spread = (group == lax.broadcasted_iota(jnp.int32, (1, groups), 1)).astype(F32).astype(BF16)
    wanted = jnp.dot(spread, order.astype(BF16), preferred_element_type=F32)
    pick = (wanted == (place + 1).astype(F32)).astype(F32).astype(BF16)
    rows = jnp.concatenate([x[:, :width] for x in refs], axis=0)
    copies = []
    for i in range(out_ref.shape[0] // PIECE):
        here = pl.ds(i * PIECE, PIECE)
        part = pick[i * PIECE : (i + 1) * PIECE, :]
        piece_ref[here, :] = jnp.dot(part, rows, preferred_element_type=F32).astype(BF16)
        copies.append(pltpu.make_async_copy(piece_ref.at[here], out_ref.at[here], sems.at[i]))
        copies[-1].start()
    for copy in copies:
        copy.wait()


def expert_kernel(x_hbm, g0, u0, g1, u1, d0, d1, out_hbm, x_ref, wide, tall, out_ref, sems, out_sems):
    units = g0.shape[1]
    ends = [(x_hbm, x_ref)]
    ends += [(w, wide.at[:, pl.ds(i * units, units)]) for i, w in enumerate((g0, u0, g1, u1))]
    ends += [(w, tall.at[pl.ds(i * units, units)]) for i, w in enumerate((d0, d1))]
    loads = [pltpu.make_async_copy(a, b, sems.at[i]) for i, (a, b) in enumerate(ends)]
    for load in loads:
        load.start()
    loads[0].wait()
    x = x_ref[...]
    hidden = []
    for i in (0, 2):
        loads[1 + i].wait()
        loads[2 + i].wait()
        both = jnp.dot(
            x, wide[:, i * units : (i + 2) * units], preferred_element_type=F32
        )
        gate, up = both[:, :units], both[:, units:]
        hidden.append((gate / (1.0 + jnp.exp(-gate)) * up).astype(BF16))
    hidden = jnp.concatenate(hidden, axis=1)
    loads[5].wait()
    loads[6].wait()
    copies = []
    for i in range(out_ref.shape[0] // PIECE):
        here = pl.ds(i * PIECE, PIECE)
        total = jnp.dot(
            hidden[i * PIECE : (i + 1) * PIECE, :], tall[...], preferred_element_type=F32
        )
        out_ref[here, :] = total.astype(BF16)
        copies.append(pltpu.make_async_copy(out_ref.at[here], out_hbm.at[here], out_sems.at[i]))
        copies[-1].start()
    for copy in copies:
        copy.wait()


def weights_kernel(slots, planes, z_ref, extra_ref, high_ref, low_ref):
    tokens, columns = high_ref.shape
    groups = columns // slots
    extra = extra_ref[...].astype(F32)
    gates = extra[:, 8:16] * 256.0 + extra[:, 16:24]
    mix = gates / jnp.sum(gates, axis=1, keepdims=True)
    dest = planes * lax.broadcasted_iota(jnp.int32, (1, EXTRA), 1) + z_ref[0]
    dest = dest.astype(F32)
    match = jnp.zeros((tokens, EXTRA), F32)
    weight = jnp.zeros((tokens, EXTRA), F32)
    for k in range(8):
        same = extra[:, k : k + 1] == dest
        match = match + same.astype(F32)
        weight = weight + jnp.where(same, mix[:, k : k + 1], 0.0)
    lower = lax.broadcasted_iota(jnp.int32, (tokens, tokens), 1) <= lax.broadcasted_iota(
        jnp.int32, (tokens, tokens), 0
    )
    lower = lower.astype(F32).astype(BF16)
    order = jnp.dot(lower, match.astype(BF16), preferred_element_type=F32) * match
    column = lax.broadcasted_iota(jnp.int32, (1, groups * slots), 1)
    group, place = slot_of(column, slots)
    spread = (group == lax.broadcasted_iota(jnp.int32, (EXTRA, 1), 0)).astype(F32).astype(BF16)
    wanted = jnp.dot(order.astype(BF16), spread, preferred_element_type=F32)
    here = wanted == (place + 1).astype(F32)
    high = weight.astype(BF16)
    low = (weight - high.astype(F32)).astype(BF16)
    for piece, ref in ((high, high_ref), (low, low_ref)):
        wide = jnp.dot(piece, spread, preferred_element_type=F32)
        ref[...] = jnp.where(here, wide, 0.0).astype(BF16)


def combine_kernel(home_ref, high_ref, low_ref, *outs):
    home = home_ref[...]
    total = jnp.dot(high_ref[...], home, preferred_element_type=F32)
    total = total + jnp.dot(low_ref[...], home, preferred_element_type=F32)
    start = 0
    for out in outs:
        rows = out.shape[0]
        out[...] = total[start : start + rows, :].astype(out.dtype)
        start += rows


def per_device(tokens, expert_ids, gate_fixed, w_gate, w_up, w_down):
    col_count = lax.axis_size("expert")
    dp_count = lax.axis_size("dp")
    planes = col_count // 2
    half = planes // 2
    rows, width = tokens.shape
    chunk = half * rows
    slots = 3 * chunk // 32
    sent = dp_count * slots
    plane = (lax.axis_index("expert") // 2).astype(jnp.int32).reshape(1)

    def along_z(x, by):
        return lax.ppermute(
            x, "expert", [(i, (i + 2 * by) % col_count) for i in range(col_count)]
        )

    def partner(x):
        return lax.ppermute(x, "expert", [(i, i ^ 1) for i in range(col_count)])

    def exchange(x):
        return lax.all_to_all(x, "dp", split_axis=0, concat_axis=0, tiled=True)

    pieces = sent // PIECE
    moved = ((sent, width), BF16)

    def dispatch(shards):
        return kernel_call(
            functools.partial(dispatch_kernel, slots, planes),
            "dispatch",
            [moved, ((chunk, EXTRA), BF16)],
            [on_chip(x) for x in shards],
            [plane],
            keep=[pltpu.HBM],
            out_specs=[HBM, VMEM],
            scratch=[pltpu.VMEM(*moved), pltpu.SemaphoreType.DMA((pieces,))],
        )

    def mixing(extra):
        return kernel_call(
            functools.partial(weights_kernel, slots, planes),
            "mixing",
            [((chunk, sent), BF16)] * 2,
            [extra],
            [plane],
        )

    panels = []
    for w in (w_gate[0], w_up[0], w_down[0]):
        panels += [w, partner(w)]
    g0, g1, u0, u1, d0, d1 = panels

    def expert(x):
        return kernel_call(
            expert_kernel,
            "expert",
            [moved],
            [off_chip(w) for w in (x, g0, u0, g1, u1, d0, d1)],
            keep=[pltpu.HBM],
            specs=[HBM] * 7,
            out_specs=[HBM],
            scratch=[
                pltpu.VMEM(*moved),
                pltpu.VMEM((g0.shape[0], 4 * g0.shape[1]), BF16),
                pltpu.VMEM((2 * d0.shape[0], d0.shape[1]), BF16),
                pltpu.VMEM(*moved),
                pltpu.SemaphoreType.DMA((7,)),
                pltpu.SemaphoreType.DMA((pieces,)),
            ],
        )[0]

    def combine(home, mix, kinds):
        outs = [((rows, width), kind) for kind in kinds]
        return kernel_call(combine_kernel, "combine", outs, [home] + list(mix), keep=[pltpu.VMEM] * 4)

    def plus(x, part):
        return (x.astype(F32) + part).astype(BF16)

    mine = kernel_call(
        pack_kernel,
        "pack",
        [((rows, width + EXTRA), BF16)],
        [off_chip(x) for x in (tokens, expert_ids.T, gate_fixed.T)],
        keep=[pltpu.VMEM],
    )[0]
    low_1, high_1 = along_z(mine, 1), along_z(mine, -1)
    low_2, high_2 = along_z(low_1, 1), along_z(high_1, -1)
    low_3, high_3 = along_z(low_2, 1), along_z(high_2, -1)
    low_4 = along_z(low_3, 1)

    near_rows, near_extra = dispatch([mine, low_1, high_1, low_2])
    near = off_chip(exchange(after(near_rows, high_2)))
    far_rows, far_extra = dispatch([high_2, low_3, high_3, low_4])
    near = after(near, far_rows)
    far = exchange(far_rows)
    near_out = after(expert(near), far)
    near_mix, far_mix = mixing(near_extra), mixing(far_extra)
    far_out = after(expert(far), near_out, *near_mix, *far_mix)
    far_home = exchange(far_out)
    near_home = exchange(after(near_out, far_home))
    to_high_2, to_low_3, to_high_3, to_low_4 = combine(far_home, far_mix, [F32, F32, BF16, BF16])
    down, up = along_z(to_low_4, -1), along_z(to_high_3, 1)
    down, up = along_z(plus(down, to_low_3), -1), along_z(plus(up, to_high_2), 1)
    near_home = after(near_home, down, up)
    own, to_low_1, to_high_1, to_low_2 = combine(near_home, near_mix, [F32] * 4)
    down, up = along_z(plus(down, to_low_2), -1), along_z(plus(up, to_high_1), 1)
    down = along_z(plus(down, to_low_1), -1)
    return own + up.astype(F32) + down.astype(F32)


def solution(mesh):
    rows = P(("dp", "expert"), None)
    panels = P(("dp", "expert"), None, None)
    return jax.shard_map(
        per_device,
        mesh=mesh,
        in_specs=(rows, rows, rows, panels, panels, panels),
        out_specs=rows,
        check_vma=False,
    )
```

profile of v0, /device:TPU:96, one launch (start us, length us, event | category | flops | bytes accessed | tf_op | source)
XLA Modules:
  0.0 155.5 jit_solution(9133121796907750948)
XLA Ops:
  1.1 3.2 %collective-permute-start = (bf16[64,2176]{1,0:T(8,128)(2,1)S(1)}, bf16[64,2176]{1,0:T(8,128)(2,1)S(1)}, u32[]{:S(2)}, u32[]{:S(2)}) collective-permute-start(bf16[64,2176]{1,0:T(8,128)(2,1)S(1)} %pack.1.refs_0_), channel_id=1, source_target_pairs={{0,2},{1,3},{2,4},{3,5},{4,6},{5,7},{6,8},{7,9},{8,10},{9,11},{10,... | collective-permute-start | bytes 835592 | tf_op jit(solution)/shard_map/ppermute | solution.py:189
  4.3 5.9 %collective-permute-done.refs_1_ = bf16[64,2176]{1,0:T(8,128)(2,1)S(1)} collective-permute-done((bf16[64,2176]{1,0:T(8,128)(2,1)S(1)}, bf16[64,2176]{1,0:T(8,128)(2,1)S(1)}, u32[]{:S(2)}, u32[]{:S(2)}) %collective-permute-start) | collective-permute-done | bytes 278560 | tf_op jit(solution)/shard_map/ppermute | solution.py:189
  10.2 3.7 %collective-permute-start.2 = (bf16[64,2176]{1,0:T(8,128)(2,1)S(1)}, bf16[64,2176]{1,0:T(8,128)(2,1)S(1)}, u32[]{:S(2)}, u32[]{:S(2)}) collective-permute-start(bf16[64,2176]{1,0:T(8,128)(2,1)S(1)} %collective-permute-done.refs_1_), channel_id=1, source_target_pairs={{0,2},{1,3},{2,4},{3,5},{4,6},{5,7},{6,8},{7,9},{8,10},{9,11},{10,... | collective-permute-start | bytes 835592 | tf_op jit(solution)/shard_map/ppermute | solution.py:189
  13.9 5.0 %collective-permute-done.2.refs_3_ = bf16[64,2176]{1,0:T(8,128)(2,1)S(1)} collective-permute-done((bf16[64,2176]{1,0:T(8,128)(2,1)S(1)}, bf16[64,2176]{1,0:T(8,128)(2,1)S(1)}, u32[]{:S(2)}, u32[]{:S(2)}) %collective-permute-start.2) | collective-permute-done | bytes 278560 | tf_op jit(solution)/shard_map/ppermute | solution.py:189
  22.3 7.2 %all-to-all-start = ((bf16[16,24,2048]{2,1,0:T(8,128)(2,1)}), bf16[16,24,2048]{2,1,0:T(8,128)(2,1)}, u32[]{:S(2)}, u32[]{:S(2)}) async-start(bf16[16,24,2048]{2,1,0:T(8,128)(2,1)} %bitcast.27), calls=%async_computation | async-start | bytes 3145728 | tf_op jit(solution)/shard_map/all_to_all | solution.py:197
  29.6 2.3 %collective-permute-start.4 = (bf16[64,2176]{1,0:T(8,128)(2,1)S(1)}, bf16[64,2176]{1,0:T(8,128)(2,1)S(1)}, u32[]{:S(2)}, u32[]{:S(2)}) collective-permute-start(bf16[64,2176]{1,0:T(8,128)(2,1)S(1)} %collective-permute-done.2.refs_3_), channel_id=1, source_target_pairs={{0,2},{1,3},{2,4},{3,5},{4,6},{5,7},{6,8},{7,9},{8,10},{9,11},{10,... | collective-permute-start | bytes 835592 | tf_op jit(solution)/shard_map/ppermute | solution.py:189
  31.8 5.1 %collective-permute-done.4.refs_1_ = bf16[64,2176]{1,0:T(8,128)(2,1)S(1)} collective-permute-done((bf16[64,2176]{1,0:T(8,128)(2,1)S(1)}, bf16[64,2176]{1,0:T(8,128)(2,1)S(1)}, u32[]{:S(2)}, u32[]{:S(2)}) %collective-permute-start.4) | collective-permute-done | bytes 278560 | tf_op jit(solution)/shard_map/ppermute | solution.py:189
  36.9 2.7 %collective-permute-start.6 = (bf16[64,2176]{1,0:T(8,128)(2,1)S(1)}, bf16[64,2176]{1,0:T(8,128)(2,1)S(1)}, u32[]{:S(2)}, u32[]{:S(2)}) collective-permute-start(bf16[64,2176]{1,0:T(8,128)(2,1)S(1)} %collective-permute-done.4.refs_1_), channel_id=1, source_target_pairs={{0,2},{1,3},{2,4},{3,5},{4,6},{5,7},{6,8},{7,9},{8,10},{9,11},{10,... | collective-permute-start | bytes 835592 | tf_op jit(solution)/shard_map/ppermute | solution.py:189
  40.1 3.5 %collective-permute-done.6.refs_3_ = bf16[64,2176]{1,0:T(8,128)(2,1)S(1)} collective-permute-done((bf16[64,2176]{1,0:T(8,128)(2,1)S(1)}, bf16[64,2176]{1,0:T(8,128)(2,1)S(1)}, u32[]{:S(2)}, u32[]{:S(2)}) %collective-permute-start.6) | collective-permute-done | bytes 278560 | tf_op jit(solution)/shard_map/ppermute | solution.py:189
  45.5 5.9 %all-to-all-done = bf16[16,24,2048]{2,1,0:T(8,128)(2,1)} async-done(((bf16[16,24,2048]{2,1,0:T(8,128)(2,1)}), bf16[16,24,2048]{2,1,0:T(8,128)(2,1)}, u32[]{:S(2)}, u32[]{:S(2)}) %all-to-all-start) | async-done | bytes 1572896 | tf_op jit(solution)/shard_map/all_to_all | solution.py:197
  51.3 4.6 %all-to-all-start.1 = ((bf16[16,24,2048]{2,1,0:T(8,128)(2,1)}), bf16[16,24,2048]{2,1,0:T(8,128)(2,1)}, u32[]{:S(2)}, u32[]{:S(2)}) async-start(bf16[16,24,2048]{2,1,0:T(8,128)(2,1)} %bitcast.28), calls=%async_computation.1 | async-start | bytes 3145728 | tf_op jit(solution)/shard_map/all_to_all | solution.py:197
  59.4 8.2 %expert.2 = bf16[384,2048]{1,0:T(8,128)(2,1)} custom-call(bf16[384,2048]{1,0:T(8,128)(2,1)} %bitcast.4.x_hbm, bf16[2048,384]{1,0:T(8,128)(2,1)} %bitcast.16, bf16[2048,384]{1,0:T(8,128)(2,1)} %bitcast.20, bf16[2048,384]{1,0:T(8,128)(2,1)} %collective-permute-done.7.g1, bf16[2048,384]{1,0:T(8,128)(2,1)} %collective-permute-done.8.u1, ...), custom_call_target="tpu_custom_call" | custom-call | tf_op jit(solution)/shard_map/expert/pallas_call | solution.py:36
  67.7 9.7 %all-to-all-done.1 = bf16[16,24,2048]{2,1,0:T(8,128)(2,1)} async-done(((bf16[16,24,2048]{2,1,0:T(8,128)(2,1)}), bf16[16,24,2048]{2,1,0:T(8,128)(2,1)}, u32[]{:S(2)}, u32[]{:S(2)}) %all-to-all-start.1) | async-done | bytes 1572896 | tf_op jit(solution)/shard_map/all_to_all | solution.py:197
  77.4 8.2 %expert.3 = bf16[384,2048]{1,0:T(8,128)(2,1)} custom-call(bf16[384,2048]{1,0:T(8,128)(2,1)} %bitcast.9.x_hbm, bf16[2048,384]{1,0:T(8,128)(2,1)} %bitcast.17, bf16[2048,384]{1,0:T(8,128)(2,1)} %bitcast.21, bf16[2048,384]{1,0:T(8,128)(2,1)} %collective-permute-done.7.g1, bf16[2048,384]{1,0:T(8,128)(2,1)} %collective-permute-done.8.u1, ...), custom_call_target="tpu_custom_call" | custom-call | tf_op jit(solution)/shard_map/expert/pallas_call | solution.py:36
  85.7 24.6 %all_to_all.46 = bf16[16,24,2048]{2,1,0:T(8,128)(2,1)S(1)} all-to-all(bf16[16,24,2048]{2,1,0:T(8,128)(2,1)} %bitcast.26), channel_id=1, replica_groups=mesh['dp'=16,'expert'=16] {'dp'}, dimensions={0} | all-to-all | bytes 3145728 | tf_op jit(solution)/shard_map/all_to_all | solution.py:197
  110.2 3.7 %all-to-all-start.3 = ((bf16[16,24,2048]{2,1,0:T(8,128)(2,1)}), bf16[16,24,2048]{2,1,0:T(8,128)(2,1)S(1)}, u32[]{:S(2)}, u32[]{:S(2)}) async-start(bf16[16,24,2048]{2,1,0:T(8,128)(2,1)} %bitcast.25), calls=%async_computation.3 | async-start | bytes 3145728 | tf_op jit(solution)/shard_map/all_to_all | solution.py:197
  117.1 2.6 %collective-permute-start.12 = (bf16[64,2048]{1,0:T(8,128)(2,1)S(1)}, bf16[64,2048]{1,0:T(8,128)(2,1)S(1)}, u32[]{:S(2)}, u32[]{:S(2)}) collective-permute-start(bf16[64,2048]{1,0:T(8,128)(2,1)S(1)} %get-tuple-element.42), channel_id=1, source_target_pairs={{0,2},{1,3},{2,4},{3,5},{4,6},{5,7},{6,8},{7,9},{8,10},{9,11},{10,... | collective-permute-start | bytes 786440 | tf_op jit(solution)/shard_map/ppermute | solution.py:189
  119.6 5.5 %collective-permute-done.12 = bf16[64,2048]{1,0:T(8,128)(2,1)S(1)} collective-permute-done((bf16[64,2048]{1,0:T(8,128)(2,1)S(1)}, bf16[64,2048]{1,0:T(8,128)(2,1)S(1)}, u32[]{:S(2)}, u32[]{:S(2)}) %collective-permute-start.12) | collective-permute-done | bytes 262176 | tf_op jit(solution)/shard_map/ppermute | solution.py:189
  125.2 2.5 %collective-permute-start.13 = (bf16[64,2048]{1,0:T(8,128)(2,1)S(1)}, bf16[64,2048]{1,0:T(8,128)(2,1)S(1)}, u32[]{:S(2)}, u32[]{:S(2)}) collective-permute-start(bf16[64,2048]{1,0:T(8,128)(2,1)S(1)} %add_convert_fusion.3), channel_id=1, source_target_pairs={{0,2},{1,3},{2,4},{3,5},{4,6},{5,7},{6,8},{7,9},{8,10},{9,11},{10,... | collective-permute-start | bytes 786440 | tf_op jit(solution)/shard_map/ppermute | solution.py:189
  127.8 3.8 %collective-permute-done.13 = bf16[64,2048]{1,0:T(8,128)(2,1)S(1)} collective-permute-done((bf16[64,2048]{1,0:T(8,128)(2,1)S(1)}, bf16[64,2048]{1,0:T(8,128)(2,1)S(1)}, u32[]{:S(2)}, u32[]{:S(2)}) %collective-permute-start.13) | collective-permute-done | bytes 262176 | tf_op jit(solution)/shard_map/ppermute | solution.py:189
  131.6 3.8 %collective-permute-done.11 = bf16[64,2048]{1,0:T(8,128)(2,1)S(1)} collective-permute-done((bf16[64,2048]{1,0:T(8,128)(2,1)S(1)}, bf16[64,2048]{1,0:T(8,128)(2,1)S(1)}, u32[]{:S(2)}, u32[]{:S(2)}) %collective-permute-start.11) | collective-permute-done | bytes 262176 | tf_op jit(solution)/shard_map/ppermute | solution.py:189
  136.9 3.3 %collective-permute-start.14 = (bf16[64,2048]{1,0:T(8,128)(2,1)S(1)}, bf16[64,2048]{1,0:T(8,128)(2,1)S(1)}, u32[]{:S(2)}, u32[]{:S(2)}) collective-permute-start(bf16[64,2048]{1,0:T(8,128)(2,1)S(1)} %add_convert_fusion.2), channel_id=1, source_target_pairs={{0,2},{1,3},{2,4},{3,5},{4,6},{5,7},{6,8},{7,9},{8,10},{9,11},{10,... | collective-permute-start | bytes 786440 | tf_op jit(solution)/shard_map/ppermute | solution.py:189
  140.2 6.7 %collective-permute-done.15 = bf16[64,2048]{1,0:T(8,128)(2,1)S(1)} collective-permute-done((bf16[64,2048]{1,0:T(8,128)(2,1)S(1)}, bf16[64,2048]{1,0:T(8,128)(2,1)S(1)}, u32[]{:S(2)}, u32[]{:S(2)}) %collective-permute-start.15) | collective-permute-done | bytes 262176 | tf_op jit(solution)/shard_map/ppermute | solution.py:189
  147.1 7.6 %collective-permute-done.16 = bf16[64,2048]{1,0:T(8,128)(2,1)S(1)} collective-permute-done((bf16[64,2048]{1,0:T(8,128)(2,1)S(1)}, bf16[64,2048]{1,0:T(8,128)(2,1)S(1)}, u32[]{:S(2)}, u32[]{:S(2)}) %collective-permute-start.16) | collective-permute-done | bytes 262176 | tf_op jit(solution)/shard_map/ppermute | solution.py:189
  (42 shorter events, 16.1 us)
Async XLA Ops:
  1.1 9.1 %collective-permute-start = (bf16[64,2176]{1,0:T(8,128)(2,1)S(1)}, bf16[64,2176]{1,0:T(8,128)(2,1)S(1)}, u32[]{:S(2)}, u32[]{:S(2)}) collective-permute-start(bf16[64,2176]{1,0:T(8,128)(2,1)S(1)} %pack.1.refs_0_), channel_id=1, source_target_pairs={{0,2},{1,3},{2,4},{3,5},{4,6},{5,7},{6,8},{7,9},{8,10},{9,11},{10,... | collective-permute-start | bytes 835592 | tf_op jit(solution)/shard_map/ppermute | solution.py:189
  4.3 9.6 %collective-permute-start.1 = (bf16[64,2176]{1,0:T(8,128)(2,1)S(1)}, bf16[64,2176]{1,0:T(8,128)(2,1)S(1)}, u32[]{:S(2)}, u32[]{:S(2)}) collective-permute-start(bf16[64,2176]{1,0:T(8,128)(2,1)S(1)} %pack.1.refs_0_), channel_id=1, source_target_pairs={{0,14},{1,15},{2,0},{3,1},{4,2},{5,3},{6,4},{7,5},{8,6},{9,7},{10,... | collective-permute-start | bytes 835592 | tf_op jit(solution)/shard_map/ppermute | solution.py:189
  10.2 8.7 %collective-permute-start.2 = (bf16[64,2176]{1,0:T(8,128)(2,1)S(1)}, bf16[64,2176]{1,0:T(8,128)(2,1)S(1)}, u32[]{:S(2)}, u32[]{:S(2)}) collective-permute-start(bf16[64,2176]{1,0:T(8,128)(2,1)S(1)} %collective-permute-done.refs_1_), channel_id=1, source_target_pairs={{0,2},{1,3},{2,4},{3,5},{4,6},{5,7},{6,8},{7,9},{8,10},{9,11},{10,... | collective-permute-start | bytes 835592 | tf_op jit(solution)/shard_map/ppermute | solution.py:189
  13.9 8.5 %collective-permute-start.3 = (bf16[64,2176]{1,0:T(8,128)(2,1)S(1)}, bf16[64,2176]{1,0:T(8,128)(2,1)S(1)}, u32[]{:S(2)}, u32[]{:S(2)}) collective-permute-start(bf16[64,2176]{1,0:T(8,128)(2,1)S(1)} %collective-permute-done.1.refs_2_), channel_id=1, source_target_pairs={{0,14},{1,15},{2,0},{3,1},{4,2},{5,3},{6,4},{7,5},{8,6},{9,7},{10,... | collective-permute-start | bytes 835592 | tf_op jit(solution)/shard_map/ppermute | solution.py:189
  22.3 17.2 %copy-start.4 = (bf16[1,2048,384]{2,1,0:T(8,128)(2,1)S(1)}, bf16[1,2048,384]{2,1,0:T(8,128)(2,1)}, u32[]{:S(2)}) copy-start(bf16[1,2048,384]{2,1,0:T(8,128)(2,1)} %param.9) | copy-start | bytes 4718596
  22.3 29.0 %all-to-all-start = ((bf16[16,24,2048]{2,1,0:T(8,128)(2,1)}), bf16[16,24,2048]{2,1,0:T(8,128)(2,1)}, u32[]{:S(2)}, u32[]{:S(2)}) async-start(bf16[16,24,2048]{2,1,0:T(8,128)(2,1)} %bitcast.27), calls=%async_computation | async-start | bytes 3145728 | tf_op jit(solution)/shard_map/all_to_all | solution.py:197
  29.6 7.3 %collective-permute-start.4 = (bf16[64,2176]{1,0:T(8,128)(2,1)S(1)}, bf16[64,2176]{1,0:T(8,128)(2,1)S(1)}, u32[]{:S(2)}, u32[]{:S(2)}) collective-permute-start(bf16[64,2176]{1,0:T(8,128)(2,1)S(1)} %collective-permute-done.2.refs_3_), channel_id=1, source_target_pairs={{0,2},{1,3},{2,4},{3,5},{4,6},{5,7},{6,8},{7,9},{8,10},{9,11},{10,... | collective-permute-start | bytes 835592 | tf_op jit(solution)/shard_map/ppermute | solution.py:189
  31.8 8.3 %collective-permute-start.5 = (bf16[64,2176]{1,0:T(8,128)(2,1)S(1)}, bf16[64,2176]{1,0:T(8,128)(2,1)S(1)}, u32[]{:S(2)}, u32[]{:S(2)}) collective-permute-start(bf16[64,2176]{1,0:T(8,128)(2,1)S(1)} %collective-permute-done.3.refs_0_), channel_id=1, source_target_pairs={{0,14},{1,15},{2,0},{3,1},{4,2},{5,3},{6,4},{7,5},{8,6},{9,7},{10,... | collective-permute-start | bytes 835592 | tf_op jit(solution)/shard_map/ppermute | solution.py:189
  36.9 6.7 %collective-permute-start.6 = (bf16[64,2176]{1,0:T(8,128)(2,1)S(1)}, bf16[64,2176]{1,0:T(8,128)(2,1)S(1)}, u32[]{:S(2)}, u32[]{:S(2)}) collective-permute-start(bf16[64,2176]{1,0:T(8,128)(2,1)S(1)} %collective-permute-done.4.refs_1_), channel_id=1, source_target_pairs={{0,2},{1,3},{2,4},{3,5},{4,6},{5,7},{6,8},{7,9},{8,10},{9,11},{10,... | collective-permute-start | bytes 835592 | tf_op jit(solution)/shard_map/ppermute | solution.py:189
  39.6 19.8 %collective-permute-start.7 = (bf16[2048,384]{1,0:T(8,128)(2,1)S(1)}, bf16[2048,384]{1,0:T(8,128)(2,1)}, u32[]{:S(2)}, u32[]{:S(2)}) collective-permute-start(bf16[2048,384]{1,0:T(8,128)(2,1)S(1)} %bitcast.18), channel_id=1, source_target_pairs={{0,1},{1,0},{2,3},{3,2},{4,5},{5,4},{6,7},{7,6},{8,9},{9,8},{10,11... | collective-permute-start | bytes 4718600 | tf_op jit(solution)/shard_map/ppermute | solution.py:194
  39.6 19.8 %collective-permute-start.8 = (bf16[2048,384]{1,0:T(8,128)(2,1)}, bf16[2048,384]{1,0:T(8,128)(2,1)}, u32[]{:S(2)}, u32[]{:S(2)}) collective-permute-start(bf16[2048,384]{1,0:T(8,128)(2,1)} %bitcast.19), channel_id=1, source_target_pairs={{0,1},{1,0},{2,3},{3,2},{4,5},{5,4},{6,7},{7,6},{8,9},{9,8},{10,11... | collective-permute-start | bytes 4718600 | tf_op jit(solution)/shard_map/ppermute | solution.py:194
  40.1 19.3 %collective-permute-start.9 = (bf16[384,2048]{1,0:T(8,128)(2,1)}, bf16[384,2048]{1,0:T(8,128)(2,1)}, u32[]{:S(2)}, u32[]{:S(2)}) collective-permute-start(bf16[384,2048]{1,0:T(8,128)(2,1)} %bitcast.22), channel_id=1, source_target_pairs={{0,1},{1,0},{2,3},{3,2},{4,5},{5,4},{6,7},{7,6},{8,9},{9,8},{10,11... | collective-permute-start | bytes 4718600 | tf_op jit(solution)/shard_map/ppermute | solution.py:194
  51.3 26.1 %all-to-all-start.1 = ((bf16[16,24,2048]{2,1,0:T(8,128)(2,1)}), bf16[16,24,2048]{2,1,0:T(8,128)(2,1)}, u32[]{:S(2)}, u32[]{:S(2)}) async-start(bf16[16,24,2048]{2,1,0:T(8,128)(2,1)} %bitcast.28), calls=%async_computation.1 | async-start | bytes 3145728 | tf_op jit(solution)/shard_map/all_to_all | solution.py:197
  58.1 0.7 copy-start
  110.2 25.2 %all-to-all-start.3 = ((bf16[16,24,2048]{2,1,0:T(8,128)(2,1)}), bf16[16,24,2048]{2,1,0:T(8,128)(2,1)S(1)}, u32[]{:S(2)}, u32[]{:S(2)}) async-start(bf16[16,24,2048]{2,1,0:T(8,128)(2,1)} %bitcast.25), calls=%async_computation.3 | async-start | bytes 3145728 | tf_op jit(solution)/shard_map/all_to_all | solution.py:197
  113.9 0.9 copy-start.1
  114.9 0.9 copy-start.3
  117.1 8.0 %collective-permute-start.12 = (bf16[64,2048]{1,0:T(8,128)(2,1)S(1)}, bf16[64,2048]{1,0:T(8,128)(2,1)S(1)}, u32[]{:S(2)}, u32[]{:S(2)}) collective-permute-start(bf16[64,2048]{1,0:T(8,128)(2,1)S(1)} %get-tuple-element.42), channel_id=1, source_target_pairs={{0,2},{1,3},{2,4},{3,5},{4,6},{5,7},{6,8},{7,9},{8,10},{9,11},{10,... | collective-permute-start | bytes 786440 | tf_op jit(solution)/shard_map/ppermute | solution.py:189
  119.6 8.1 %collective-permute-start.10 = (bf16[64,2048]{1,0:T(8,128)(2,1)S(1)}, bf16[64,2048]{1,0:T(8,128)(2,1)S(1)}, u32[]{:S(2)}, u32[]{:S(2)}) collective-permute-start(bf16[64,2048]{1,0:T(8,128)(2,1)S(1)} %get-tuple-element.40), channel_id=1, source_target_pairs={{0,14},{1,15},{2,0},{3,1},{4,2},{5,3},{6,4},{7,5},{8,6},{9,7},{10,... | collective-permute-start | bytes 786440 | tf_op jit(solution)/shard_map/ppermute | solution.py:189
  125.2 6.4 %collective-permute-start.13 = (bf16[64,2048]{1,0:T(8,128)(2,1)S(1)}, bf16[64,2048]{1,0:T(8,128)(2,1)S(1)}, u32[]{:S(2)}, u32[]{:S(2)}) collective-permute-start(bf16[64,2048]{1,0:T(8,128)(2,1)S(1)} %add_convert_fusion.3), channel_id=1, source_target_pairs={{0,2},{1,3},{2,4},{3,5},{4,6},{5,7},{6,8},{7,9},{8,10},{9,11},{10,... | collective-permute-start | bytes 786440 | tf_op jit(solution)/shard_map/ppermute | solution.py:189
  127.7 7.7 %collective-permute-start.11 = (bf16[64,2048]{1,0:T(8,128)(2,1)S(1)}, bf16[64,2048]{1,0:T(8,128)(2,1)S(1)}, u32[]{:S(2)}, u32[]{:S(2)}) collective-permute-start(bf16[64,2048]{1,0:T(8,128)(2,1)S(1)} %add_convert_fusion.4), channel_id=1, source_target_pairs={{0,14},{1,15},{2,0},{3,1},{4,2},{5,3},{6,4},{7,5},{8,6},{9,7},{10,... | collective-permute-start | bytes 786440 | tf_op jit(solution)/shard_map/ppermute | solution.py:189
  136.7 10.2 %collective-permute-start.15 = (bf16[64,2048]{1,0:T(8,128)(2,1)S(1)}, bf16[64,2048]{1,0:T(8,128)(2,1)S(1)}, u32[]{:S(2)}, u32[]{:S(2)}) collective-permute-start(bf16[64,2048]{1,0:T(8,128)(2,1)S(1)} %add_convert_fusion.1), channel_id=1, source_target_pairs={{0,14},{1,15},{2,0},{3,1},{4,2},{5,3},{6,4},{7,5},{8,6},{9,7},{10,... | collective-permute-start | bytes 786440 | tf_op jit(solution)/shard_map/ppermute | solution.py:189
  136.9 10.2 %collective-permute-start.14 = (bf16[64,2048]{1,0:T(8,128)(2,1)S(1)}, bf16[64,2048]{1,0:T(8,128)(2,1)S(1)}, u32[]{:S(2)}, u32[]{:S(2)}) collective-permute-start(bf16[64,2048]{1,0:T(8,128)(2,1)S(1)} %add_convert_fusion.2), channel_id=1, source_target_pairs={{0,2},{1,3},{2,4},{3,5},{4,6},{5,7},{6,8},{7,9},{8,10},{9,11},{10,... | collective-permute-start | bytes 786440 | tf_op jit(solution)/shard_map/ppermute | solution.py:189
  147.0 7.7 %collective-permute-start.16 = (bf16[64,2048]{1,0:T(8,128)(2,1)S(1)}, bf16[64,2048]{1,0:T(8,128)(2,1)S(1)}, u32[]{:S(2)}, u32[]{:S(2)}) collective-permute-start(bf16[64,2048]{1,0:T(8,128)(2,1)S(1)} %add_convert_fusion), channel_id=1, source_target_pairs={{0,14},{1,15},{2,0},{3,1},{4,2},{5,3},{6,4},{7,5},{8,6},{9,7},{10,... | collective-permute-start | bytes 786440 | tf_op jit(solution)/shard_map/ppermute | solution.py:189
  (1 other events, 0.7 us)
where the time goes:
time: 157 us; the launch traced here: 156 us
  waiting for transfers between devices  64.1 us (41%)
  starting transfers between devices  36.5 us (23%)
  Pallas kernels  25.8 us (16%)
  blocking collectives  24.6 us (16%)
  local copies, waits for them, and re-layouts  3.2 us (2%)
    ppermute x14, waiting for transfers between devices, along_z(): lax.ppermute(x, 'expert', [(i, (i + 2 * by) % col_count) for i in range(c...  48.5 us
    pallas_call x9, Pallas kernels, kernel_call(): pl.pallas_call(body, out_shape=[where(*out) for where, out in zip(keep, o...  25.8 us
    all_to_all x1, blocking collectives, exchange(): return lax.all_to_all(x, 'dp', split_axis=0, concat_axis=0, tiled=True)  24.6 us
    ppermute x14, starting transfers between devices, along_z(): lax.ppermute(x, 'expert', [(i, (i + 2 * by) % col_count) for i in range(c...  20.5 us
    all_to_all x3, waiting for transfers between devices, exchange(): return lax.all_to_all(x, 'dp', split_axis=0, concat_axis=0, tiled=True)  15.6 us
    all_to_all x3, starting transfers between devices, exchange(): return lax.all_to_all(x, 'dp', split_axis=0, concat_axis=0, tiled=True)  15.5 us
    unnamed x10, local copies, waits for them, and re-layouts  3.2 us
  transfers between devices with their start and end apart: 20, of which 12 were waited for; matrix products, arithmetic and copies ran while one was open for 0% of the time, Pallas kernels for 10%

commit v1 on v0

v1 whole, which is shorter than its diff:
```python
import functools

import jax
import jax.numpy as jnp
from jax import lax
from jax.experimental import pallas as pl
from jax.experimental.pallas import tpu as pltpu
from jax.sharding import PartitionSpec as P

F32 = jnp.float32
BF16 = jnp.bfloat16
EXTRA = 128
VMEM = pl.BlockSpec(memory_space=pltpu.VMEM)
SMEM = pl.BlockSpec(memory_space=pltpu.SMEM)
HBM = pl.BlockSpec(memory_space=pltpu.HBM)
LANES = 512
PARAMS = pltpu.CompilerParams(vmem_limit_bytes=24 << 20)


def on_chip(x):
    return pltpu.with_memory_space_constraint(x, pltpu.VMEM)


def off_chip(x):
    return pltpu.with_memory_space_constraint(x, pltpu.HBM)


def after(x, *others):
    return lax.optimization_barrier((x,) + others)[0]


def kernel_call(
    body, name, outs, arrays, scalars=(), keep=(), specs=None, out_specs=None, scratch=()
):
    keep = list(keep) + [jax.ShapeDtypeStruct] * (len(outs) - len(keep))
    return pl.pallas_call(
        body,
        out_shape=[where(*out) for where, out in zip(keep, outs)],
        in_specs=[SMEM] * len(scalars) + (specs or [VMEM] * len(arrays)),
        out_specs=out_specs or [VMEM] * len(outs),
        scratch_shapes=list(scratch),
        compiler_params=PARAMS,
        name=name,
    )(*scalars, *arrays)


def slot_of(index, slots):
    group = jnp.zeros_like(index)
    for d in range(1, 16):
        group = group + (index >= d * slots).astype(jnp.int32)
    return group, index - group * slots


def pack_kernel(tokens_ref, ids_ref, gates_ref, out_ref):
    rows, width = tokens_ref.shape
    gates = gates_ref[...]
    columns = [ids_ref[...], gates >> 8, gates & 255]
    top = jnp.concatenate(columns, axis=0).astype(F32)
    top = jnp.concatenate([top, jnp.zeros((top.shape[0], EXTRA - rows), F32)], axis=1)
    extra = jnp.concatenate([top, jnp.zeros((EXTRA - top.shape[0], EXTRA), F32)], axis=0).T
    out_ref[:, :width] = tokens_ref[...]
    out_ref[:, width:] = extra[:rows, :].astype(BF16)


def to_blocks(rows_ref, blocks_ref, base, slots, groups, total=None, offset=0):
    parts = rows_ref.shape[1] // LANES
    for d in groups:
        rows = rows_ref[pl.ds(base + d * slots, slots), :]
        for q in range(parts):
            there = pl.ds((d * parts + q) * (total or slots) + offset, slots)
            blocks_ref[there, :] = rows[:, q * LANES : (q + 1) * LANES]


def to_rows(blocks_ref, rows_ref, base, slots, groups, total=None, offset=0):
    parts = rows_ref.shape[1] // LANES
    for d in groups:
        for q in range(parts):
            here = pl.ds((d * parts + q) * (total or slots) + offset, slots)
            there = pl.ds(base + d * slots, slots)
            rows_ref[there, q * LANES : (q + 1) * LANES] = blocks_ref[here, :]


def pick_rows(extra, planes, groups, slots, plane):
    tokens = extra.shape[0]
    extra = extra.astype(F32)
    spare = -tokens % EXTRA
    if spare:
        extra = jnp.concatenate([extra, jnp.zeros((spare, EXTRA), F32)], axis=0)
    extra = extra.T[:8, :tokens]
    dest = planes * lax.broadcasted_iota(jnp.int32, (groups, 1), 0) + plane
    dest = dest.astype(F32)
    match = jnp.zeros((groups, tokens), F32)
    for k in range(8):
        match = match + (extra[k : k + 1, :] == dest).astype(F32)
    upper = lax.broadcasted_iota(jnp.int32, (tokens, tokens), 0) <= lax.broadcasted_iota(
        jnp.int32, (tokens, tokens), 1
    )
    upper = upper.astype(F32).astype(BF16)
    order = jnp.dot(match.astype(BF16), upper, preferred_element_type=F32) * match
    row = lax.broadcasted_iota(jnp.int32, (groups * slots, 1), 0)
    group, place = slot_of(row, slots)
    spread = (group == lax.broadcasted_iota(jnp.int32, (1, groups), 1)).astype(F32).astype(BF16)
    wanted = jnp.dot(spread, order.astype(BF16), preferred_element_type=F32)
    return (wanted == (place + 1).astype(F32)).astype(F32).astype(BF16)


def dispatch_kernel(sizes, slots, planes, groups, z_ref, *refs):
    count = sum(sizes)
    shards, refs = refs[:count], refs[count:]
    out_ref, extras, (rows_ref, block_ref, sems) = refs[0], refs[1:-3], refs[-3:]
    width = rows_ref.shape[1]
    base, offset, total = 0, 0, sum(slots)
    for i, (size, take) in enumerate(zip(sizes, slots)):
        mine, shards = shards[:size], shards[size:]
        extra = jnp.concatenate([x[:, width:] for x in mine], axis=0)
        extras[i][...] = extra
        pick = pick_rows(extra, planes, groups, take, z_ref[0])
        rows = jnp.concatenate([x[:, :width] for x in mine], axis=0)
        rows_ref[pl.ds(base, groups * take), :] = jnp.dot(
            pick, rows, preferred_element_type=F32
        ).astype(BF16)
        base += groups * take
    size = block_ref.shape[0] // 2
    copies = []
    for i in range(2):
        half = groups // 2
        base, offset = 0, 0
        for take in slots:
            to_blocks(
                rows_ref, block_ref, base, take, range(i * half, (i + 1) * half), total, offset
            )
            base += groups * take
            offset += take
        here = pl.ds(i * size, size)
        copies.append(pltpu.make_async_copy(block_ref.at[here], out_ref.at[here], sems.at[i]))
        copies[-1].start()
    for copy in copies:
        copy.wait()


def feed_forward(x_ref, wide, tall, out_ref, loads):
    units = tall.shape[0] // 2
    x = x_ref[...]
    hidden = []
    for i in (0, 2):
        for load in loads[i : i + 2]:
            load.wait()
        both = jnp.dot(x, wide[:, i * units : (i + 2) * units], preferred_element_type=F32)
        gate, up = both[:, :units], both[:, units:]
        hidden.append((gate / (1.0 + jnp.exp(-gate)) * up).astype(BF16))
    hidden = jnp.concatenate(hidden, axis=1)
    for load in loads[4:]:
        load.wait()
    out_ref[...] = jnp.dot(hidden, tall[...], preferred_element_type=F32).astype(BF16)


def weight_loads(panels, wide, tall, sems):
    units = panels[0].shape[1]
    ends = [(w, wide.at[:, pl.ds(i * units, units)]) for i, w in enumerate(panels[:4])]
    ends += [(w, tall.at[pl.ds(i * units, units)]) for i, w in enumerate(panels[4:])]
    return [pltpu.make_async_copy(a, b, sems.at[i]) for i, (a, b) in enumerate(ends)]


def expert_kernel(slots, groups, *refs):
    count = len(slots)
    flat = [take for part in slots for take in part]
    chunks, panels, refs = refs[:count], refs[count : count + 6], refs[count + 6 :]
    outs, refs = refs[: len(flat)], refs[len(flat) :]
    wide, tall, x_ref, out_ref = refs[:4]
    blocks, refs = refs[4 : 4 + count], refs[4 + count :]
    leaving, (sems, chunk_sems, out_sems) = refs[: len(flat)], refs[len(flat) :]
    arrive = [pltpu.make_async_copy(chunks[i], blocks[i], chunk_sems.at[i]) for i in range(count)]
    loads = weight_loads(panels, wide, tall, sems)
    for copy in arrive + loads:
        copy.start()
    base = 0
    for i in range(count):
        arrive[i].wait()
        offset = 0
        for take in slots[i]:
            to_rows(blocks[i], x_ref, base, take, range(groups), sum(slots[i]), offset)
            base += groups * take
            offset += take
    feed_forward(x_ref, wide, tall, out_ref, loads)
    leave, base = [], 0
    for i, take in enumerate(flat):
        to_blocks(out_ref, leaving[i], base, take, range(groups))
        base += groups * take
        leave.append(pltpu.make_async_copy(leaving[i], outs[i], out_sems.at[i]))
        leave[-1].start()
    for copy in leave:
        copy.wait()


def last_kernel(slots, groups, chunk_ref, g0, u0, g1, u1, d0, d1, out_hbm, *refs):
    wide, tall, x_ref, out_ref, block_ref, sems, out_sems = refs
    loads = weight_loads((g0, u0, g1, u1, d0, d1), wide, tall, sems)
    for load in loads:
        load.start()
    to_rows(chunk_ref, x_ref, 0, slots, range(groups))
    feed_forward(x_ref, wide, tall, out_ref, loads)
    size = block_ref.shape[0] // 2
    copies = []
    for i in range(2):
        half = groups // 2
        to_blocks(out_ref, block_ref, 0, slots, range(i * half, (i + 1) * half))
        here = pl.ds(i * size, size)
        copies.append(pltpu.make_async_copy(block_ref.at[here], out_hbm.at[here], out_sems.at[i]))
        copies[-1].start()
    for copy in copies:
        copy.wait()


def mixing_kernel(slots, planes, groups, z_ref, *refs):
    count = len(slots)
    for i in range(count):
        mix_slots(slots[i], planes, groups, z_ref, refs[i], *refs[count + 2 * i : count + 2 * i + 2])


def mix_slots(slots, planes, groups, z_ref, extra_ref, high_ref, low_ref):
    tokens = extra_ref.shape[0]
    extra = extra_ref[...].astype(F32)
    gates = extra[:, 8:16] * 256.0 + extra[:, 16:24]
    mix = gates / jnp.sum(gates, axis=1, keepdims=True)
    dest = planes * lax.broadcasted_iota(jnp.int32, (1, EXTRA), 1) + z_ref[0]
    dest = dest.astype(F32)
    match = jnp.zeros((tokens, EXTRA), F32)
    weight = jnp.zeros((tokens, EXTRA), F32)
    for k in range(8):
        same = extra[:, k : k + 1] == dest
        match = match + same.astype(F32)
        weight = weight + jnp.where(same, mix[:, k : k + 1], 0.0)
    lower = lax.broadcasted_iota(jnp.int32, (tokens, tokens), 1) <= lax.broadcasted_iota(
        jnp.int32, (tokens, tokens), 0
    )
    lower = lower.astype(F32).astype(BF16)
    order = jnp.dot(lower, match.astype(BF16), preferred_element_type=F32) * match
    column = lax.broadcasted_iota(jnp.int32, (1, groups * slots), 1)
    group, place = slot_of(column, slots)
    spread = (group == lax.broadcasted_iota(jnp.int32, (EXTRA, 1), 0)).astype(F32).astype(BF16)
    wanted = jnp.dot(order.astype(BF16), spread, preferred_element_type=F32)
    here = wanted == (place + 1).astype(F32)
    high = weight.astype(BF16)
    low = (weight - high.astype(F32)).astype(BF16)
    for piece, ref in ((high, high_ref), (low, low_ref)):
        wide = jnp.dot(piece, spread, preferred_element_type=F32)
        ref[...] = jnp.where(here, wide, 0.0).astype(BF16)


def combine_kernel(slots, groups, home_ref, high_ref, low_ref, *outs):
    outs, rows_ref = outs[:-1], outs[-1]
    to_rows(home_ref, rows_ref, 0, slots, range(groups))
    home = rows_ref[...]
    total = jnp.dot(high_ref[...], home, preferred_element_type=F32)
    total = total + jnp.dot(low_ref[...], home, preferred_element_type=F32)
    start = 0
    for out in outs:
        rows = out.shape[0]
        out[...] = total[start : start + rows, :].astype(out.dtype)
        start += rows


def per_device(tokens, expert_ids, gate_fixed, w_gate, w_up, w_down):
    col_count = lax.axis_size("expert")
    groups = lax.axis_size("dp")
    planes = col_count // 2
    rows, width = tokens.shape
    units = w_gate.shape[2]
    parts = width // LANES
    per_shard = 3 * rows // 32
    plane = (lax.axis_index("expert") // 2).astype(jnp.int32).reshape(1)

    def along_z(x, by):
        return lax.ppermute(
            x, "expert", [(i, (i + 2 * by) % col_count) for i in range(col_count)]
        )

    def partner(x):
        return lax.ppermute(x, "expert", [(i, i ^ 1) for i in range(col_count)])

    def exchange(x):
        return lax.all_to_all(x, "dp", split_axis=0, concat_axis=0, tiled=True)

    def full(slots):
        return ((groups * slots, width), BF16)

    def packed(slots):
        return ((groups * slots * parts, LANES), BF16)

    def dispatch(*sets):
        sizes = [len(shards) for shards in sets]
        slots = [per_shard * size for size in sizes]
        total = sum(slots)
        return kernel_call(
            functools.partial(dispatch_kernel, sizes, slots, planes, groups),
            "dispatch",
            [packed(total)] + [((rows * size, EXTRA), BF16) for size in sizes],
            [on_chip(x) for shards in sets for x in shards],
            [plane],
            keep=[pltpu.HBM],
            out_specs=[HBM] + [VMEM] * len(sizes),
            scratch=[
                pltpu.VMEM(*full(total)),
                pltpu.VMEM(*packed(total)),
                pltpu.SemaphoreType.DMA((2,)),
            ],
        )

    def mixing(extras):
        slots = [per_shard * x.shape[0] // rows for x in extras]
        shapes = [((x.shape[0], groups * n), BF16) for x, n in zip(extras, slots)]
        mixes = kernel_call(
            functools.partial(mixing_kernel, slots, planes, groups),
            "mixing",
            [shape for shape in shapes for _ in range(2)],
            extras,
            [plane],
        )
        return list(zip(mixes[::2], mixes[1::2]))

    panels = []
    for w in (w_gate[0], w_up[0], w_down[0]):
        panels += [w, partner(w)]
    g0, g1, u0, u1, d0, d1 = panels
    wide, tall = ((width, 4 * units), BF16), ((2 * units, width), BF16)

    def expert(chunks, slots):
        count = len(chunks)
        flat = [take for part in slots for take in part]
        return kernel_call(
            functools.partial(expert_kernel, slots, groups),
            "expert",
            [packed(n) for n in flat],
            [off_chip(w) for w in (*chunks, g0, u0, g1, u1, d0, d1)],
            keep=[pltpu.HBM] * len(flat),
            specs=[HBM] * (count + 6),
            out_specs=[HBM] * len(flat),
            scratch=[
                pltpu.VMEM(*wide),
                pltpu.VMEM(*tall),
                pltpu.VMEM(*full(sum(flat))),
                pltpu.VMEM(*full(sum(flat))),
                *[pltpu.VMEM(*packed(sum(part))) for part in slots],
                *[pltpu.VMEM(*packed(n)) for n in flat],
                pltpu.SemaphoreType.DMA((6,)),
                pltpu.SemaphoreType.DMA((count,)),
                pltpu.SemaphoreType.DMA((len(flat),)),
            ],
        )

    def last(chunk, slots):
        return kernel_call(
            functools.partial(last_kernel, slots, groups),
            "last",
            [packed(slots)],
            [chunk] + [off_chip(w) for w in (g0, u0, g1, u1, d0, d1)],
            keep=[pltpu.HBM],
            specs=[VMEM] + [HBM] * 6,
            out_specs=[HBM],
            scratch=[
                pltpu.VMEM(*wide),
                pltpu.VMEM(*tall),
                pltpu.VMEM(*full(slots)),
                pltpu.VMEM(*full(slots)),
                pltpu.VMEM(*packed(slots)),
                pltpu.SemaphoreType.DMA((6,)),
                pltpu.SemaphoreType.DMA((2,)),
            ],
        )[0]

    def combine(home, mix, kinds):
        slots = per_shard * len(kinds)
        return kernel_call(
            functools.partial(combine_kernel, slots, groups),
            "combine",
            [((rows, width), kind) for kind in kinds],
            [home] + list(mix),
            keep=[pltpu.VMEM] * len(kinds),
            scratch=[pltpu.VMEM(*full(slots))],
        )

    def plus(x, part):
        return (x.astype(F32) + part).astype(BF16)

    mine = kernel_call(
        pack_kernel,
        "pack",
        [((rows, width + EXTRA), BF16)],
        [off_chip(x) for x in (tokens, expert_ids.T, gate_fixed.T)],
        keep=[pltpu.VMEM],
    )[0]
    low_1, high_1 = along_z(mine, 1), along_z(mine, -1)
    low_2, high_2 = along_z(low_1, 1), along_z(high_1, -1)
    low_3, high_3 = along_z(low_2, 1), along_z(high_2, -1)
    low_4 = along_z(low_3, 1)

    near_rows, extra_0, extra_1 = dispatch([mine], [low_1, high_1])
    near = off_chip(exchange(near_rows))
    rows_2, extra_2 = dispatch([low_2, high_2])
    there_2 = off_chip(exchange(after(rows_2, near, low_3, high_3)))
    rows_3, extra_3 = dispatch([low_3, high_3, low_4])
    there_3 = exchange(after(rows_3, there_2))
    first = [after(x, rows_3) for x in (near, there_2)]
    one, two, three = per_shard, 2 * per_shard, 3 * per_shard
    out_0, out_1, out_2 = expert(first, [[one, two], [two]])
    mix_0, mix_1, mix_2, mix_3 = mixing([extra_0, extra_1, extra_2, extra_3])
    there_3 = after(there_3, out_0, *mix_0)
    out_3 = last(there_3, three)

    back_3 = exchange(out_3)
    back_2 = exchange(after(out_2, back_3))
    back_1 = exchange(after(out_1, back_2))
    back_0 = exchange(after(out_0, back_1))
    to_low_3, to_high_3, to_low_4 = combine(back_3, mix_3, [F32, BF16, BF16])
    down, up = along_z(to_low_4, -1), along_z(to_high_3, 1)
    back_2 = after(back_2, down, up)
    down = along_z(plus(down, to_low_3), -1)
    to_low_2, to_high_2 = combine(back_2, mix_2, [F32] * 2)
    up = along_z(plus(up, to_high_2), 1)
    back_1 = after(back_1, down, up)
    down = along_z(plus(down, to_low_2), -1)
    to_low_1, to_high_1 = combine(back_1, mix_1, [F32] * 2)
    down, up = along_z(plus(down, to_low_1), -1), along_z(plus(up, to_high_1), 1)
    (own,) = combine(back_0, mix_0, [F32])
    return own + up.astype(F32) + down.astype(F32)


def solution(mesh):
    rows = P(("dp", "expert"), None)
    panels = P(("dp", "expert"), None, None)
    return jax.shard_map(
        per_device,
        mesh=mesh,
        in_specs=(rows, rows, rows, panels, panels, panels),
        out_specs=rows,
        check_vma=False,
    )
```

time: 157 us -> 163 us (1.038)
  starting transfers between devices: 36.5 us -> 50.5 us
  waiting for transfers between devices: 64.1 us -> 60 us
  Pallas kernels: 25.8 us -> 29.5 us
  blocking collectives: 24.6 us -> 21.3 us
  local copies, waits for them, and re-layouts: 3.2 us -> 0.01 us
    all_to_all x3 -> x6, starting transfers between devices: 15.5 us -> 32.1 us  [exchange(): return lax.all_to_all(x, 'dp', split_axis=0, concat_axis=0, tiled=True)]
    ppermute x14, waiting for transfers between devices: 48.5 us -> 33.5 us  [along_z(): lax.ppermute(x, 'expert', [(i, (i + 2 * by) % col_count) for i in range(c...]
    all_to_all x3 -> x6, waiting for transfers between devices: 15.6 us -> 26.5 us  [exchange(): return lax.all_to_all(x, 'dp', split_axis=0, concat_axis=0, tiled=True)]
    pallas_call x9 -> x11, Pallas kernels: 25.8 us -> 29.5 us  [kernel_call(): pl.pallas_call(body, out_shape=[where(*out) for where, out in zip(keep, o...]
    all_to_all x1, blocking collectives: 24.6 us -> 21.3 us  [exchange(): return lax.all_to_all(x, 'dp', split_axis=0, concat_axis=0, tiled=True)]
    unnamed x10 -> x4, local copies, waits for them, and re-layouts: 3.2 us -> 0.01 us
    ppermute x14, starting transfers between devices: 20.5 us -> 17.7 us  [along_z(): lax.ppermute(x, 'expert', [(i, (i + 2 * by) % col_count) for i in range(c...]
  transfers between devices with their start and end apart: 20 -> 23, of which waited for: 12 -> 12; matrix products, arithmetic and copies ran while one was open for 0% -> 0% of each run, Pallas kernels for 10% -> 12%
where the time goes in v1:
time: 163 us
  waiting for transfers between devices  60 us (37%)
  starting transfers between devices  50.5 us (31%)
  Pallas kernels  29.5 us (18%)
  blocking collectives  21.3 us (13%)
    ppermute x14, waiting for transfers between devices, along_z(): lax.ppermute(x, 'expert', [(i, (i + 2 * by) % col_count) for i in range(c...  33.5 us
    all_to_all x6, starting transfers between devices, exchange(): return lax.all_to_all(x, 'dp', split_axis=0, concat_axis=0, tiled=True)  32.1 us
    pallas_call x11, Pallas kernels, kernel_call(): pl.pallas_call(body, out_shape=[where(*out) for where, out in zip(keep, o...  29.5 us
    all_to_all x6, waiting for transfers between devices, exchange(): return lax.all_to_all(x, 'dp', split_axis=0, concat_axis=0, tiled=True)  26.5 us
    all_to_all x1, blocking collectives, exchange(): return lax.all_to_all(x, 'dp', split_axis=0, concat_axis=0, tiled=True)  21.3 us
    ppermute x14, starting transfers between devices, along_z(): lax.ppermute(x, 'expert', [(i, (i + 2 * by) % col_count) for i in range(c...  17.7 us
  transfers between devices with their start and end apart: 23, of which 12 were waited for; matrix products, arithmetic and copies ran while one was open for 0% of the time, Pallas kernels for 12%

profile of v1, /device:TPU:96, one launch (start us, length us, event | category | flops | bytes accessed | tf_op | source)
XLA Modules:
  0.0 162.8 jit_solution(4961581370224418062)
XLA Ops:
  1.1 3.2 %collective-permute-start = (bf16[64,2176]{1,0:T(8,128)(2,1)S(1)}, bf16[64,2176]{1,0:T(8,128)(2,1)S(1)}, u32[]{:S(2)}, u32[]{:S(2)}) collective-permute-start(bf16[64,2176]{1,0:T(8,128)(2,1)S(1)} %pack.1.refs_0_), channel_id=1, source_target_pairs={{0,2},{1,3},{2,4},{3,5},{4,6},{5,7},{6,8},{7,9},{8,10},{9,11},{10,... | collective-permute-start | bytes 835592 | tf_op jit(solution)/shard_map/ppermute | solution.py:274
  4.3 5.9 %collective-permute-done.refs_1_ = bf16[64,2176]{1,0:T(8,128)(2,1)S(1)} collective-permute-done((bf16[64,2176]{1,0:T(8,128)(2,1)S(1)}, bf16[64,2176]{1,0:T(8,128)(2,1)S(1)}, u32[]{:S(2)}, u32[]{:S(2)}) %collective-permute-start) | collective-permute-done | bytes 278560 | tf_op jit(solution)/shard_map/ppermute | solution.py:274
  10.2 3.4 %collective-permute-done.1.refs_2_ = bf16[64,2176]{1,0:T(8,128)(2,1)S(1)} collective-permute-done((bf16[64,2176]{1,0:T(8,128)(2,1)S(1)}, bf16[64,2176]{1,0:T(8,128)(2,1)S(1)}, u32[]{:S(2)}, u32[]{:S(2)}) %collective-permute-start.1) | collective-permute-done | bytes 278560 | tf_op jit(solution)/shard_map/ppermute | solution.py:274
  15.7 7.0 %all-to-all-start = ((bf16[16,72,512]{2,1,0:T(8,128)(2,1)}), bf16[16,72,512]{2,1,0:T(8,128)(2,1)S(1)}, u32[]{:S(2)}, u32[]{:S(2)}) async-start(bf16[16,72,512]{2,1,0:T(8,128)(2,1)} %bitcast.29), calls=%async_computation | async-start | bytes 2359296 | tf_op jit(solution)/shard_map/all_to_all | solution.py:282
  24.9 4.9 %collective-permute-done.2.refs_0_ = bf16[64,2176]{1,0:T(8,128)(2,1)S(1)} collective-permute-done((bf16[64,2176]{1,0:T(8,128)(2,1)S(1)}, bf16[64,2176]{1,0:T(8,128)(2,1)S(1)}, u32[]{:S(2)}, u32[]{:S(2)}) %collective-permute-start.2) | collective-permute-done | bytes 278560 | tf_op jit(solution)/shard_map/ppermute | solution.py:274
  33.4 2.9 %collective-permute-done.3.refs_0_ = bf16[64,2176]{1,0:T(8,128)(2,1)S(1)} collective-permute-done((bf16[64,2176]{1,0:T(8,128)(2,1)S(1)}, bf16[64,2176]{1,0:T(8,128)(2,1)S(1)}, u32[]{:S(2)}, u32[]{:S(2)}) %collective-permute-start.3) | collective-permute-done | bytes 278560 | tf_op jit(solution)/shard_map/ppermute | solution.py:274
  36.3 3.0 %collective-permute-done.5.refs_1_ = bf16[64,2176]{1,0:T(8,128)(2,1)S(1)} collective-permute-done((bf16[64,2176]{1,0:T(8,128)(2,1)S(1)}, bf16[64,2176]{1,0:T(8,128)(2,1)S(1)}, u32[]{:S(2)}, u32[]{:S(2)}) %collective-permute-start.5) | collective-permute-done | bytes 278560 | tf_op jit(solution)/shard_map/ppermute | solution.py:274
  40.5 5.7 %all-to-all-start.1 = ((bf16[16,48,512]{2,1,0:T(8,128)(2,1)}), bf16[16,48,512]{2,1,0:T(8,128)(2,1)S(1)}, u32[]{:S(2)}, u32[]{:S(2)}) async-start(bf16[16,48,512]{2,1,0:T(8,128)(2,1)} %bitcast.30), calls=%async_computation.1 | async-start | bytes 1572864 | tf_op jit(solution)/shard_map/all_to_all | solution.py:282
  47.0 9.0 %collective-permute-done.6.refs_2_ = bf16[64,2176]{1,0:T(8,128)(2,1)S(1)} collective-permute-done((bf16[64,2176]{1,0:T(8,128)(2,1)S(1)}, bf16[64,2176]{1,0:T(8,128)(2,1)S(1)}, u32[]{:S(2)}, u32[]{:S(2)}) %collective-permute-start.6) | collective-permute-done | bytes 278560 | tf_op jit(solution)/shard_map/ppermute | solution.py:274
  57.9 7.2 %all-to-all-start.2 = ((bf16[16,72,512]{2,1,0:T(8,128)(2,1)}), bf16[16,72,512]{2,1,0:T(8,128)(2,1)S(1)}, u32[]{:S(2)}, u32[]{:S(2)}) async-start(bf16[16,72,512]{2,1,0:T(8,128)(2,1)} %bitcast.28), calls=%async_computation.2 | async-start | bytes 2359296 | tf_op jit(solution)/shard_map/all_to_all | solution.py:282
  67.1 11.6 %expert.1 = (bf16[384,512]{1,0:T(8,128)(2,1)}, bf16[768,512]{1,0:T(8,128)(2,1)}, bf16[768,512]{1,0:T(8,128)(2,1)}) custom-call(bf16[1152,512]{1,0:T(8,128)(2,1)} %bitcast.26, bf16[768,512]{1,0:T(8,128)(2,1)} %bitcast.27, bf16[2048,384]{1,0:T(8,128)(2,1)} %bitcast.7.refs_2_.g0, bf16[2048,384]{1,0:T(8,128)(2,1)} %bitcast.8.refs_3_.u0, ...), custom_call_target="tpu_custom_call" | custom-call | tf_op jit(solution)/shard_map/expert/pallas_call | solution.py:36
  78.7 5.4 %all-to-all-done.2 = bf16[16,72,512]{2,1,0:T(8,128)(2,1)S(1)} async-done(((bf16[16,72,512]{2,1,0:T(8,128)(2,1)}), bf16[16,72,512]{2,1,0:T(8,128)(2,1)S(1)}, u32[]{:S(2)}, u32[]{:S(2)}) %all-to-all-start.2) | async-done | bytes 1179680 | tf_op jit(solution)/shard_map/all_to_all | solution.py:282
  84.0 6.9 %last.1 = bf16[1152,512]{1,0:T(8,128)(2,1)} custom-call(bf16[1152,512]{1,0:T(8,128)(2,1)S(1)} %bitcast.20, bf16[2048,384]{1,0:T(8,128)(2,1)} %bitcast.7.refs_2_.g0, bf16[2048,384]{1,0:T(8,128)(2,1)} %bitcast.8.refs_3_.u0, bf16[2048,384]{1,0:T(8,128)(2,1)} %collective-permute-done.7.refs_4_.g1, bf16[2048,384]{1,0:T(8,128)(2,1)} %collective-permute-done.8.refs_5_.u1, ...), custom_call_target="tpu_custom_call" | custom-call | tf_op jit(solution)/shard_map/last/pallas_call | solution.py:36
  90.9 21.3 %all_to_all.82 = bf16[16,72,512]{2,1,0:T(8,128)(2,1)S(1)} all-to-all(bf16[16,72,512]{2,1,0:T(8,128)(2,1)} %bitcast.25), channel_id=1, replica_groups=mesh['dp'=16,'expert'=16] {'dp'}, dimensions={0} | all-to-all | bytes 2359296 | tf_op jit(solution)/shard_map/all_to_all | solution.py:282
  112.3 3.6 %all-to-all-start.4 = ((bf16[16,48,512]{2,1,0:T(8,128)(2,1)}), bf16[16,48,512]{2,1,0:T(8,128)(2,1)S(1)}, u32[]{:S(2)}, u32[]{:S(2)}) async-start(bf16[16,48,512]{2,1,0:T(8,128)(2,1)} %bitcast.14), calls=%async_computation.4 | async-start | bytes 1572864 | tf_op jit(solution)/shard_map/all_to_all | solution.py:282
  117.0 3.2 %collective-permute-start.10 = (bf16[64,2048]{1,0:T(8,128)(2,1)S(1)}, bf16[64,2048]{1,0:T(8,128)(2,1)S(1)}, u32[]{:S(2)}, u32[]{:S(2)}) collective-permute-start(bf16[64,2048]{1,0:T(8,128)(2,1)S(1)} %get-tuple-element.62), channel_id=1, source_target_pairs={{0,2},{1,3},{2,4},{3,5},{4,6},{5,7},{6,8},{7,9},{8,10},{9,11},{10,... | collective-permute-start | bytes 786440 | tf_op jit(solution)/shard_map/ppermute | solution.py:274
  120.2 4.3 %collective-permute-done.11 = bf16[64,2048]{1,0:T(8,128)(2,1)S(1)} collective-permute-done((bf16[64,2048]{1,0:T(8,128)(2,1)S(1)}, bf16[64,2048]{1,0:T(8,128)(2,1)S(1)}, u32[]{:S(2)}, u32[]{:S(2)}) %collective-permute-start.11) | collective-permute-done | bytes 262176 | tf_op jit(solution)/shard_map/ppermute | solution.py:274
  125.0 3.2 %all-to-all-done.4 = bf16[16,48,512]{2,1,0:T(8,128)(2,1)S(1)} async-done(((bf16[16,48,512]{2,1,0:T(8,128)(2,1)}), bf16[16,48,512]{2,1,0:T(8,128)(2,1)S(1)}, u32[]{:S(2)}, u32[]{:S(2)}) %all-to-all-start.4) | async-done | bytes 786464 | tf_op jit(solution)/shard_map/all_to_all | solution.py:282
  128.2 4.0 %all-to-all-start.5 = ((bf16[16,48,512]{2,1,0:T(8,128)(2,1)}), bf16[16,48,512]{2,1,0:T(8,128)(2,1)S(1)}, u32[]{:S(2)}, u32[]{:S(2)}) async-start(bf16[16,48,512]{2,1,0:T(8,128)(2,1)} %bitcast.16), calls=%async_computation.5 | async-start | bytes 1572864 | tf_op jit(solution)/shard_map/all_to_all | solution.py:282
  132.7 3.3 %collective-permute-start.12 = (bf16[64,2048]{1,0:T(8,128)(2,1)S(1)}, bf16[64,2048]{1,0:T(8,128)(2,1)S(1)}, u32[]{:S(2)}, u32[]{:S(2)}) collective-permute-start(bf16[64,2048]{1,0:T(8,128)(2,1)S(1)} %add_convert_fusion.4), channel_id=1, source_target_pairs={{0,2},{1,3},{2,4},{3,5},{4,6},{5,7},{6,8},{7,9},{8,10},{9,11},{10,... | collective-permute-start | bytes 786440 | tf_op jit(solution)/shard_map/ppermute | solution.py:274
  136.1 7.5 %all-to-all-done.5 = bf16[16,48,512]{2,1,0:T(8,128)(2,1)S(1)} async-done(((bf16[16,48,512]{2,1,0:T(8,128)(2,1)}), bf16[16,48,512]{2,1,0:T(8,128)(2,1)S(1)}, u32[]{:S(2)}, u32[]{:S(2)}) %all-to-all-start.5) | async-done | bytes 786464 | tf_op jit(solution)/shard_map/all_to_all | solution.py:282
  144.2 3.3 %collective-permute-start.14 = (bf16[64,2048]{1,0:T(8,128)(2,1)S(1)}, bf16[64,2048]{1,0:T(8,128)(2,1)S(1)}, u32[]{:S(2)}, u32[]{:S(2)}) collective-permute-start(bf16[64,2048]{1,0:T(8,128)(2,1)S(1)} %add_convert_fusion.2), channel_id=1, source_target_pairs={{0,2},{1,3},{2,4},{3,5},{4,6},{5,7},{6,8},{7,9},{8,10},{9,11},{10,... | collective-permute-start | bytes 786440 | tf_op jit(solution)/shard_map/ppermute | solution.py:274
  147.5 4.6 %all-to-all-start.6 = ((bf16[16,24,512]{2,1,0:T(8,128)(2,1)}), bf16[16,24,512]{2,1,0:T(8,128)(2,1)S(1)}, u32[]{:S(2)}, u32[]{:S(2)}) async-start(bf16[16,24,512]{2,1,0:T(8,128)(2,1)} %bitcast.18), calls=%async_computation.6 | async-start | bytes 786432 | tf_op jit(solution)/shard_map/all_to_all | solution.py:282
  152.3 9.2 %all-to-all-done.6 = bf16[16,24,512]{2,1,0:T(8,128)(2,1)S(1)} async-done(((bf16[16,24,512]{2,1,0:T(8,128)(2,1)}), bf16[16,24,512]{2,1,0:T(8,128)(2,1)S(1)}, u32[]{:S(2)}, u32[]{:S(2)}) %all-to-all-start.6) | async-done | bytes 393248 | tf_op jit(solution)/shard_map/all_to_all | solution.py:282
  (44 shorter events, 18.8 us)
Async XLA Ops:
  1.1 9.1 %collective-permute-start = (bf16[64,2176]{1,0:T(8,128)(2,1)S(1)}, bf16[64,2176]{1,0:T(8,128)(2,1)S(1)}, u32[]{:S(2)}, u32[]{:S(2)}) collective-permute-start(bf16[64,2176]{1,0:T(8,128)(2,1)S(1)} %pack.1.refs_0_), channel_id=1, source_target_pairs={{0,2},{1,3},{2,4},{3,5},{4,6},{5,7},{6,8},{7,9},{8,10},{9,11},{10,... | collective-permute-start | bytes 835592 | tf_op jit(solution)/shard_map/ppermute | solution.py:274
  4.3 9.3 %collective-permute-start.1 = (bf16[64,2176]{1,0:T(8,128)(2,1)S(1)}, bf16[64,2176]{1,0:T(8,128)(2,1)S(1)}, u32[]{:S(2)}, u32[]{:S(2)}) collective-permute-start(bf16[64,2176]{1,0:T(8,128)(2,1)S(1)} %pack.1.refs_0_), channel_id=1, source_target_pairs={{0,14},{1,15},{2,0},{3,1},{4,2},{5,3},{6,4},{7,5},{8,6},{9,7},{10,... | collective-permute-start | bytes 835592 | tf_op jit(solution)/shard_map/ppermute | solution.py:274
  15.7 24.8 %all-to-all-start = ((bf16[16,72,512]{2,1,0:T(8,128)(2,1)}), bf16[16,72,512]{2,1,0:T(8,128)(2,1)S(1)}, u32[]{:S(2)}, u32[]{:S(2)}) async-start(bf16[16,72,512]{2,1,0:T(8,128)(2,1)} %bitcast.29), calls=%async_computation | async-start | bytes 2359296 | tf_op jit(solution)/shard_map/all_to_all | solution.py:282
  22.8 7.0 %collective-permute-start.2 = (bf16[64,2176]{1,0:T(8,128)(2,1)S(1)}, bf16[64,2176]{1,0:T(8,128)(2,1)S(1)}, u32[]{:S(2)}, u32[]{:S(2)}) collective-permute-start(bf16[64,2176]{1,0:T(8,128)(2,1)S(1)} %collective-permute-done.refs_1_), channel_id=1, source_target_pairs={{0,2},{1,3},{2,4},{3,5},{4,6},{5,7},{6,8},{7,9},{8,10},{9,11},{10,... | collective-permute-start | bytes 835592 | tf_op jit(solution)/shard_map/ppermute | solution.py:274
  23.1 8.5 %collective-permute-start.4 = (bf16[64,2176]{1,0:T(8,128)(2,1)S(1)}, bf16[64,2176]{1,0:T(8,128)(2,1)S(1)}, u32[]{:S(2)}, u32[]{:S(2)}) collective-permute-start(bf16[64,2176]{1,0:T(8,128)(2,1)S(1)} %collective-permute-done.1.refs_2_), channel_id=1, source_target_pairs={{0,14},{1,15},{2,0},{3,1},{4,2},{5,3},{6,4},{7,5},{8,6},{9,7},{10,... | collective-permute-start | bytes 835592 | tf_op jit(solution)/shard_map/ppermute | solution.py:274
  29.8 6.5 %collective-permute-start.3 = (bf16[64,2176]{1,0:T(8,128)(2,1)S(1)}, bf16[64,2176]{1,0:T(8,128)(2,1)S(1)}, u32[]{:S(2)}, u32[]{:S(2)}) collective-permute-start(bf16[64,2176]{1,0:T(8,128)(2,1)S(1)} %collective-permute-done.2.refs_0_), channel_id=1, source_target_pairs={{0,2},{1,3},{2,4},{3,5},{4,6},{5,7},{6,8},{7,9},{8,10},{9,11},{10,... | collective-permute-start | bytes 835592 | tf_op jit(solution)/shard_map/ppermute | solution.py:274
  31.6 7.8 %collective-permute-start.5 = (bf16[64,2176]{1,0:T(8,128)(2,1)S(1)}, bf16[64,2176]{1,0:T(8,128)(2,1)S(1)}, u32[]{:S(2)}, u32[]{:S(2)}) collective-permute-start(bf16[64,2176]{1,0:T(8,128)(2,1)S(1)} %collective-permute-done.4.refs_1_), channel_id=1, source_target_pairs={{0,14},{1,15},{2,0},{3,1},{4,2},{5,3},{6,4},{7,5},{8,6},{9,7},{10,... | collective-permute-start | bytes 835592 | tf_op jit(solution)/shard_map/ppermute | solution.py:274
  40.5 17.3 %copy-start = (bf16[16,72,512]{2,1,0:T(8,128)(2,1)}, bf16[16,72,512]{2,1,0:T(8,128)(2,1)S(1)}, u32[]{:S(2)}) copy-start(bf16[16,72,512]{2,1,0:T(8,128)(2,1)S(1)} %all-to-all-done) | copy-start | bytes 3538948
  40.5 17.3 %all-to-all-start.1 = ((bf16[16,48,512]{2,1,0:T(8,128)(2,1)}), bf16[16,48,512]{2,1,0:T(8,128)(2,1)S(1)}, u32[]{:S(2)}, u32[]{:S(2)}) async-start(bf16[16,48,512]{2,1,0:T(8,128)(2,1)} %bitcast.30), calls=%async_computation.1 | async-start | bytes 1572864 | tf_op jit(solution)/shard_map/all_to_all | solution.py:282
  46.2 20.8 %collective-permute-start.7 = (bf16[2048,384]{1,0:T(8,128)(2,1)}, bf16[2048,384]{1,0:T(8,128)(2,1)}, u32[]{:S(2)}, u32[]{:S(2)}) collective-permute-start(bf16[2048,384]{1,0:T(8,128)(2,1)} %bitcast.7.refs_2_.g0), channel_id=1, source_target_pairs={{0,1},{1,0},{2,3},{3,2},{4,5},{5,4},{6,7},{7,6},{8,9},{9,8},{10,11... | collective-permute-start | bytes 4718600 | tf_op jit(solution)/shard_map/ppermute | solution.py:279
  46.3 20.7 %collective-permute-start.8 = (bf16[2048,384]{1,0:T(8,128)(2,1)}, bf16[2048,384]{1,0:T(8,128)(2,1)}, u32[]{:S(2)}, u32[]{:S(2)}) collective-permute-start(bf16[2048,384]{1,0:T(8,128)(2,1)} %bitcast.8.refs_3_.u0), channel_id=1, source_target_pairs={{0,1},{1,0},{2,3},{3,2},{4,5},{5,4},{6,7},{7,6},{8,9},{9,8},{10,11... | collective-permute-start | bytes 4718600 | tf_op jit(solution)/shard_map/ppermute | solution.py:279
  46.8 20.3 %collective-permute-start.9 = (bf16[384,2048]{1,0:T(8,128)(2,1)}, bf16[384,2048]{1,0:T(8,128)(2,1)}, u32[]{:S(2)}, u32[]{:S(2)}) collective-permute-start(bf16[384,2048]{1,0:T(8,128)(2,1)} %bitcast.9.refs_6_.d0), channel_id=1, source_target_pairs={{0,1},{1,0},{2,3},{3,2},{4,5},{5,4},{6,7},{7,6},{8,9},{9,8},{10,11... | collective-permute-start | bytes 4718600 | tf_op jit(solution)/shard_map/ppermute | solution.py:279
  46.9 9.0 %collective-permute-start.6 = (bf16[64,2176]{1,0:T(8,128)(2,1)S(1)}, bf16[64,2176]{1,0:T(8,128)(2,1)S(1)}, u32[]{:S(2)}, u32[]{:S(2)}) collective-permute-start(bf16[64,2176]{1,0:T(8,128)(2,1)S(1)} %collective-permute-done.3.refs_0_), channel_id=1, source_target_pairs={{0,2},{1,3},{2,4},{3,5},{4,6},{5,7},{6,8},{7,9},{8,10},{9,11},{10,... | collective-permute-start | bytes 835592 | tf_op jit(solution)/shard_map/ppermute | solution.py:274
  57.9 26.2 %all-to-all-start.2 = ((bf16[16,72,512]{2,1,0:T(8,128)(2,1)}), bf16[16,72,512]{2,1,0:T(8,128)(2,1)S(1)}, u32[]{:S(2)}, u32[]{:S(2)}) async-start(bf16[16,72,512]{2,1,0:T(8,128)(2,1)} %bitcast.28), calls=%async_computation.2 | async-start | bytes 2359296 | tf_op jit(solution)/shard_map/all_to_all | solution.py:282
  112.3 15.9 %all-to-all-start.4 = ((bf16[16,48,512]{2,1,0:T(8,128)(2,1)}), bf16[16,48,512]{2,1,0:T(8,128)(2,1)S(1)}, u32[]{:S(2)}, u32[]{:S(2)}) async-start(bf16[16,48,512]{2,1,0:T(8,128)(2,1)} %bitcast.14), calls=%async_computation.4 | async-start | bytes 1572864 | tf_op jit(solution)/shard_map/all_to_all | solution.py:282
  116.9 7.7 %collective-permute-start.11 = (bf16[64,2048]{1,0:T(8,128)(2,1)S(1)}, bf16[64,2048]{1,0:T(8,128)(2,1)S(1)}, u32[]{:S(2)}, u32[]{:S(2)}) collective-permute-start(bf16[64,2048]{1,0:T(8,128)(2,1)S(1)} %get-tuple-element.63), channel_id=1, source_target_pairs={{0,14},{1,15},{2,0},{3,1},{4,2},{5,3},{6,4},{7,5},{8,6},{9,7},{10,... | collective-permute-start | bytes 786440 | tf_op jit(solution)/shard_map/ppermute | solution.py:274
  117.0 7.9 %collective-permute-start.10 = (bf16[64,2048]{1,0:T(8,128)(2,1)S(1)}, bf16[64,2048]{1,0:T(8,128)(2,1)S(1)}, u32[]{:S(2)}, u32[]{:S(2)}) collective-permute-start(bf16[64,2048]{1,0:T(8,128)(2,1)S(1)} %get-tuple-element.62), channel_id=1, source_target_pairs={{0,2},{1,3},{2,4},{3,5},{4,6},{5,7},{6,8},{7,9},{8,10},{9,11},{10,... | collective-permute-start | bytes 786440 | tf_op jit(solution)/shard_map/ppermute | solution.py:274
  124.6 11.3 %collective-permute-start.13 = (bf16[64,2048]{1,0:T(8,128)(2,1)S(1)}, bf16[64,2048]{1,0:T(8,128)(2,1)S(1)}, u32[]{:S(2)}, u32[]{:S(2)}) collective-permute-start(bf16[64,2048]{1,0:T(8,128)(2,1)S(1)} %add_convert_fusion.3), channel_id=1, source_target_pairs={{0,14},{1,15},{2,0},{3,1},{4,2},{5,3},{6,4},{7,5},{8,6},{9,7},{10,... | collective-permute-start | bytes 786440 | tf_op jit(solution)/shard_map/ppermute | solution.py:274
  128.2 15.5 %all-to-all-start.5 = ((bf16[16,48,512]{2,1,0:T(8,128)(2,1)}), bf16[16,48,512]{2,1,0:T(8,128)(2,1)S(1)}, u32[]{:S(2)}, u32[]{:S(2)}) async-start(bf16[16,48,512]{2,1,0:T(8,128)(2,1)} %bitcast.16), calls=%async_computation.5 | async-start | bytes 1572864 | tf_op jit(solution)/shard_map/all_to_all | solution.py:282
  132.7 11.0 %collective-permute-start.12 = (bf16[64,2048]{1,0:T(8,128)(2,1)S(1)}, bf16[64,2048]{1,0:T(8,128)(2,1)S(1)}, u32[]{:S(2)}, u32[]{:S(2)}) collective-permute-start(bf16[64,2048]{1,0:T(8,128)(2,1)S(1)} %add_convert_fusion.4), channel_id=1, source_target_pairs={{0,2},{1,3},{2,4},{3,5},{4,6},{5,7},{6,8},{7,9},{8,10},{9,11},{10,... | collective-permute-start | bytes 786440 | tf_op jit(solution)/shard_map/ppermute | solution.py:274
  136.0 16.1 %collective-permute-start.15 = (bf16[64,2048]{1,0:T(8,128)(2,1)S(1)}, bf16[64,2048]{1,0:T(8,128)(2,1)S(1)}, u32[]{:S(2)}, u32[]{:S(2)}) collective-permute-start(bf16[64,2048]{1,0:T(8,128)(2,1)S(1)} %add_convert_fusion.1), channel_id=1, source_target_pairs={{0,14},{1,15},{2,0},{3,1},{4,2},{5,3},{6,4},{7,5},{8,6},{9,7},{10,... | collective-permute-start | bytes 786440 | tf_op jit(solution)/shard_map/ppermute | solution.py:274
  144.2 17.7 %collective-permute-start.14 = (bf16[64,2048]{1,0:T(8,128)(2,1)S(1)}, bf16[64,2048]{1,0:T(8,128)(2,1)S(1)}, u32[]{:S(2)}, u32[]{:S(2)}) collective-permute-start(bf16[64,2048]{1,0:T(8,128)(2,1)S(1)} %add_convert_fusion.2), channel_id=1, source_target_pairs={{0,2},{1,3},{2,4},{3,5},{4,6},{5,7},{6,8},{7,9},{8,10},{9,11},{10,... | collective-permute-start | bytes 786440 | tf_op jit(solution)/shard_map/ppermute | solution.py:274
  147.5 14.0 %all-to-all-start.6 = ((bf16[16,24,512]{2,1,0:T(8,128)(2,1)}), bf16[16,24,512]{2,1,0:T(8,128)(2,1)S(1)}, u32[]{:S(2)}, u32[]{:S(2)}) async-start(bf16[16,24,512]{2,1,0:T(8,128)(2,1)} %bitcast.18), calls=%async_computation.6 | async-start | bytes 786432 | tf_op jit(solution)/shard_map/all_to_all | solution.py:282
  152.2 9.7 %collective-permute-start.16 = (bf16[64,2048]{1,0:T(8,128)(2,1)S(1)}, bf16[64,2048]{1,0:T(8,128)(2,1)S(1)}, u32[]{:S(2)}, u32[]{:S(2)}) collective-permute-start(bf16[64,2048]{1,0:T(8,128)(2,1)S(1)} %add_convert_fusion), channel_id=1, source_target_pairs={{0,14},{1,15},{2,0},{3,1},{4,2},{5,3},{6,4},{7,5},{8,6},{9,7},{10,... | collective-permute-start | bytes 786440 | tf_op jit(solution)/shard_map/ppermute | solution.py:274
  (1 other events, 9.3 us)

commit v2 on v0

--- a/solution.py
+++ b/solution.py
@@ -97,28 +97,26 @@
         copy.wait()
 
 
-def expert_kernel(x_hbm, g0, u0, g1, u1, d0, d1, out_hbm, x_ref, wide, tall, out_ref, sems, out_sems):
+def expert_kernel(x_ref, g0, u0, g1, u1, d0, d1, out_hbm, wide, tall, out_ref, sems, out_sems):
     units = g0.shape[1]
-    ends = [(x_hbm, x_ref)]
-    ends += [(w, wide.at[:, pl.ds(i * units, units)]) for i, w in enumerate((g0, u0, g1, u1))]
+    ends = [(w, wide.at[:, pl.ds(i * units, units)]) for i, w in enumerate((g0, u0, g1, u1))]
     ends += [(w, tall.at[pl.ds(i * units, units)]) for i, w in enumerate((d0, d1))]
     loads = [pltpu.make_async_copy(a, b, sems.at[i]) for i, (a, b) in enumerate(ends)]
     for load in loads:
         load.start()
-    loads[0].wait()
     x = x_ref[...]
     hidden = []
     for i in (0, 2):
-        loads[1 + i].wait()
-        loads[2 + i].wait()
+        loads[i].wait()
+        loads[i + 1].wait()
         both = jnp.dot(
             x, wide[:, i * units : (i + 2) * units], preferred_element_type=F32
         )
         gate, up = both[:, :units], both[:, units:]
         hidden.append((gate / (1.0 + jnp.exp(-gate)) * up).astype(BF16))
     hidden = jnp.concatenate(hidden, axis=1)
+    loads[4].wait()
     loads[5].wait()
-    loads[6].wait()
     copies = []
     for i in range(out_ref.shape[0] // PIECE):
         here = pl.ds(i * PIECE, PIECE)
@@ -218,6 +216,7 @@
             [((chunk, sent), BF16)] * 2,
             [extra],
             [plane],
+            keep=[pltpu.HBM] * 2,
         )
 
     panels = []
@@ -230,23 +229,22 @@
             expert_kernel,
             "expert",
             [moved],
-            [off_chip(w) for w in (x, g0, u0, g1, u1, d0, d1)],
+            [x] + [off_chip(w) for w in (g0, u0, g1, u1, d0, d1)],
             keep=[pltpu.HBM],
-            specs=[HBM] * 7,
+            specs=[VMEM] + [HBM] * 6,
             out_specs=[HBM],
             scratch=[
-                pltpu.VMEM(*moved),
                 pltpu.VMEM((g0.shape[0], 4 * g0.shape[1]), BF16),
                 pltpu.VMEM((2 * d0.shape[0], d0.shape[1]), BF16),
                 pltpu.VMEM(*moved),
-                pltpu.SemaphoreType.DMA((7,)),
+                pltpu.SemaphoreType.DMA((6,)),
                 pltpu.SemaphoreType.DMA((pieces,)),
             ],
         )[0]
 
     def combine(home, mix, kinds):
         outs = [((rows, width), kind) for kind in kinds]
-        return kernel_call(combine_kernel, "combine", outs, [home] + list(mix), keep=[pltpu.VMEM] * 4)
+        return kernel_call(combine_kernel, "combine", outs, [home] + [off_chip(m) for m in mix], keep=[pltpu.VMEM] * 4)
 
     def plus(x, part):
         return (x.astype(F32) + part).astype(BF16)

time: 157 us -> 156 us (level)
  Pallas kernels: 25.8 us -> 29.8 us
  local copies, waits for them, and re-layouts: 3.2 us -> 0.01 us
    pallas_call x9, Pallas kernels: 25.8 us -> 29.8 us  [kernel_call(): pl.pallas_call(body, out_shape=[where(*out) for where, out in zip(keep, o...]
    unnamed x10 -> x2, local copies, waits for them, and re-layouts: 3.2 us -> 0.01 us
  transfers between devices with their start and end apart: 20 -> 20, of which waited for: 12 -> 13; matrix products, arithmetic and copies ran while one was open for 0% -> 0% of each run, Pallas kernels for 10% -> 12%
where the time goes in v2:
time: 156 us
  waiting for transfers between devices  64.1 us (41%)
  starting transfers between devices  35.3 us (23%)
  Pallas kernels  29.8 us (19%)
  blocking collectives  25.3 us (16%)
    ppermute x14, waiting for transfers between devices, along_z(): lax.ppermute(x, 'expert', [(i, (i + 2 * by) % col_count) for i in range(c...  47.6 us
    pallas_call x9, Pallas kernels, kernel_call(): pl.pallas_call(body, out_shape=[where(*out) for where, out in zip(keep, o...  29.8 us
    all_to_all x1, blocking collectives, exchange(): return lax.all_to_all(x, 'dp', split_axis=0, concat_axis=0, tiled=True)  25.3 us
    ppermute x14, starting transfers between devices, along_z(): lax.ppermute(x, 'expert', [(i, (i + 2 * by) % col_count) for i in range(c...  20 us
    all_to_all x3, waiting for transfers between devices, exchange(): return lax.all_to_all(x, 'dp', split_axis=0, concat_axis=0, tiled=True)  16.5 us
    all_to_all x3, starting transfers between devices, exchange(): return lax.all_to_all(x, 'dp', split_axis=0, concat_axis=0, tiled=True)  14.8 us
  transfers between devices with their start and end apart: 20, of which 13 were waited for; matrix products, arithmetic and copies ran while one was open for 0% of the time, Pallas kernels for 12%

profile of v2, /device:TPU:96, one launch (start us, length us, event | category | flops | bytes accessed | tf_op | source)
XLA Modules:
  0.0 155.7 jit_solution(16033939578709032640)
XLA Ops:
  1.1 3.2 %collective-permute-start = (bf16[64,2176]{1,0:T(8,128)(2,1)S(1)}, bf16[64,2176]{1,0:T(8,128)(2,1)S(1)}, u32[]{:S(2)}, u32[]{:S(2)}) collective-permute-start(bf16[64,2176]{1,0:T(8,128)(2,1)S(1)} %pack.1.refs_0_), channel_id=1, source_target_pairs={{0,2},{1,3},{2,4},{3,5},{4,6},{5,7},{6,8},{7,9},{8,10},{9,11},{10,... | collective-permute-start | bytes 835592 | tf_op jit(solution)/shard_map/ppermute | solution.py:187
  4.3 5.9 %collective-permute-done.refs_1_ = bf16[64,2176]{1,0:T(8,128)(2,1)S(1)} collective-permute-done((bf16[64,2176]{1,0:T(8,128)(2,1)S(1)}, bf16[64,2176]{1,0:T(8,128)(2,1)S(1)}, u32[]{:S(2)}, u32[]{:S(2)}) %collective-permute-start) | collective-permute-done | bytes 278560 | tf_op jit(solution)/shard_map/ppermute | solution.py:187
  10.2 3.7 %collective-permute-start.2 = (bf16[64,2176]{1,0:T(8,128)(2,1)S(1)}, bf16[64,2176]{1,0:T(8,128)(2,1)S(1)}, u32[]{:S(2)}, u32[]{:S(2)}) collective-permute-start(bf16[64,2176]{1,0:T(8,128)(2,1)S(1)} %collective-permute-done.refs_1_), channel_id=1, source_target_pairs={{0,2},{1,3},{2,4},{3,5},{4,6},{5,7},{6,8},{7,9},{8,10},{9,11},{10,... | collective-permute-start | bytes 835592 | tf_op jit(solution)/shard_map/ppermute | solution.py:187
  13.9 5.0 %collective-permute-done.2.refs_3_ = bf16[64,2176]{1,0:T(8,128)(2,1)S(1)} collective-permute-done((bf16[64,2176]{1,0:T(8,128)(2,1)S(1)}, bf16[64,2176]{1,0:T(8,128)(2,1)S(1)}, u32[]{:S(2)}, u32[]{:S(2)}) %collective-permute-start.2) | collective-permute-done | bytes 278560 | tf_op jit(solution)/shard_map/ppermute | solution.py:187
  22.3 7.2 %all-to-all-start = ((bf16[16,24,2048]{2,1,0:T(8,128)(2,1)}), bf16[16,24,2048]{2,1,0:T(8,128)(2,1)}, u32[]{:S(2)}, u32[]{:S(2)}) async-start(bf16[16,24,2048]{2,1,0:T(8,128)(2,1)} %bitcast.28), calls=%async_computation | async-start | bytes 3145728 | tf_op jit(solution)/shard_map/all_to_all | solution.py:195
  31.8 5.2 %collective-permute-done.4.refs_1_ = bf16[64,2176]{1,0:T(8,128)(2,1)S(1)} collective-permute-done((bf16[64,2176]{1,0:T(8,128)(2,1)S(1)}, bf16[64,2176]{1,0:T(8,128)(2,1)S(1)}, u32[]{:S(2)}, u32[]{:S(2)}) %collective-permute-start.4) | collective-permute-done | bytes 278560 | tf_op jit(solution)/shard_map/ppermute | solution.py:187
  37.0 2.6 %collective-permute-start.6 = (bf16[64,2176]{1,0:T(8,128)(2,1)S(1)}, bf16[64,2176]{1,0:T(8,128)(2,1)S(1)}, u32[]{:S(2)}, u32[]{:S(2)}) collective-permute-start(bf16[64,2176]{1,0:T(8,128)(2,1)S(1)} %collective-permute-done.4.refs_1_), channel_id=1, source_target_pairs={{0,2},{1,3},{2,4},{3,5},{4,6},{5,7},{6,8},{7,9},{8,10},{9,11},{10,... | collective-permute-start | bytes 835592 | tf_op jit(solution)/shard_map/ppermute | solution.py:187
  40.0 3.5 %collective-permute-done.6.refs_3_ = bf16[64,2176]{1,0:T(8,128)(2,1)S(1)} collective-permute-done((bf16[64,2176]{1,0:T(8,128)(2,1)S(1)}, bf16[64,2176]{1,0:T(8,128)(2,1)S(1)}, u32[]{:S(2)}, u32[]{:S(2)}) %collective-permute-start.6) | collective-permute-done | bytes 278560 | tf_op jit(solution)/shard_map/ppermute | solution.py:187
  45.5 5.8 %all-to-all-done = bf16[16,24,2048]{2,1,0:T(8,128)(2,1)} async-done(((bf16[16,24,2048]{2,1,0:T(8,128)(2,1)}), bf16[16,24,2048]{2,1,0:T(8,128)(2,1)}, u32[]{:S(2)}, u32[]{:S(2)}) %all-to-all-start) | async-done | bytes 1572896 | tf_op jit(solution)/shard_map/all_to_all | solution.py:195
  51.3 3.9 %all-to-all-start.1 = ((bf16[16,24,2048]{2,1,0:T(8,128)(2,1)}), bf16[16,24,2048]{2,1,0:T(8,128)(2,1)S(1)}, u32[]{:S(2)}, u32[]{:S(2)}) async-start(bf16[16,24,2048]{2,1,0:T(8,128)(2,1)} %bitcast.29), calls=%async_computation.1 | async-start | bytes 3145728 | tf_op jit(solution)/shard_map/all_to_all | solution.py:195
  58.8 9.2 %expert.2 = bf16[384,2048]{1,0:T(8,128)(2,1)} custom-call(bf16[384,2048]{1,0:T(8,128)(2,1)} %bitcast.4.x_ref, bf16[2048,384]{1,0:T(8,128)(2,1)} %bitcast.17, bf16[2048,384]{1,0:T(8,128)(2,1)} %bitcast.21, bf16[2048,384]{1,0:T(8,128)(2,1)} %collective-permute-done.7.g1, bf16[2048,384]{1,0:T(8,128)(2,1)} %collective-permute-done.8.u1, ...), custom_call_target="tpu_custom_call" | custom-call | tf_op jit(solution)/shard_map/expert/pallas_call | solution.py:36
  68.0 8.9 %all-to-all-done.1 = bf16[16,24,2048]{2,1,0:T(8,128)(2,1)S(1)} async-done(((bf16[16,24,2048]{2,1,0:T(8,128)(2,1)}), bf16[16,24,2048]{2,1,0:T(8,128)(2,1)S(1)}, u32[]{:S(2)}, u32[]{:S(2)}) %all-to-all-start.1) | async-done | bytes 1572896 | tf_op jit(solution)/shard_map/all_to_all | solution.py:195
  76.8 7.7 %expert.3 = bf16[384,2048]{1,0:T(8,128)(2,1)} custom-call(bf16[384,2048]{1,0:T(8,128)(2,1)S(1)} %bitcast.14, bf16[2048,384]{1,0:T(8,128)(2,1)} %bitcast.18, bf16[2048,384]{1,0:T(8,128)(2,1)} %bitcast.22, bf16[2048,384]{1,0:T(8,128)(2,1)} %collective-permute-done.7.g1, bf16[2048,384]{1,0:T(8,128)(2,1)} %collective-permute-done.8.u1, ...), custom_call_target="tpu_custom_call" | custom-call | tf_op jit(solution)/shard_map/expert/pallas_call | solution.py:36
  84.6 25.3 %all_to_all.46 = bf16[16,24,2048]{2,1,0:T(8,128)(2,1)S(1)} all-to-all(bf16[16,24,2048]{2,1,0:T(8,128)(2,1)} %bitcast.27), channel_id=1, replica_groups=mesh['dp'=16,'expert'=16] {'dp'}, dimensions={0} | all-to-all | bytes 3145728 | tf_op jit(solution)/shard_map/all_to_all | solution.py:195
  109.8 3.7 %all-to-all-start.3 = ((bf16[16,24,2048]{2,1,0:T(8,128)(2,1)}), bf16[16,24,2048]{2,1,0:T(8,128)(2,1)S(1)}, u32[]{:S(2)}, u32[]{:S(2)}) async-start(bf16[16,24,2048]{2,1,0:T(8,128)(2,1)} %bitcast.26), calls=%async_computation.3 | async-start | bytes 3145728 | tf_op jit(solution)/shard_map/all_to_all | solution.py:195
  113.6 2.3 %combine.2 = (f32[64,2048]{1,0:T(8,128)S(1)}, f32[64,2048]{1,0:T(8,128)S(1)}, bf16[64,2048]{1,0:T(8,128)(2,1)S(1)}, bf16[64,2048]{1,0:T(8,128)(2,1)S(1)}) custom-call(bf16[384,2048]{1,0:T(8,128)(2,1)S(1)} %bitcast.16, bf16[256,384]{1,0:T(8,128)(2,1)} %get-tuple-element.36.high_ref, bf16[256,384]{1,0:T(8,128)(2,1)} %get-tuple-element.37.low_ref), custom_call_target="tpu_custom_call" | custom-call | tf_op jit(solution)/shard_map/combine/pallas_call | solution.py:36
  118.0 5.0 %collective-permute-done.12 = bf16[64,2048]{1,0:T(8,128)(2,1)S(1)} collective-permute-done((bf16[64,2048]{1,0:T(8,128)(2,1)S(1)}, bf16[64,2048]{1,0:T(8,128)(2,1)S(1)}, u32[]{:S(2)}, u32[]{:S(2)}) %collective-permute-start.12) | collective-permute-done | bytes 262176 | tf_op jit(solution)/shard_map/ppermute | solution.py:187
  123.0 2.7 %collective-permute-start.13 = (bf16[64,2048]{1,0:T(8,128)(2,1)S(1)}, bf16[64,2048]{1,0:T(8,128)(2,1)S(1)}, u32[]{:S(2)}, u32[]{:S(2)}) collective-permute-start(bf16[64,2048]{1,0:T(8,128)(2,1)S(1)} %add_convert_fusion.3), channel_id=1, source_target_pairs={{0,2},{1,3},{2,4},{3,5},{4,6},{5,7},{6,8},{7,9},{8,10},{9,11},{10,... | collective-permute-start | bytes 786440 | tf_op jit(solution)/shard_map/ppermute | solution.py:187
  125.8 3.7 %collective-permute-done.13 = bf16[64,2048]{1,0:T(8,128)(2,1)S(1)} collective-permute-done((bf16[64,2048]{1,0:T(8,128)(2,1)S(1)}, bf16[64,2048]{1,0:T(8,128)(2,1)S(1)}, u32[]{:S(2)}, u32[]{:S(2)}) %collective-permute-start.13) | collective-permute-done | bytes 262176 | tf_op jit(solution)/shard_map/ppermute | solution.py:187
  129.6 3.8 %collective-permute-done.11 = bf16[64,2048]{1,0:T(8,128)(2,1)S(1)} collective-permute-done((bf16[64,2048]{1,0:T(8,128)(2,1)S(1)}, bf16[64,2048]{1,0:T(8,128)(2,1)S(1)}, u32[]{:S(2)}, u32[]{:S(2)}) %collective-permute-start.11) | collective-permute-done | bytes 262176 | tf_op jit(solution)/shard_map/ppermute | solution.py:187
  135.2 2.3 %combine.3 = (f32[64,2048]{1,0:T(8,128)S(1)}, f32[64,2048]{1,0:T(8,128)S(1)}, f32[64,2048]{1,0:T(8,128)S(1)}, f32[64,2048]{1,0:T(8,128)S(1)}) custom-call(bf16[384,2048]{1,0:T(8,128)(2,1)S(1)} %bitcast.15, bf16[256,384]{1,0:T(8,128)(2,1)} %get-tuple-element.33.high_ref, bf16[256,384]{1,0:T(8,128)(2,1)} %get-tuple-element.34.low_ref), custom_call_target="tpu_custom_call" | custom-call | tf_op jit(solution)/shard_map/combine/pallas_call | solution.py:36
  137.7 3.3 %collective-permute-start.14 = (bf16[64,2048]{1,0:T(8,128)(2,1)S(1)}, bf16[64,2048]{1,0:T(8,128)(2,1)S(1)}, u32[]{:S(2)}, u32[]{:S(2)}) collective-permute-start(bf16[64,2048]{1,0:T(8,128)(2,1)S(1)} %add_convert_fusion.2), channel_id=1, source_target_pairs={{0,2},{1,3},{2,4},{3,5},{4,6},{5,7},{6,8},{7,9},{8,10},{9,11},{10,... | collective-permute-start | bytes 786440 | tf_op jit(solution)/shard_map/ppermute | solution.py:187
  141.0 6.1 %collective-permute-done.15 = bf16[64,2048]{1,0:T(8,128)(2,1)S(1)} collective-permute-done((bf16[64,2048]{1,0:T(8,128)(2,1)S(1)}, bf16[64,2048]{1,0:T(8,128)(2,1)S(1)}, u32[]{:S(2)}, u32[]{:S(2)}) %collective-permute-start.15) | collective-permute-done | bytes 262176 | tf_op jit(solution)/shard_map/ppermute | solution.py:187
  147.3 7.6 %collective-permute-done.16 = bf16[64,2048]{1,0:T(8,128)(2,1)S(1)} collective-permute-done((bf16[64,2048]{1,0:T(8,128)(2,1)S(1)}, bf16[64,2048]{1,0:T(8,128)(2,1)S(1)}, u32[]{:S(2)}, u32[]{:S(2)}) %collective-permute-start.16) | collective-permute-done | bytes 262176 | tf_op jit(solution)/shard_map/ppermute | solution.py:187
  (34 shorter events, 18.0 us)
Async XLA Ops:
  1.1 9.1 %collective-permute-start = (bf16[64,2176]{1,0:T(8,128)(2,1)S(1)}, bf16[64,2176]{1,0:T(8,128)(2,1)S(1)}, u32[]{:S(2)}, u32[]{:S(2)}) collective-permute-start(bf16[64,2176]{1,0:T(8,128)(2,1)S(1)} %pack.1.refs_0_), channel_id=1, source_target_pairs={{0,2},{1,3},{2,4},{3,5},{4,6},{5,7},{6,8},{7,9},{8,10},{9,11},{10,... | collective-permute-start | bytes 835592 | tf_op jit(solution)/shard_map/ppermute | solution.py:187
  4.3 9.6 %collective-permute-start.1 = (bf16[64,2176]{1,0:T(8,128)(2,1)S(1)}, bf16[64,2176]{1,0:T(8,128)(2,1)S(1)}, u32[]{:S(2)}, u32[]{:S(2)}) collective-permute-start(bf16[64,2176]{1,0:T(8,128)(2,1)S(1)} %pack.1.refs_0_), channel_id=1, source_target_pairs={{0,14},{1,15},{2,0},{3,1},{4,2},{5,3},{6,4},{7,5},{8,6},{9,7},{10,... | collective-permute-start | bytes 835592 | tf_op jit(solution)/shard_map/ppermute | solution.py:187
  10.2 8.7 %collective-permute-start.2 = (bf16[64,2176]{1,0:T(8,128)(2,1)S(1)}, bf16[64,2176]{1,0:T(8,128)(2,1)S(1)}, u32[]{:S(2)}, u32[]{:S(2)}) collective-permute-start(bf16[64,2176]{1,0:T(8,128)(2,1)S(1)} %collective-permute-done.refs_1_), channel_id=1, source_target_pairs={{0,2},{1,3},{2,4},{3,5},{4,6},{5,7},{6,8},{7,9},{8,10},{9,11},{10,... | collective-permute-start | bytes 835592 | tf_op jit(solution)/shard_map/ppermute | solution.py:187
  13.9 8.5 %collective-permute-start.3 = (bf16[64,2176]{1,0:T(8,128)(2,1)S(1)}, bf16[64,2176]{1,0:T(8,128)(2,1)S(1)}, u32[]{:S(2)}, u32[]{:S(2)}) collective-permute-start(bf16[64,2176]{1,0:T(8,128)(2,1)S(1)} %collective-permute-done.1.refs_2_), channel_id=1, source_target_pairs={{0,14},{1,15},{2,0},{3,1},{4,2},{5,3},{6,4},{7,5},{8,6},{9,7},{10,... | collective-permute-start | bytes 835592 | tf_op jit(solution)/shard_map/ppermute | solution.py:187
  22.3 17.2 %copy-start = (bf16[1,2048,384]{2,1,0:T(8,128)(2,1)S(1)}, bf16[1,2048,384]{2,1,0:T(8,128)(2,1)}, u32[]{:S(2)}) copy-start(bf16[1,2048,384]{2,1,0:T(8,128)(2,1)} %param.9) | copy-start | bytes 4718596
  22.3 29.0 %all-to-all-start = ((bf16[16,24,2048]{2,1,0:T(8,128)(2,1)}), bf16[16,24,2048]{2,1,0:T(8,128)(2,1)}, u32[]{:S(2)}, u32[]{:S(2)}) async-start(bf16[16,24,2048]{2,1,0:T(8,128)(2,1)} %bitcast.28), calls=%async_computation | async-start | bytes 3145728 | tf_op jit(solution)/shard_map/all_to_all | solution.py:195
  29.6 7.4 %collective-permute-start.4 = (bf16[64,2176]{1,0:T(8,128)(2,1)S(1)}, bf16[64,2176]{1,0:T(8,128)(2,1)S(1)}, u32[]{:S(2)}, u32[]{:S(2)}) collective-permute-start(bf16[64,2176]{1,0:T(8,128)(2,1)S(1)} %collective-permute-done.2.refs_3_), channel_id=1, source_target_pairs={{0,2},{1,3},{2,4},{3,5},{4,6},{5,7},{6,8},{7,9},{8,10},{9,11},{10,... | collective-permute-start | bytes 835592 | tf_op jit(solution)/shard_map/ppermute | solution.py:187
  31.8 8.3 %collective-permute-start.5 = (bf16[64,2176]{1,0:T(8,128)(2,1)S(1)}, bf16[64,2176]{1,0:T(8,128)(2,1)S(1)}, u32[]{:S(2)}, u32[]{:S(2)}) collective-permute-start(bf16[64,2176]{1,0:T(8,128)(2,1)S(1)} %collective-permute-done.3.refs_0_), channel_id=1, source_target_pairs={{0,14},{1,15},{2,0},{3,1},{4,2},{5,3},{6,4},{7,5},{8,6},{9,7},{10,... | collective-permute-start | bytes 835592 | tf_op jit(solution)/shard_map/ppermute | solution.py:187
  37.0 6.6 %collective-permute-start.6 = (bf16[64,2176]{1,0:T(8,128)(2,1)S(1)}, bf16[64,2176]{1,0:T(8,128)(2,1)S(1)}, u32[]{:S(2)}, u32[]{:S(2)}) collective-permute-start(bf16[64,2176]{1,0:T(8,128)(2,1)S(1)} %collective-permute-done.4.refs_1_), channel_id=1, source_target_pairs={{0,2},{1,3},{2,4},{3,5},{4,6},{5,7},{6,8},{7,9},{8,10},{9,11},{10,... | collective-permute-start | bytes 835592 | tf_op jit(solution)/shard_map/ppermute | solution.py:187
  39.5 19.3 %collective-permute-start.7 = (bf16[2048,384]{1,0:T(8,128)(2,1)S(1)}, bf16[2048,384]{1,0:T(8,128)(2,1)}, u32[]{:S(2)}, u32[]{:S(2)}) collective-permute-start(bf16[2048,384]{1,0:T(8,128)(2,1)S(1)} %bitcast.19), channel_id=1, source_target_pairs={{0,1},{1,0},{2,3},{3,2},{4,5},{5,4},{6,7},{7,6},{8,9},{9,8},{10,11... | collective-permute-start | bytes 4718600 | tf_op jit(solution)/shard_map/ppermute | solution.py:192
  39.5 19.3 %collective-permute-start.8 = (bf16[2048,384]{1,0:T(8,128)(2,1)}, bf16[2048,384]{1,0:T(8,128)(2,1)}, u32[]{:S(2)}, u32[]{:S(2)}) collective-permute-start(bf16[2048,384]{1,0:T(8,128)(2,1)} %bitcast.20), channel_id=1, source_target_pairs={{0,1},{1,0},{2,3},{3,2},{4,5},{5,4},{6,7},{7,6},{8,9},{9,8},{10,11... | collective-permute-start | bytes 4718600 | tf_op jit(solution)/shard_map/ppermute | solution.py:192
  40.0 18.8 %collective-permute-start.9 = (bf16[384,2048]{1,0:T(8,128)(2,1)}, bf16[384,2048]{1,0:T(8,128)(2,1)}, u32[]{:S(2)}, u32[]{:S(2)}) collective-permute-start(bf16[384,2048]{1,0:T(8,128)(2,1)} %bitcast.23), channel_id=1, source_target_pairs={{0,1},{1,0},{2,3},{3,2},{4,5},{5,4},{6,7},{7,6},{8,9},{9,8},{10,11... | collective-permute-start | bytes 4718600 | tf_op jit(solution)/shard_map/ppermute | solution.py:192
  51.3 25.5 %all-to-all-start.1 = ((bf16[16,24,2048]{2,1,0:T(8,128)(2,1)}), bf16[16,24,2048]{2,1,0:T(8,128)(2,1)S(1)}, u32[]{:S(2)}, u32[]{:S(2)}) async-start(bf16[16,24,2048]{2,1,0:T(8,128)(2,1)} %bitcast.29), calls=%async_computation.1 | async-start | bytes 3145728 | tf_op jit(solution)/shard_map/all_to_all | solution.py:195
  109.8 25.4 %all-to-all-start.3 = ((bf16[16,24,2048]{2,1,0:T(8,128)(2,1)}), bf16[16,24,2048]{2,1,0:T(8,128)(2,1)S(1)}, u32[]{:S(2)}, u32[]{:S(2)}) async-start(bf16[16,24,2048]{2,1,0:T(8,128)(2,1)} %bitcast.26), calls=%async_computation.3 | async-start | bytes 3145728 | tf_op jit(solution)/shard_map/all_to_all | solution.py:195
  115.8 7.1 %collective-permute-start.12 = (bf16[64,2048]{1,0:T(8,128)(2,1)S(1)}, bf16[64,2048]{1,0:T(8,128)(2,1)S(1)}, u32[]{:S(2)}, u32[]{:S(2)}) collective-permute-start(bf16[64,2048]{1,0:T(8,128)(2,1)S(1)} %get-tuple-element.42), channel_id=1, source_target_pairs={{0,2},{1,3},{2,4},{3,5},{4,6},{5,7},{6,8},{7,9},{8,10},{9,11},{10,... | collective-permute-start | bytes 786440 | tf_op jit(solution)/shard_map/ppermute | solution.py:187
  118.0 7.7 %collective-permute-start.10 = (bf16[64,2048]{1,0:T(8,128)(2,1)S(1)}, bf16[64,2048]{1,0:T(8,128)(2,1)S(1)}, u32[]{:S(2)}, u32[]{:S(2)}) collective-permute-start(bf16[64,2048]{1,0:T(8,128)(2,1)S(1)} %get-tuple-element.40), channel_id=1, source_target_pairs={{0,14},{1,15},{2,0},{3,1},{4,2},{5,3},{6,4},{7,5},{8,6},{9,7},{10,... | collective-permute-start | bytes 786440 | tf_op jit(solution)/shard_map/ppermute | solution.py:187
  123.0 6.6 %collective-permute-start.13 = (bf16[64,2048]{1,0:T(8,128)(2,1)S(1)}, bf16[64,2048]{1,0:T(8,128)(2,1)S(1)}, u32[]{:S(2)}, u32[]{:S(2)}) collective-permute-start(bf16[64,2048]{1,0:T(8,128)(2,1)S(1)} %add_convert_fusion.3), channel_id=1, source_target_pairs={{0,2},{1,3},{2,4},{3,5},{4,6},{5,7},{6,8},{7,9},{8,10},{9,11},{10,... | collective-permute-start | bytes 786440 | tf_op jit(solution)/shard_map/ppermute | solution.py:187
  125.7 7.7 %collective-permute-start.11 = (bf16[64,2048]{1,0:T(8,128)(2,1)S(1)}, bf16[64,2048]{1,0:T(8,128)(2,1)S(1)}, u32[]{:S(2)}, u32[]{:S(2)}) collective-permute-start(bf16[64,2048]{1,0:T(8,128)(2,1)S(1)} %add_convert_fusion.4), channel_id=1, source_target_pairs={{0,14},{1,15},{2,0},{3,1},{4,2},{5,3},{6,4},{7,5},{8,6},{9,7},{10,... | collective-permute-start | bytes 786440 | tf_op jit(solution)/shard_map/ppermute | solution.py:187
  137.5 9.6 %collective-permute-start.15 = (bf16[64,2048]{1,0:T(8,128)(2,1)S(1)}, bf16[64,2048]{1,0:T(8,128)(2,1)S(1)}, u32[]{:S(2)}, u32[]{:S(2)}) collective-permute-start(bf16[64,2048]{1,0:T(8,128)(2,1)S(1)} %add_convert_fusion.1), channel_id=1, source_target_pairs={{0,14},{1,15},{2,0},{3,1},{4,2},{5,3},{6,4},{7,5},{8,6},{9,7},{10,... | collective-permute-start | bytes 786440 | tf_op jit(solution)/shard_map/ppermute | solution.py:187
  137.7 9.6 %collective-permute-start.14 = (bf16[64,2048]{1,0:T(8,128)(2,1)S(1)}, bf16[64,2048]{1,0:T(8,128)(2,1)S(1)}, u32[]{:S(2)}, u32[]{:S(2)}) collective-permute-start(bf16[64,2048]{1,0:T(8,128)(2,1)S(1)} %add_convert_fusion.2), channel_id=1, source_target_pairs={{0,2},{1,3},{2,4},{3,5},{4,6},{5,7},{6,8},{7,9},{8,10},{9,11},{10,... | collective-permute-start | bytes 786440 | tf_op jit(solution)/shard_map/ppermute | solution.py:187
  147.2 7.7 %collective-permute-start.16 = (bf16[64,2048]{1,0:T(8,128)(2,1)S(1)}, bf16[64,2048]{1,0:T(8,128)(2,1)S(1)}, u32[]{:S(2)}, u32[]{:S(2)}) collective-permute-start(bf16[64,2048]{1,0:T(8,128)(2,1)S(1)} %add_convert_fusion), channel_id=1, source_target_pairs={{0,14},{1,15},{2,0},{3,1},{4,2},{5,3},{6,4},{7,5},{8,6},{9,7},{10,... | collective-permute-start | bytes 786440 | tf_op jit(solution)/shard_map/ppermute | solution.py:187

commit v3 on v2

--- a/solution.py
+++ b/solution.py
@@ -130,8 +130,8 @@
         copy.wait()
 
 
-def weights_kernel(slots, planes, z_ref, extra_ref, high_ref, low_ref):
-    tokens, columns = high_ref.shape
+def weights_kernel(slots, planes, z_ref, extra_ref, out_ref):
+    tokens, columns = extra_ref.shape[0], out_ref.shape[1]
     groups = columns // slots
     extra = extra_ref[...].astype(F32)
     gates = extra[:, 8:16] * 256.0 + extra[:, 16:24]
@@ -156,15 +156,15 @@
     here = wanted == (place + 1).astype(F32)
     high = weight.astype(BF16)
     low = (weight - high.astype(F32)).astype(BF16)
-    for piece, ref in ((high, high_ref), (low, low_ref)):
+    for i, piece in enumerate((high, low)):
         wide = jnp.dot(piece, spread, preferred_element_type=F32)
-        ref[...] = jnp.where(here, wide, 0.0).astype(BF16)
-
-
-def combine_kernel(home_ref, high_ref, low_ref, *outs):
-    home = home_ref[...]
-    total = jnp.dot(high_ref[...], home, preferred_element_type=F32)
-    total = total + jnp.dot(low_ref[...], home, preferred_element_type=F32)
+        out_ref[pl.ds(i * tokens, tokens), :] = jnp.where(here, wide, 0.0).astype(BF16)
+
+
+def combine_kernel(home_ref, mix_ref, *outs):
+    tokens = mix_ref.shape[0] // 2
+    total = jnp.dot(mix_ref[...], home_ref[...], preferred_element_type=F32)
+    total = total[:tokens, :] + total[tokens:, :]
     start = 0
     for out in outs:
         rows = out.shape[0]
@@ -213,11 +213,11 @@
         return kernel_call(
             functools.partial(weights_kernel, slots, planes),
             "mixing",
-            [((chunk, sent), BF16)] * 2,
+            [((2 * chunk, sent), BF16)],
             [extra],
             [plane],
-            keep=[pltpu.HBM] * 2,
-        )
+            keep=[pltpu.HBM],
+        )[0]
 
     panels = []
     for w in (w_gate[0], w_up[0], w_down[0]):
@@ -244,7 +244,7 @@
 
     def combine(home, mix, kinds):
         outs = [((rows, width), kind) for kind in kinds]
-        return kernel_call(combine_kernel, "combine", outs, [home] + [off_chip(m) for m in mix], keep=[pltpu.VMEM] * 4)
+        return kernel_call(combine_kernel, "combine", outs, [home, mix], keep=[pltpu.VMEM] * 4)
 
     def plus(x, part):
         return (x.astype(F32) + part).astype(BF16)
@@ -268,14 +268,14 @@
     far = exchange(far_rows)
     near_out = after(expert(near), far)
     near_mix, far_mix = mixing(near_extra), mixing(far_extra)
-    far_out = after(expert(far), near_out, *near_mix, *far_mix)
+    far_out = after(expert(far), near_out, near_mix, far_mix)
     far_home = exchange(far_out)
     near_home = exchange(after(near_out, far_home))
-    to_high_2, to_low_3, to_high_3, to_low_4 = combine(far_home, far_mix, [F32, F32, BF16, BF16])
+    to_high_2, to_low_3, to_high_3, to_low_4 = combine(far_home, off_chip(far_mix), [F32, F32, BF16, BF16])
     down, up = along_z(to_low_4, -1), along_z(to_high_3, 1)
     down, up = along_z(plus(down, to_low_3), -1), along_z(plus(up, to_high_2), 1)
     near_home = after(near_home, down, up)
-    own, to_low_1, to_high_1, to_low_2 = combine(near_home, near_mix, [F32] * 4)
+    own, to_low_1, to_high_1, to_low_2 = combine(near_home, off_chip(near_mix), [F32] * 4)
     down, up = along_z(plus(down, to_low_2), -1), along_z(plus(up, to_high_1), 1)
     down = along_z(plus(down, to_low_1), -1)
     return own + up.astype(F32) + down.astype(F32)

time: 156 us -> 156 us (level)
  no operation moved by 1% of the time
where the time goes in v3:
time: 156 us
  waiting for transfers between devices  64 us (41%)
  starting transfers between devices  35.3 us (23%)
  Pallas kernels  29.8 us (19%)
  blocking collectives  25.3 us (16%)
    ppermute x14, waiting for transfers between devices, along_z(): lax.ppermute(x, 'expert', [(i, (i + 2 * by) % col_count) for i in range(c...  47.6 us
    pallas_call x9, Pallas kernels, kernel_call(): pl.pallas_call(body, out_shape=[where(*out) for where, out in zip(keep, o...  29.8 us
    all_to_all x1, blocking collectives, exchange(): return lax.all_to_all(x, 'dp', split_axis=0, concat_axis=0, tiled=True)  25.3 us
    ppermute x14, starting transfers between devices, along_z(): lax.ppermute(x, 'expert', [(i, (i + 2 * by) % col_count) for i in range(c...  20 us
    all_to_all x3, waiting for transfers between devices, exchange(): return lax.all_to_all(x, 'dp', split_axis=0, concat_axis=0, tiled=True)  16.4 us
    all_to_all x3, starting transfers between devices, exchange(): return lax.all_to_all(x, 'dp', split_axis=0, concat_axis=0, tiled=True)  14.8 us
  transfers between devices with their start and end apart: 20, of which 13 were waited for; matrix products, arithmetic and copies ran while one was open for 0% of the time, Pallas kernels for 12%

profile of v3, /device:TPU:96, one launch (start us, length us, event | category | flops | bytes accessed | tf_op | source)
XLA Modules:
  0.0 155.7 jit_solution(9916956649077264082)
XLA Ops:
  1.1 3.2 %collective-permute-start = (bf16[64,2176]{1,0:T(8,128)(2,1)S(1)}, bf16[64,2176]{1,0:T(8,128)(2,1)S(1)}, u32[]{:S(2)}, u32[]{:S(2)}) collective-permute-start(bf16[64,2176]{1,0:T(8,128)(2,1)S(1)} %pack.1.refs_0_), channel_id=1, source_target_pairs={{0,2},{1,3},{2,4},{3,5},{4,6},{5,7},{6,8},{7,9},{8,10},{9,11},{10,... | collective-permute-start | bytes 835592 | tf_op jit(solution)/shard_map/ppermute | solution.py:187
  4.3 5.9 %collective-permute-done.refs_1_ = bf16[64,2176]{1,0:T(8,128)(2,1)S(1)} collective-permute-done((bf16[64,2176]{1,0:T(8,128)(2,1)S(1)}, bf16[64,2176]{1,0:T(8,128)(2,1)S(1)}, u32[]{:S(2)}, u32[]{:S(2)}) %collective-permute-start) | collective-permute-done | bytes 278560 | tf_op jit(solution)/shard_map/ppermute | solution.py:187
  10.2 3.7 %collective-permute-start.2 = (bf16[64,2176]{1,0:T(8,128)(2,1)S(1)}, bf16[64,2176]{1,0:T(8,128)(2,1)S(1)}, u32[]{:S(2)}, u32[]{:S(2)}) collective-permute-start(bf16[64,2176]{1,0:T(8,128)(2,1)S(1)} %collective-permute-done.refs_1_), channel_id=1, source_target_pairs={{0,2},{1,3},{2,4},{3,5},{4,6},{5,7},{6,8},{7,9},{8,10},{9,11},{10,... | collective-permute-start | bytes 835592 | tf_op jit(solution)/shard_map/ppermute | solution.py:187
  13.9 5.0 %collective-permute-done.2.refs_3_ = bf16[64,2176]{1,0:T(8,128)(2,1)S(1)} collective-permute-done((bf16[64,2176]{1,0:T(8,128)(2,1)S(1)}, bf16[64,2176]{1,0:T(8,128)(2,1)S(1)}, u32[]{:S(2)}, u32[]{:S(2)}) %collective-permute-start.2) | collective-permute-done | bytes 278560 | tf_op jit(solution)/shard_map/ppermute | solution.py:187
  22.3 7.2 %all-to-all-start = ((bf16[16,24,2048]{2,1,0:T(8,128)(2,1)}), bf16[16,24,2048]{2,1,0:T(8,128)(2,1)}, u32[]{:S(2)}, u32[]{:S(2)}) async-start(bf16[16,24,2048]{2,1,0:T(8,128)(2,1)} %bitcast.28), calls=%async_computation | async-start | bytes 3145728 | tf_op jit(solution)/shard_map/all_to_all | solution.py:195
  31.8 5.2 %collective-permute-done.4.refs_1_ = bf16[64,2176]{1,0:T(8,128)(2,1)S(1)} collective-permute-done((bf16[64,2176]{1,0:T(8,128)(2,1)S(1)}, bf16[64,2176]{1,0:T(8,128)(2,1)S(1)}, u32[]{:S(2)}, u32[]{:S(2)}) %collective-permute-start.4) | collective-permute-done | bytes 278560 | tf_op jit(solution)/shard_map/ppermute | solution.py:187
  37.0 2.5 %collective-permute-start.6 = (bf16[64,2176]{1,0:T(8,128)(2,1)S(1)}, bf16[64,2176]{1,0:T(8,128)(2,1)S(1)}, u32[]{:S(2)}, u32[]{:S(2)}) collective-permute-start(bf16[64,2176]{1,0:T(8,128)(2,1)S(1)} %collective-permute-done.4.refs_1_), channel_id=1, source_target_pairs={{0,2},{1,3},{2,4},{3,5},{4,6},{5,7},{6,8},{7,9},{8,10},{9,11},{10,... | collective-permute-start | bytes 835592 | tf_op jit(solution)/shard_map/ppermute | solution.py:187
  40.0 3.5 %collective-permute-done.6.refs_3_ = bf16[64,2176]{1,0:T(8,128)(2,1)S(1)} collective-permute-done((bf16[64,2176]{1,0:T(8,128)(2,1)S(1)}, bf16[64,2176]{1,0:T(8,128)(2,1)S(1)}, u32[]{:S(2)}, u32[]{:S(2)}) %collective-permute-start.6) | collective-permute-done | bytes 278560 | tf_op jit(solution)/shard_map/ppermute | solution.py:187
  45.5 5.8 %all-to-all-done = bf16[16,24,2048]{2,1,0:T(8,128)(2,1)} async-done(((bf16[16,24,2048]{2,1,0:T(8,128)(2,1)}), bf16[16,24,2048]{2,1,0:T(8,128)(2,1)}, u32[]{:S(2)}, u32[]{:S(2)}) %all-to-all-start) | async-done | bytes 1572896 | tf_op jit(solution)/shard_map/all_to_all | solution.py:195
  51.3 3.9 %all-to-all-start.1 = ((bf16[16,24,2048]{2,1,0:T(8,128)(2,1)}), bf16[16,24,2048]{2,1,0:T(8,128)(2,1)S(1)}, u32[]{:S(2)}, u32[]{:S(2)}) async-start(bf16[16,24,2048]{2,1,0:T(8,128)(2,1)} %bitcast.29), calls=%async_computation.1 | async-start | bytes 3145728 | tf_op jit(solution)/shard_map/all_to_all | solution.py:195
  58.9 9.1 %expert.2 = bf16[384,2048]{1,0:T(8,128)(2,1)} custom-call(bf16[384,2048]{1,0:T(8,128)(2,1)} %bitcast.4.x_ref, bf16[2048,384]{1,0:T(8,128)(2,1)} %bitcast.17, bf16[2048,384]{1,0:T(8,128)(2,1)} %bitcast.21, bf16[2048,384]{1,0:T(8,128)(2,1)} %collective-permute-done.7.g1, bf16[2048,384]{1,0:T(8,128)(2,1)} %collective-permute-done.8.u1, ...), custom_call_target="tpu_custom_call" | custom-call | tf_op jit(solution)/shard_map/expert/pallas_call | solution.py:36
  68.1 8.8 %all-to-all-done.1 = bf16[16,24,2048]{2,1,0:T(8,128)(2,1)S(1)} async-done(((bf16[16,24,2048]{2,1,0:T(8,128)(2,1)}), bf16[16,24,2048]{2,1,0:T(8,128)(2,1)S(1)}, u32[]{:S(2)}, u32[]{:S(2)}) %all-to-all-start.1) | async-done | bytes 1572896 | tf_op jit(solution)/shard_map/all_to_all | solution.py:195
  76.8 7.7 %expert.3 = bf16[384,2048]{1,0:T(8,128)(2,1)} custom-call(bf16[384,2048]{1,0:T(8,128)(2,1)S(1)} %bitcast.14, bf16[2048,384]{1,0:T(8,128)(2,1)} %bitcast.18, bf16[2048,384]{1,0:T(8,128)(2,1)} %bitcast.22, bf16[2048,384]{1,0:T(8,128)(2,1)} %collective-permute-done.7.g1, bf16[2048,384]{1,0:T(8,128)(2,1)} %collective-permute-done.8.u1, ...), custom_call_target="tpu_custom_call" | custom-call | tf_op jit(solution)/shard_map/expert/pallas_call | solution.py:36
  84.6 25.3 %all_to_all.46 = bf16[16,24,2048]{2,1,0:T(8,128)(2,1)S(1)} all-to-all(bf16[16,24,2048]{2,1,0:T(8,128)(2,1)} %bitcast.27), channel_id=1, replica_groups=mesh['dp'=16,'expert'=16] {'dp'}, dimensions={0} | all-to-all | bytes 3145728 | tf_op jit(solution)/shard_map/all_to_all | solution.py:195
  109.8 3.7 %all-to-all-start.3 = ((bf16[16,24,2048]{2,1,0:T(8,128)(2,1)}), bf16[16,24,2048]{2,1,0:T(8,128)(2,1)S(1)}, u32[]{:S(2)}, u32[]{:S(2)}) async-start(bf16[16,24,2048]{2,1,0:T(8,128)(2,1)} %bitcast.26), calls=%async_computation.3 | async-start | bytes 3145728 | tf_op jit(solution)/shard_map/all_to_all | solution.py:195
  113.6 2.2 %combine.2 = (f32[64,2048]{1,0:T(8,128)S(1)}, f32[64,2048]{1,0:T(8,128)S(1)}, bf16[64,2048]{1,0:T(8,128)(2,1)S(1)}, bf16[64,2048]{1,0:T(8,128)(2,1)S(1)}) custom-call(bf16[384,2048]{1,0:T(8,128)(2,1)S(1)} %bitcast.16, bf16[512,384]{1,0:T(8,128)(2,1)} %mixing.3.mix_ref), custom_call_target="tpu_custom_call" | custom-call | tf_op jit(solution)/shard_map/combine/pallas_call | solution.py:36
  117.9 5.0 %collective-permute-done.12 = bf16[64,2048]{1,0:T(8,128)(2,1)S(1)} collective-permute-done((bf16[64,2048]{1,0:T(8,128)(2,1)S(1)}, bf16[64,2048]{1,0:T(8,128)(2,1)S(1)}, u32[]{:S(2)}, u32[]{:S(2)}) %collective-permute-start.12) | collective-permute-done | bytes 262176 | tf_op jit(solution)/shard_map/ppermute | solution.py:187
  123.0 2.7 %collective-permute-start.13 = (bf16[64,2048]{1,0:T(8,128)(2,1)S(1)}, bf16[64,2048]{1,0:T(8,128)(2,1)S(1)}, u32[]{:S(2)}, u32[]{:S(2)}) collective-permute-start(bf16[64,2048]{1,0:T(8,128)(2,1)S(1)} %add_convert_fusion.3), channel_id=1, source_target_pairs={{0,2},{1,3},{2,4},{3,5},{4,6},{5,7},{6,8},{7,9},{8,10},{9,11},{10,... | collective-permute-start | bytes 786440 | tf_op jit(solution)/shard_map/ppermute | solution.py:187
  125.8 3.7 %collective-permute-done.13 = bf16[64,2048]{1,0:T(8,128)(2,1)S(1)} collective-permute-done((bf16[64,2048]{1,0:T(8,128)(2,1)S(1)}, bf16[64,2048]{1,0:T(8,128)(2,1)S(1)}, u32[]{:S(2)}, u32[]{:S(2)}) %collective-permute-start.13) | collective-permute-done | bytes 262176 | tf_op jit(solution)/shard_map/ppermute | solution.py:187
  129.5 3.8 %collective-permute-done.11 = bf16[64,2048]{1,0:T(8,128)(2,1)S(1)} collective-permute-done((bf16[64,2048]{1,0:T(8,128)(2,1)S(1)}, bf16[64,2048]{1,0:T(8,128)(2,1)S(1)}, u32[]{:S(2)}, u32[]{:S(2)}) %collective-permute-start.11) | collective-permute-done | bytes 262176 | tf_op jit(solution)/shard_map/ppermute | solution.py:187
  135.2 2.2 %combine.3 = (f32[64,2048]{1,0:T(8,128)S(1)}, f32[64,2048]{1,0:T(8,128)S(1)}, f32[64,2048]{1,0:T(8,128)S(1)}, f32[64,2048]{1,0:T(8,128)S(1)}) custom-call(bf16[384,2048]{1,0:T(8,128)(2,1)S(1)} %bitcast.15, bf16[512,384]{1,0:T(8,128)(2,1)} %mixing.2.mix_ref), custom_call_target="tpu_custom_call" | custom-call | tf_op jit(solution)/shard_map/combine/pallas_call | solution.py:36
  137.6 3.3 %collective-permute-start.14 = (bf16[64,2048]{1,0:T(8,128)(2,1)S(1)}, bf16[64,2048]{1,0:T(8,128)(2,1)S(1)}, u32[]{:S(2)}, u32[]{:S(2)}) collective-permute-start(bf16[64,2048]{1,0:T(8,128)(2,1)S(1)} %add_convert_fusion.2), channel_id=1, source_target_pairs={{0,2},{1,3},{2,4},{3,5},{4,6},{5,7},{6,8},{7,9},{8,10},{9,11},{10,... | collective-permute-start | bytes 786440 | tf_op jit(solution)/shard_map/ppermute | solution.py:187
  140.9 6.1 %collective-permute-done.15 = bf16[64,2048]{1,0:T(8,128)(2,1)S(1)} collective-permute-done((bf16[64,2048]{1,0:T(8,128)(2,1)S(1)}, bf16[64,2048]{1,0:T(8,128)(2,1)S(1)}, u32[]{:S(2)}, u32[]{:S(2)}) %collective-permute-start.15) | collective-permute-done | bytes 262176 | tf_op jit(solution)/shard_map/ppermute | solution.py:187
  147.2 7.6 %collective-permute-done.16 = bf16[64,2048]{1,0:T(8,128)(2,1)S(1)} collective-permute-done((bf16[64,2048]{1,0:T(8,128)(2,1)S(1)}, bf16[64,2048]{1,0:T(8,128)(2,1)S(1)}, u32[]{:S(2)}, u32[]{:S(2)}) %collective-permute-start.16) | collective-permute-done | bytes 262176 | tf_op jit(solution)/shard_map/ppermute | solution.py:187
  (34 shorter events, 18.2 us)
Async XLA Ops:
  1.1 9.1 %collective-permute-start = (bf16[64,2176]{1,0:T(8,128)(2,1)S(1)}, bf16[64,2176]{1,0:T(8,128)(2,1)S(1)}, u32[]{:S(2)}, u32[]{:S(2)}) collective-permute-start(bf16[64,2176]{1,0:T(8,128)(2,1)S(1)} %pack.1.refs_0_), channel_id=1, source_target_pairs={{0,2},{1,3},{2,4},{3,5},{4,6},{5,7},{6,8},{7,9},{8,10},{9,11},{10,... | collective-permute-start | bytes 835592 | tf_op jit(solution)/shard_map/ppermute | solution.py:187
  4.3 9.6 %collective-permute-start.1 = (bf16[64,2176]{1,0:T(8,128)(2,1)S(1)}, bf16[64,2176]{1,0:T(8,128)(2,1)S(1)}, u32[]{:S(2)}, u32[]{:S(2)}) collective-permute-start(bf16[64,2176]{1,0:T(8,128)(2,1)S(1)} %pack.1.refs_0_), channel_id=1, source_target_pairs={{0,14},{1,15},{2,0},{3,1},{4,2},{5,3},{6,4},{7,5},{8,6},{9,7},{10,... | collective-permute-start | bytes 835592 | tf_op jit(solution)/shard_map/ppermute | solution.py:187
  10.2 8.7 %collective-permute-start.2 = (bf16[64,2176]{1,0:T(8,128)(2,1)S(1)}, bf16[64,2176]{1,0:T(8,128)(2,1)S(1)}, u32[]{:S(2)}, u32[]{:S(2)}) collective-permute-start(bf16[64,2176]{1,0:T(8,128)(2,1)S(1)} %collective-permute-done.refs_1_), channel_id=1, source_target_pairs={{0,2},{1,3},{2,4},{3,5},{4,6},{5,7},{6,8},{7,9},{8,10},{9,11},{10,... | collective-permute-start | bytes 835592 | tf_op jit(solution)/shard_map/ppermute | solution.py:187
  13.9 8.5 %collective-permute-start.3 = (bf16[64,2176]{1,0:T(8,128)(2,1)S(1)}, bf16[64,2176]{1,0:T(8,128)(2,1)S(1)}, u32[]{:S(2)}, u32[]{:S(2)}) collective-permute-start(bf16[64,2176]{1,0:T(8,128)(2,1)S(1)} %collective-permute-done.1.refs_2_), channel_id=1, source_target_pairs={{0,14},{1,15},{2,0},{3,1},{4,2},{5,3},{6,4},{7,5},{8,6},{9,7},{10,... | collective-permute-start | bytes 835592 | tf_op jit(solution)/shard_map/ppermute | solution.py:187
  22.3 17.2 %copy-start = (bf16[1,2048,384]{2,1,0:T(8,128)(2,1)S(1)}, bf16[1,2048,384]{2,1,0:T(8,128)(2,1)}, u32[]{:S(2)}) copy-start(bf16[1,2048,384]{2,1,0:T(8,128)(2,1)} %param.9) | copy-start | bytes 4718596
  22.3 29.0 %all-to-all-start = ((bf16[16,24,2048]{2,1,0:T(8,128)(2,1)}), bf16[16,24,2048]{2,1,0:T(8,128)(2,1)}, u32[]{:S(2)}, u32[]{:S(2)}) async-start(bf16[16,24,2048]{2,1,0:T(8,128)(2,1)} %bitcast.28), calls=%async_computation | async-start | bytes 3145728 | tf_op jit(solution)/shard_map/all_to_all | solution.py:195
  29.6 7.4 %collective-permute-start.4 = (bf16[64,2176]{1,0:T(8,128)(2,1)S(1)}, bf16[64,2176]{1,0:T(8,128)(2,1)S(1)}, u32[]{:S(2)}, u32[]{:S(2)}) collective-permute-start(bf16[64,2176]{1,0:T(8,128)(2,1)S(1)} %collective-permute-done.2.refs_3_), channel_id=1, source_target_pairs={{0,2},{1,3},{2,4},{3,5},{4,6},{5,7},{6,8},{7,9},{8,10},{9,11},{10,... | collective-permute-start | bytes 835592 | tf_op jit(solution)/shard_map/ppermute | solution.py:187
  31.8 8.3 %collective-permute-start.5 = (bf16[64,2176]{1,0:T(8,128)(2,1)S(1)}, bf16[64,2176]{1,0:T(8,128)(2,1)S(1)}, u32[]{:S(2)}, u32[]{:S(2)}) collective-permute-start(bf16[64,2176]{1,0:T(8,128)(2,1)S(1)} %collective-permute-done.3.refs_0_), channel_id=1, source_target_pairs={{0,14},{1,15},{2,0},{3,1},{4,2},{5,3},{6,4},{7,5},{8,6},{9,7},{10,... | collective-permute-start | bytes 835592 | tf_op jit(solution)/shard_map/ppermute | solution.py:187
  37.0 6.6 %collective-permute-start.6 = (bf16[64,2176]{1,0:T(8,128)(2,1)S(1)}, bf16[64,2176]{1,0:T(8,128)(2,1)S(1)}, u32[]{:S(2)}, u32[]{:S(2)}) collective-permute-start(bf16[64,2176]{1,0:T(8,128)(2,1)S(1)} %collective-permute-done.4.refs_1_), channel_id=1, source_target_pairs={{0,2},{1,3},{2,4},{3,5},{4,6},{5,7},{6,8},{7,9},{8,10},{9,11},{10,... | collective-permute-start | bytes 835592 | tf_op jit(solution)/shard_map/ppermute | solution.py:187
  39.5 19.4 %collective-permute-start.7 = (bf16[2048,384]{1,0:T(8,128)(2,1)S(1)}, bf16[2048,384]{1,0:T(8,128)(2,1)}, u32[]{:S(2)}, u32[]{:S(2)}) collective-permute-start(bf16[2048,384]{1,0:T(8,128)(2,1)S(1)} %bitcast.19), channel_id=1, source_target_pairs={{0,1},{1,0},{2,3},{3,2},{4,5},{5,4},{6,7},{7,6},{8,9},{9,8},{10,11... | collective-permute-start | bytes 4718600 | tf_op jit(solution)/shard_map/ppermute | solution.py:192
  39.5 19.4 %collective-permute-start.8 = (bf16[2048,384]{1,0:T(8,128)(2,1)}, bf16[2048,384]{1,0:T(8,128)(2,1)}, u32[]{:S(2)}, u32[]{:S(2)}) collective-permute-start(bf16[2048,384]{1,0:T(8,128)(2,1)} %bitcast.20), channel_id=1, source_target_pairs={{0,1},{1,0},{2,3},{3,2},{4,5},{5,4},{6,7},{7,6},{8,9},{9,8},{10,11... | collective-permute-start | bytes 4718600 | tf_op jit(solution)/shard_map/ppermute | solution.py:192
  40.0 18.9 %collective-permute-start.9 = (bf16[384,2048]{1,0:T(8,128)(2,1)}, bf16[384,2048]{1,0:T(8,128)(2,1)}, u32[]{:S(2)}, u32[]{:S(2)}) collective-permute-start(bf16[384,2048]{1,0:T(8,128)(2,1)} %bitcast.23), channel_id=1, source_target_pairs={{0,1},{1,0},{2,3},{3,2},{4,5},{5,4},{6,7},{7,6},{8,9},{9,8},{10,11... | collective-permute-start | bytes 4718600 | tf_op jit(solution)/shard_map/ppermute | solution.py:192
  51.3 25.5 %all-to-all-start.1 = ((bf16[16,24,2048]{2,1,0:T(8,128)(2,1)}), bf16[16,24,2048]{2,1,0:T(8,128)(2,1)S(1)}, u32[]{:S(2)}, u32[]{:S(2)}) async-start(bf16[16,24,2048]{2,1,0:T(8,128)(2,1)} %bitcast.29), calls=%async_computation.1 | async-start | bytes 3145728 | tf_op jit(solution)/shard_map/all_to_all | solution.py:195
  109.8 25.4 %all-to-all-start.3 = ((bf16[16,24,2048]{2,1,0:T(8,128)(2,1)}), bf16[16,24,2048]{2,1,0:T(8,128)(2,1)S(1)}, u32[]{:S(2)}, u32[]{:S(2)}) async-start(bf16[16,24,2048]{2,1,0:T(8,128)(2,1)} %bitcast.26), calls=%async_computation.3 | async-start | bytes 3145728 | tf_op jit(solution)/shard_map/all_to_all | solution.py:195
  115.8 7.1 %collective-permute-start.12 = (bf16[64,2048]{1,0:T(8,128)(2,1)S(1)}, bf16[64,2048]{1,0:T(8,128)(2,1)S(1)}, u32[]{:S(2)}, u32[]{:S(2)}) collective-permute-start(bf16[64,2048]{1,0:T(8,128)(2,1)S(1)} %get-tuple-element.34), channel_id=1, source_target_pairs={{0,2},{1,3},{2,4},{3,5},{4,6},{5,7},{6,8},{7,9},{8,10},{9,11},{10,... | collective-permute-start | bytes 786440 | tf_op jit(solution)/shard_map/ppermute | solution.py:187
  117.9 7.7 %collective-permute-start.10 = (bf16[64,2048]{1,0:T(8,128)(2,1)S(1)}, bf16[64,2048]{1,0:T(8,128)(2,1)S(1)}, u32[]{:S(2)}, u32[]{:S(2)}) collective-permute-start(bf16[64,2048]{1,0:T(8,128)(2,1)S(1)} %get-tuple-element.32), channel_id=1, source_target_pairs={{0,14},{1,15},{2,0},{3,1},{4,2},{5,3},{6,4},{7,5},{8,6},{9,7},{10,... | collective-permute-start | bytes 786440 | tf_op jit(solution)/shard_map/ppermute | solution.py:187
  123.0 6.6 %collective-permute-start.13 = (bf16[64,2048]{1,0:T(8,128)(2,1)S(1)}, bf16[64,2048]{1,0:T(8,128)(2,1)S(1)}, u32[]{:S(2)}, u32[]{:S(2)}) collective-permute-start(bf16[64,2048]{1,0:T(8,128)(2,1)S(1)} %add_convert_fusion.3), channel_id=1, source_target_pairs={{0,2},{1,3},{2,4},{3,5},{4,6},{5,7},{6,8},{7,9},{8,10},{9,11},{10,... | collective-permute-start | bytes 786440 | tf_op jit(solution)/shard_map/ppermute | solution.py:187
  125.7 7.7 %collective-permute-start.11 = (bf16[64,2048]{1,0:T(8,128)(2,1)S(1)}, bf16[64,2048]{1,0:T(8,128)(2,1)S(1)}, u32[]{:S(2)}, u32[]{:S(2)}) collective-permute-start(bf16[64,2048]{1,0:T(8,128)(2,1)S(1)} %add_convert_fusion.4), channel_id=1, source_target_pairs={{0,14},{1,15},{2,0},{3,1},{4,2},{5,3},{6,4},{7,5},{8,6},{9,7},{10,... | collective-permute-start | bytes 786440 | tf_op jit(solution)/shard_map/ppermute | solution.py:187
  137.5 9.6 %collective-permute-start.15 = (bf16[64,2048]{1,0:T(8,128)(2,1)S(1)}, bf16[64,2048]{1,0:T(8,128)(2,1)S(1)}, u32[]{:S(2)}, u32[]{:S(2)}) collective-permute-start(bf16[64,2048]{1,0:T(8,128)(2,1)S(1)} %add_convert_fusion.1), channel_id=1, source_target_pairs={{0,14},{1,15},{2,0},{3,1},{4,2},{5,3},{6,4},{7,5},{8,6},{9,7},{10,... | collective-permute-start | bytes 786440 | tf_op jit(solution)/shard_map/ppermute | solution.py:187
  137.6 9.6 %collective-permute-start.14 = (bf16[64,2048]{1,0:T(8,128)(2,1)S(1)}, bf16[64,2048]{1,0:T(8,128)(2,1)S(1)}, u32[]{:S(2)}, u32[]{:S(2)}) collective-permute-start(bf16[64,2048]{1,0:T(8,128)(2,1)S(1)} %add_convert_fusion.2), channel_id=1, source_target_pairs={{0,2},{1,3},{2,4},{3,5},{4,6},{5,7},{6,8},{7,9},{8,10},{9,11},{10,... | collective-permute-start | bytes 786440 | tf_op jit(solution)/shard_map/ppermute | solution.py:187
  147.1 7.7 %collective-permute-start.16 = (bf16[64,2048]{1,0:T(8,128)(2,1)S(1)}, bf16[64,2048]{1,0:T(8,128)(2,1)S(1)}, u32[]{:S(2)}, u32[]{:S(2)}) collective-permute-start(bf16[64,2048]{1,0:T(8,128)(2,1)S(1)} %add_convert_fusion), channel_id=1, source_target_pairs={{0,14},{1,15},{2,0},{3,1},{4,2},{5,3},{6,4},{7,5},{8,6},{9,7},{10,... | collective-permute-start | bytes 786440 | tf_op jit(solution)/shard_map/ppermute | solution.py:187

commit v4 on v3

--- a/solution.py
+++ b/solution.py
@@ -209,14 +209,14 @@
             scratch=[pltpu.VMEM(*moved), pltpu.SemaphoreType.DMA((pieces,))],
         )
 
-    def mixing(extra):
+    def mixing(extra, where):
         return kernel_call(
             functools.partial(weights_kernel, slots, planes),
             "mixing",
             [((2 * chunk, sent), BF16)],
             [extra],
             [plane],
-            keep=[pltpu.HBM],
+            keep=[where],
         )[0]
 
     panels = []
@@ -267,15 +267,16 @@
     near = after(near, far_rows)
     far = exchange(far_rows)
     near_out = after(expert(near), far)
-    near_mix, far_mix = mixing(near_extra), mixing(far_extra)
-    far_out = after(expert(far), near_out, near_mix, far_mix)
+    far_mix = mixing(far_extra, pltpu.HBM)
+    far_out = after(expert(far), near_out, far_mix)
     far_home = exchange(far_out)
+    near_mix = mixing(after(near_extra, far_home), pltpu.VMEM)
     near_home = exchange(after(near_out, far_home))
     to_high_2, to_low_3, to_high_3, to_low_4 = combine(far_home, off_chip(far_mix), [F32, F32, BF16, BF16])
     down, up = along_z(to_low_4, -1), along_z(to_high_3, 1)
     down, up = along_z(plus(down, to_low_3), -1), along_z(plus(up, to_high_2), 1)
     near_home = after(near_home, down, up)
-    own, to_low_1, to_high_1, to_low_2 = combine(near_home, off_chip(near_mix), [F32] * 4)
+    own, to_low_1, to_high_1, to_low_2 = combine(near_home, near_mix, [F32] * 4)
     down, up = along_z(plus(down, to_low_2), -1), along_z(plus(up, to_high_1), 1)
     down = along_z(plus(down, to_low_1), -1)
     return own + up.astype(F32) + down.astype(F32)

time: 156 us -> 155 us (level)
  Pallas kernels: 29.8 us -> 28.1 us
    pallas_call x9, Pallas kernels: 29.8 us -> 28.1 us  [kernel_call(): pl.pallas_call(body, out_shape=[where(*out) for where, out in zip(keep, o...]
where the time goes in v4:
time: 155 us
  waiting for transfers between devices  64 us (41%)
  starting transfers between devices  35.8 us (23%)
  Pallas kernels  28.1 us (18%)
  blocking collectives  25.2 us (16%)
    ppermute x14, waiting for transfers between devices, along_z(): lax.ppermute(x, 'expert', [(i, (i + 2 * by) % col_count) for i in range(c...  46.1 us
    pallas_call x9, Pallas kernels, kernel_call(): pl.pallas_call(body, out_shape=[where(*out) for where, out in zip(keep, o...  28.1 us
    all_to_all x1, blocking collectives, exchange(): return lax.all_to_all(x, 'dp', split_axis=0, concat_axis=0, tiled=True)  25.2 us
    ppermute x14, starting transfers between devices, along_z(): lax.ppermute(x, 'expert', [(i, (i + 2 * by) % col_count) for i in range(c...  20.7 us
    all_to_all x3, waiting for transfers between devices, exchange(): return lax.all_to_all(x, 'dp', split_axis=0, concat_axis=0, tiled=True)  17.9 us
    all_to_all x3, starting transfers between devices, exchange(): return lax.all_to_all(x, 'dp', split_axis=0, concat_axis=0, tiled=True)  14.7 us
  transfers between devices with their start and end apart: 20, of which 13 were waited for; matrix products, arithmetic and copies ran while one was open for 0% of the time, Pallas kernels for 12%

profile of v4, /device:TPU:96, one launch (start us, length us, event | category | flops | bytes accessed | tf_op | source)
XLA Modules:
  0.0 154.6 jit_solution(3446232896488754815)
XLA Ops:
  1.1 3.2 %collective-permute-start = (bf16[64,2176]{1,0:T(8,128)(2,1)S(1)}, bf16[64,2176]{1,0:T(8,128)(2,1)S(1)}, u32[]{:S(2)}, u32[]{:S(2)}) collective-permute-start(bf16[64,2176]{1,0:T(8,128)(2,1)S(1)} %pack.1.refs_0_), channel_id=1, source_target_pairs={{0,2},{1,3},{2,4},{3,5},{4,6},{5,7},{6,8},{7,9},{8,10},{9,11},{10,... | collective-permute-start | bytes 835592 | tf_op jit(solution)/shard_map/ppermute | solution.py:187
  4.3 5.9 %collective-permute-done.refs_1_ = bf16[64,2176]{1,0:T(8,128)(2,1)S(1)} collective-permute-done((bf16[64,2176]{1,0:T(8,128)(2,1)S(1)}, bf16[64,2176]{1,0:T(8,128)(2,1)S(1)}, u32[]{:S(2)}, u32[]{:S(2)}) %collective-permute-start) | collective-permute-done | bytes 278560 | tf_op jit(solution)/shard_map/ppermute | solution.py:187
  10.2 3.7 %collective-permute-start.2 = (bf16[64,2176]{1,0:T(8,128)(2,1)S(1)}, bf16[64,2176]{1,0:T(8,128)(2,1)S(1)}, u32[]{:S(2)}, u32[]{:S(2)}) collective-permute-start(bf16[64,2176]{1,0:T(8,128)(2,1)S(1)} %collective-permute-done.refs_1_), channel_id=1, source_target_pairs={{0,2},{1,3},{2,4},{3,5},{4,6},{5,7},{6,8},{7,9},{8,10},{9,11},{10,... | collective-permute-start | bytes 835592 | tf_op jit(solution)/shard_map/ppermute | solution.py:187
  13.9 5.0 %collective-permute-done.2.refs_3_ = bf16[64,2176]{1,0:T(8,128)(2,1)S(1)} collective-permute-done((bf16[64,2176]{1,0:T(8,128)(2,1)S(1)}, bf16[64,2176]{1,0:T(8,128)(2,1)S(1)}, u32[]{:S(2)}, u32[]{:S(2)}) %collective-permute-start.2) | collective-permute-done | bytes 278560 | tf_op jit(solution)/shard_map/ppermute | solution.py:187
  22.3 7.1 %all-to-all-start = ((bf16[16,24,2048]{2,1,0:T(8,128)(2,1)}), bf16[16,24,2048]{2,1,0:T(8,128)(2,1)}, u32[]{:S(2)}, u32[]{:S(2)}) async-start(bf16[16,24,2048]{2,1,0:T(8,128)(2,1)} %bitcast.19), calls=%async_computation | async-start | bytes 3145728 | tf_op jit(solution)/shard_map/all_to_all | solution.py:195
  29.4 2.2 %collective-permute-start.4 = (bf16[64,2176]{1,0:T(8,128)(2,1)S(1)}, bf16[64,2176]{1,0:T(8,128)(2,1)S(1)}, u32[]{:S(2)}, u32[]{:S(2)}) collective-permute-start(bf16[64,2176]{1,0:T(8,128)(2,1)S(1)} %collective-permute-done.2.refs_3_), channel_id=1, source_target_pairs={{0,2},{1,3},{2,4},{3,5},{4,6},{5,7},{6,8},{7,9},{8,10},{9,11},{10,... | collective-permute-start | bytes 835592 | tf_op jit(solution)/shard_map/ppermute | solution.py:187
  31.7 5.1 %collective-permute-done.4.refs_1_ = bf16[64,2176]{1,0:T(8,128)(2,1)S(1)} collective-permute-done((bf16[64,2176]{1,0:T(8,128)(2,1)S(1)}, bf16[64,2176]{1,0:T(8,128)(2,1)S(1)}, u32[]{:S(2)}, u32[]{:S(2)}) %collective-permute-start.4) | collective-permute-done | bytes 278560 | tf_op jit(solution)/shard_map/ppermute | solution.py:187
  36.8 2.6 %collective-permute-start.6 = (bf16[64,2176]{1,0:T(8,128)(2,1)S(1)}, bf16[64,2176]{1,0:T(8,128)(2,1)S(1)}, u32[]{:S(2)}, u32[]{:S(2)}) collective-permute-start(bf16[64,2176]{1,0:T(8,128)(2,1)S(1)} %collective-permute-done.4.refs_1_), channel_id=1, source_target_pairs={{0,2},{1,3},{2,4},{3,5},{4,6},{5,7},{6,8},{7,9},{8,10},{9,11},{10,... | collective-permute-start | bytes 835592 | tf_op jit(solution)/shard_map/ppermute | solution.py:187
  40.0 3.5 %collective-permute-done.6.refs_3_ = bf16[64,2176]{1,0:T(8,128)(2,1)S(1)} collective-permute-done((bf16[64,2176]{1,0:T(8,128)(2,1)S(1)}, bf16[64,2176]{1,0:T(8,128)(2,1)S(1)}, u32[]{:S(2)}, u32[]{:S(2)}) %collective-permute-start.6) | collective-permute-done | bytes 278560 | tf_op jit(solution)/shard_map/ppermute | solution.py:187
  45.4 5.8 %all-to-all-done = bf16[16,24,2048]{2,1,0:T(8,128)(2,1)} async-done(((bf16[16,24,2048]{2,1,0:T(8,128)(2,1)}), bf16[16,24,2048]{2,1,0:T(8,128)(2,1)}, u32[]{:S(2)}, u32[]{:S(2)}) %all-to-all-start) | async-done | bytes 1572896 | tf_op jit(solution)/shard_map/all_to_all | solution.py:195
  51.2 3.9 %all-to-all-start.1 = ((bf16[16,24,2048]{2,1,0:T(8,128)(2,1)}), bf16[16,24,2048]{2,1,0:T(8,128)(2,1)S(1)}, u32[]{:S(2)}, u32[]{:S(2)}) async-start(bf16[16,24,2048]{2,1,0:T(8,128)(2,1)} %bitcast.20), calls=%async_computation.1 | async-start | bytes 3145728 | tf_op jit(solution)/shard_map/all_to_all | solution.py:195
  56.9 9.2 %expert.2 = bf16[384,2048]{1,0:T(8,128)(2,1)} custom-call(bf16[384,2048]{1,0:T(8,128)(2,1)} %bitcast.4.x_ref, bf16[2048,384]{1,0:T(8,128)(2,1)} %bitcast.5.g0, bf16[2048,384]{1,0:T(8,128)(2,1)} %bitcast.6.u0, bf16[2048,384]{1,0:T(8,128)(2,1)} %collective-permute-done.7.g1, bf16[2048,384]{1,0:T(8,128)(2,1)} %collective-permute-done.8.u1, ...), custom_call_target="tpu_custom_call" | custom-call | tf_op jit(solution)/shard_map/expert/pallas_call | solution.py:36
  66.1 10.6 %all-to-all-done.1 = bf16[16,24,2048]{2,1,0:T(8,128)(2,1)S(1)} async-done(((bf16[16,24,2048]{2,1,0:T(8,128)(2,1)}), bf16[16,24,2048]{2,1,0:T(8,128)(2,1)S(1)}, u32[]{:S(2)}, u32[]{:S(2)}) %all-to-all-start.1) | async-done | bytes 1572896 | tf_op jit(solution)/shard_map/all_to_all | solution.py:195
  76.7 7.7 %expert.3 = bf16[384,2048]{1,0:T(8,128)(2,1)} custom-call(bf16[384,2048]{1,0:T(8,128)(2,1)S(1)} %bitcast.14, bf16[2048,384]{1,0:T(8,128)(2,1)} %bitcast.5.g0, bf16[2048,384]{1,0:T(8,128)(2,1)} %bitcast.6.u0, bf16[2048,384]{1,0:T(8,128)(2,1)} %collective-permute-done.7.g1, bf16[2048,384]{1,0:T(8,128)(2,1)} %collective-permute-done.8.u1, ...), custom_call_target="tpu_custom_call" | custom-call | tf_op jit(solution)/shard_map/expert/pallas_call | solution.py:36
  84.5 25.2 %all_to_all.46 = bf16[16,24,2048]{2,1,0:T(8,128)(2,1)S(1)} all-to-all(bf16[16,24,2048]{2,1,0:T(8,128)(2,1)} %bitcast.18), channel_id=1, replica_groups=mesh['dp'=16,'expert'=16] {'dp'}, dimensions={0} | all-to-all | bytes 3145728 | tf_op jit(solution)/shard_map/all_to_all | solution.py:195
  109.7 3.7 %all-to-all-start.3 = ((bf16[16,24,2048]{2,1,0:T(8,128)(2,1)}), bf16[16,24,2048]{2,1,0:T(8,128)(2,1)S(1)}, u32[]{:S(2)}, u32[]{:S(2)}) async-start(bf16[16,24,2048]{2,1,0:T(8,128)(2,1)} %bitcast.17), calls=%async_computation.3 | async-start | bytes 3145728 | tf_op jit(solution)/shard_map/all_to_all | solution.py:195
  113.4 2.2 %combine.2 = (f32[64,2048]{1,0:T(8,128)S(1)}, f32[64,2048]{1,0:T(8,128)S(1)}, bf16[64,2048]{1,0:T(8,128)(2,1)S(1)}, bf16[64,2048]{1,0:T(8,128)(2,1)S(1)}) custom-call(bf16[384,2048]{1,0:T(8,128)(2,1)S(1)} %bitcast.16, bf16[512,384]{1,0:T(8,128)(2,1)} %mixing.2.mix_ref), custom_call_target="tpu_custom_call" | custom-call | tf_op jit(solution)/shard_map/combine/pallas_call | solution.py:36
  117.8 4.7 %collective-permute-done.12 = bf16[64,2048]{1,0:T(8,128)(2,1)S(1)} collective-permute-done((bf16[64,2048]{1,0:T(8,128)(2,1)S(1)}, bf16[64,2048]{1,0:T(8,128)(2,1)S(1)}, u32[]{:S(2)}, u32[]{:S(2)}) %collective-permute-start.12) | collective-permute-done | bytes 262176 | tf_op jit(solution)/shard_map/ppermute | solution.py:187
  122.6 3.2 %collective-permute-start.13 = (bf16[64,2048]{1,0:T(8,128)(2,1)S(1)}, bf16[64,2048]{1,0:T(8,128)(2,1)S(1)}, u32[]{:S(2)}, u32[]{:S(2)}) collective-permute-start(bf16[64,2048]{1,0:T(8,128)(2,1)S(1)} %add_convert_fusion.3), channel_id=1, source_target_pairs={{0,2},{1,3},{2,4},{3,5},{4,6},{5,7},{6,8},{7,9},{8,10},{9,11},{10,... | collective-permute-start | bytes 786440 | tf_op jit(solution)/shard_map/ppermute | solution.py:187
  127.0 2.7 %collective-permute-done.13 = bf16[64,2048]{1,0:T(8,128)(2,1)S(1)} collective-permute-done((bf16[64,2048]{1,0:T(8,128)(2,1)S(1)}, bf16[64,2048]{1,0:T(8,128)(2,1)S(1)}, u32[]{:S(2)}, u32[]{:S(2)}) %collective-permute-start.13) | collective-permute-done | bytes 262176 | tf_op jit(solution)/shard_map/ppermute | solution.py:187
  129.7 3.8 %collective-permute-done.11 = bf16[64,2048]{1,0:T(8,128)(2,1)S(1)} collective-permute-done((bf16[64,2048]{1,0:T(8,128)(2,1)S(1)}, bf16[64,2048]{1,0:T(8,128)(2,1)S(1)}, u32[]{:S(2)}, u32[]{:S(2)}) %collective-permute-start.11) | collective-permute-done | bytes 262176 | tf_op jit(solution)/shard_map/ppermute | solution.py:187
  136.5 3.3 %collective-permute-start.14 = (bf16[64,2048]{1,0:T(8,128)(2,1)S(1)}, bf16[64,2048]{1,0:T(8,128)(2,1)S(1)}, u32[]{:S(2)}, u32[]{:S(2)}) collective-permute-start(bf16[64,2048]{1,0:T(8,128)(2,1)S(1)} %add_convert_fusion.2), channel_id=1, source_target_pairs={{0,2},{1,3},{2,4},{3,5},{4,6},{5,7},{6,8},{7,9},{8,10},{9,11},{10,... | collective-permute-start | bytes 786440 | tf_op jit(solution)/shard_map/ppermute | solution.py:187
  139.8 6.1 %collective-permute-done.15 = bf16[64,2048]{1,0:T(8,128)(2,1)S(1)} collective-permute-done((bf16[64,2048]{1,0:T(8,128)(2,1)S(1)}, bf16[64,2048]{1,0:T(8,128)(2,1)S(1)}, u32[]{:S(2)}, u32[]{:S(2)}) %collective-permute-start.15) | collective-permute-done | bytes 262176 | tf_op jit(solution)/shard_map/ppermute | solution.py:187
  146.1 7.6 %collective-permute-done.16 = bf16[64,2048]{1,0:T(8,128)(2,1)S(1)} collective-permute-done((bf16[64,2048]{1,0:T(8,128)(2,1)S(1)}, bf16[64,2048]{1,0:T(8,128)(2,1)S(1)}, u32[]{:S(2)}, u32[]{:S(2)}) %collective-permute-start.16) | collective-permute-done | bytes 262176 | tf_op jit(solution)/shard_map/ppermute | solution.py:187
  (32 shorter events, 16.2 us)
Async XLA Ops:
  1.1 9.1 %collective-permute-start = (bf16[64,2176]{1,0:T(8,128)(2,1)S(1)}, bf16[64,2176]{1,0:T(8,128)(2,1)S(1)}, u32[]{:S(2)}, u32[]{:S(2)}) collective-permute-start(bf16[64,2176]{1,0:T(8,128)(2,1)S(1)} %pack.1.refs_0_), channel_id=1, source_target_pairs={{0,2},{1,3},{2,4},{3,5},{4,6},{5,7},{6,8},{7,9},{8,10},{9,11},{10,... | collective-permute-start | bytes 835592 | tf_op jit(solution)/shard_map/ppermute | solution.py:187
  4.3 9.6 %collective-permute-start.1 = (bf16[64,2176]{1,0:T(8,128)(2,1)S(1)}, bf16[64,2176]{1,0:T(8,128)(2,1)S(1)}, u32[]{:S(2)}, u32[]{:S(2)}) collective-permute-start(bf16[64,2176]{1,0:T(8,128)(2,1)S(1)} %pack.1.refs_0_), channel_id=1, source_target_pairs={{0,14},{1,15},{2,0},{3,1},{4,2},{5,3},{6,4},{7,5},{8,6},{9,7},{10,... | collective-permute-start | bytes 835592 | tf_op jit(solution)/shard_map/ppermute | solution.py:187
  10.2 8.7 %collective-permute-start.2 = (bf16[64,2176]{1,0:T(8,128)(2,1)S(1)}, bf16[64,2176]{1,0:T(8,128)(2,1)S(1)}, u32[]{:S(2)}, u32[]{:S(2)}) collective-permute-start(bf16[64,2176]{1,0:T(8,128)(2,1)S(1)} %collective-permute-done.refs_1_), channel_id=1, source_target_pairs={{0,2},{1,3},{2,4},{3,5},{4,6},{5,7},{6,8},{7,9},{8,10},{9,11},{10,... | collective-permute-start | bytes 835592 | tf_op jit(solution)/shard_map/ppermute | solution.py:187
  13.9 8.5 %collective-permute-start.3 = (bf16[64,2176]{1,0:T(8,128)(2,1)S(1)}, bf16[64,2176]{1,0:T(8,128)(2,1)S(1)}, u32[]{:S(2)}, u32[]{:S(2)}) collective-permute-start(bf16[64,2176]{1,0:T(8,128)(2,1)S(1)} %collective-permute-done.1.refs_2_), channel_id=1, source_target_pairs={{0,14},{1,15},{2,0},{3,1},{4,2},{5,3},{6,4},{7,5},{8,6},{9,7},{10,... | collective-permute-start | bytes 835592 | tf_op jit(solution)/shard_map/ppermute | solution.py:187
  22.3 28.8 %all-to-all-start = ((bf16[16,24,2048]{2,1,0:T(8,128)(2,1)}), bf16[16,24,2048]{2,1,0:T(8,128)(2,1)}, u32[]{:S(2)}, u32[]{:S(2)}) async-start(bf16[16,24,2048]{2,1,0:T(8,128)(2,1)} %bitcast.19), calls=%async_computation | async-start | bytes 3145728 | tf_op jit(solution)/shard_map/all_to_all | solution.py:195
  29.4 7.4 %collective-permute-start.4 = (bf16[64,2176]{1,0:T(8,128)(2,1)S(1)}, bf16[64,2176]{1,0:T(8,128)(2,1)S(1)}, u32[]{:S(2)}, u32[]{:S(2)}) collective-permute-start(bf16[64,2176]{1,0:T(8,128)(2,1)S(1)} %collective-permute-done.2.refs_3_), channel_id=1, source_target_pairs={{0,2},{1,3},{2,4},{3,5},{4,6},{5,7},{6,8},{7,9},{8,10},{9,11},{10,... | collective-permute-start | bytes 835592 | tf_op jit(solution)/shard_map/ppermute | solution.py:187
  31.7 8.3 %collective-permute-start.5 = (bf16[64,2176]{1,0:T(8,128)(2,1)S(1)}, bf16[64,2176]{1,0:T(8,128)(2,1)S(1)}, u32[]{:S(2)}, u32[]{:S(2)}) collective-permute-start(bf16[64,2176]{1,0:T(8,128)(2,1)S(1)} %collective-permute-done.3.refs_0_), channel_id=1, source_target_pairs={{0,14},{1,15},{2,0},{3,1},{4,2},{5,3},{6,4},{7,5},{8,6},{9,7},{10,... | collective-permute-start | bytes 835592 | tf_op jit(solution)/shard_map/ppermute | solution.py:187
  36.8 6.7 %collective-permute-start.6 = (bf16[64,2176]{1,0:T(8,128)(2,1)S(1)}, bf16[64,2176]{1,0:T(8,128)(2,1)S(1)}, u32[]{:S(2)}, u32[]{:S(2)}) collective-permute-start(bf16[64,2176]{1,0:T(8,128)(2,1)S(1)} %collective-permute-done.4.refs_1_), channel_id=1, source_target_pairs={{0,2},{1,3},{2,4},{3,5},{4,6},{5,7},{6,8},{7,9},{8,10},{9,11},{10,... | collective-permute-start | bytes 835592 | tf_op jit(solution)/shard_map/ppermute | solution.py:187
  39.4 17.5 %collective-permute-start.7 = (bf16[2048,384]{1,0:T(8,128)(2,1)}, bf16[2048,384]{1,0:T(8,128)(2,1)}, u32[]{:S(2)}, u32[]{:S(2)}) collective-permute-start(bf16[2048,384]{1,0:T(8,128)(2,1)} %bitcast.5.g0), channel_id=1, source_target_pairs={{0,1},{1,0},{2,3},{3,2},{4,5},{5,4},{6,7},{7,6},{8,9},{9,8},{10,11... | collective-permute-start | bytes 4718600 | tf_op jit(solution)/shard_map/ppermute | solution.py:192
  39.4 17.5 %collective-permute-start.8 = (bf16[2048,384]{1,0:T(8,128)(2,1)}, bf16[2048,384]{1,0:T(8,128)(2,1)}, u32[]{:S(2)}, u32[]{:S(2)}) collective-permute-start(bf16[2048,384]{1,0:T(8,128)(2,1)} %bitcast.6.u0), channel_id=1, source_target_pairs={{0,1},{1,0},{2,3},{3,2},{4,5},{5,4},{6,7},{7,6},{8,9},{9,8},{10,11... | collective-permute-start | bytes 4718600 | tf_op jit(solution)/shard_map/ppermute | solution.py:192
  39.9 17.0 %collective-permute-start.9 = (bf16[384,2048]{1,0:T(8,128)(2,1)}, bf16[384,2048]{1,0:T(8,128)(2,1)}, u32[]{:S(2)}, u32[]{:S(2)}) collective-permute-start(bf16[384,2048]{1,0:T(8,128)(2,1)} %bitcast.7.d0), channel_id=1, source_target_pairs={{0,1},{1,0},{2,3},{3,2},{4,5},{5,4},{6,7},{7,6},{8,9},{9,8},{10,11... | collective-permute-start | bytes 4718600 | tf_op jit(solution)/shard_map/ppermute | solution.py:192
  51.2 25.5 %all-to-all-start.1 = ((bf16[16,24,2048]{2,1,0:T(8,128)(2,1)}), bf16[16,24,2048]{2,1,0:T(8,128)(2,1)S(1)}, u32[]{:S(2)}, u32[]{:S(2)}) async-start(bf16[16,24,2048]{2,1,0:T(8,128)(2,1)} %bitcast.20), calls=%async_computation.1 | async-start | bytes 3145728 | tf_op jit(solution)/shard_map/all_to_all | solution.py:195
  109.7 25.4 %all-to-all-start.3 = ((bf16[16,24,2048]{2,1,0:T(8,128)(2,1)}), bf16[16,24,2048]{2,1,0:T(8,128)(2,1)S(1)}, u32[]{:S(2)}, u32[]{:S(2)}) async-start(bf16[16,24,2048]{2,1,0:T(8,128)(2,1)} %bitcast.17), calls=%async_computation.3 | async-start | bytes 3145728 | tf_op jit(solution)/shard_map/all_to_all | solution.py:195
  115.7 6.9 %collective-permute-start.12 = (bf16[64,2048]{1,0:T(8,128)(2,1)S(1)}, bf16[64,2048]{1,0:T(8,128)(2,1)S(1)}, u32[]{:S(2)}, u32[]{:S(2)}) collective-permute-start(bf16[64,2048]{1,0:T(8,128)(2,1)S(1)} %get-tuple-element.34), channel_id=1, source_target_pairs={{0,2},{1,3},{2,4},{3,5},{4,6},{5,7},{6,8},{7,9},{8,10},{9,11},{10,... | collective-permute-start | bytes 786440 | tf_op jit(solution)/shard_map/ppermute | solution.py:187
  117.8 7.9 %collective-permute-start.10 = (bf16[64,2048]{1,0:T(8,128)(2,1)S(1)}, bf16[64,2048]{1,0:T(8,128)(2,1)S(1)}, u32[]{:S(2)}, u32[]{:S(2)}) collective-permute-start(bf16[64,2048]{1,0:T(8,128)(2,1)S(1)} %get-tuple-element.32), channel_id=1, source_target_pairs={{0,14},{1,15},{2,0},{3,1},{4,2},{5,3},{6,4},{7,5},{8,6},{9,7},{10,... | collective-permute-start | bytes 786440 | tf_op jit(solution)/shard_map/ppermute | solution.py:187
  122.6 7.1 %collective-permute-start.13 = (bf16[64,2048]{1,0:T(8,128)(2,1)S(1)}, bf16[64,2048]{1,0:T(8,128)(2,1)S(1)}, u32[]{:S(2)}, u32[]{:S(2)}) collective-permute-start(bf16[64,2048]{1,0:T(8,128)(2,1)S(1)} %add_convert_fusion.3), channel_id=1, source_target_pairs={{0,2},{1,3},{2,4},{3,5},{4,6},{5,7},{6,8},{7,9},{8,10},{9,11},{10,... | collective-permute-start | bytes 786440 | tf_op jit(solution)/shard_map/ppermute | solution.py:187
  125.8 7.7 %collective-permute-start.11 = (bf16[64,2048]{1,0:T(8,128)(2,1)S(1)}, bf16[64,2048]{1,0:T(8,128)(2,1)S(1)}, u32[]{:S(2)}, u32[]{:S(2)}) collective-permute-start(bf16[64,2048]{1,0:T(8,128)(2,1)S(1)} %add_convert_fusion.4), channel_id=1, source_target_pairs={{0,14},{1,15},{2,0},{3,1},{4,2},{5,3},{6,4},{7,5},{8,6},{9,7},{10,... | collective-permute-start | bytes 786440 | tf_op jit(solution)/shard_map/ppermute | solution.py:187
  136.4 9.6 %collective-permute-start.15 = (bf16[64,2048]{1,0:T(8,128)(2,1)S(1)}, bf16[64,2048]{1,0:T(8,128)(2,1)S(1)}, u32[]{:S(2)}, u32[]{:S(2)}) collective-permute-start(bf16[64,2048]{1,0:T(8,128)(2,1)S(1)} %add_convert_fusion.1), channel_id=1, source_target_pairs={{0,14},{1,15},{2,0},{3,1},{4,2},{5,3},{6,4},{7,5},{8,6},{9,7},{10,... | collective-permute-start | bytes 786440 | tf_op jit(solution)/shard_map/ppermute | solution.py:187
  136.5 9.6 %collective-permute-start.14 = (bf16[64,2048]{1,0:T(8,128)(2,1)S(1)}, bf16[64,2048]{1,0:T(8,128)(2,1)S(1)}, u32[]{:S(2)}, u32[]{:S(2)}) collective-permute-start(bf16[64,2048]{1,0:T(8,128)(2,1)S(1)} %add_convert_fusion.2), channel_id=1, source_target_pairs={{0,2},{1,3},{2,4},{3,5},{4,6},{5,7},{6,8},{7,9},{8,10},{9,11},{10,... | collective-permute-start | bytes 786440 | tf_op jit(solution)/shard_map/ppermute | solution.py:187
  146.0 7.7 %collective-permute-start.16 = (bf16[64,2048]{1,0:T(8,128)(2,1)S(1)}, bf16[64,2048]{1,0:T(8,128)(2,1)S(1)}, u32[]{:S(2)}, u32[]{:S(2)}) collective-permute-start(bf16[64,2048]{1,0:T(8,128)(2,1)S(1)} %add_convert_fusion), channel_id=1, source_target_pairs={{0,14},{1,15},{2,0},{3,1},{4,2},{5,3},{6,4},{7,5},{8,6},{9,7},{10,... | collective-permute-start | bytes 786440 | tf_op jit(solution)/shard_map/ppermute | solution.py:187

commit v5 on v4

--- a/solution.py
+++ b/solution.py
@@ -272,7 +272,7 @@
     far_home = exchange(far_out)
     near_mix = mixing(after(near_extra, far_home), pltpu.VMEM)
     near_home = exchange(after(near_out, far_home))
-    to_high_2, to_low_3, to_high_3, to_low_4 = combine(far_home, off_chip(far_mix), [F32, F32, BF16, BF16])
+    to_high_2, to_low_3, to_high_3, to_low_4 = combine(far_home, far_mix, [F32, F32, BF16, BF16])
     down, up = along_z(to_low_4, -1), along_z(to_high_3, 1)
     down, up = along_z(plus(down, to_low_3), -1), along_z(plus(up, to_high_2), 1)
     near_home = after(near_home, down, up)

time: 155 us -> 155 us (level)
  starting transfers between devices: 35.8 us -> 38.8 us
  waiting for transfers between devices: 64 us -> 61.7 us
    ppermute x14, starting transfers between devices: 20.7 us -> 23.3 us  [along_z(): lax.ppermute(x, 'expert', [(i, (i + 2 * by) % col_count) for i in range(c...]
    ppermute x14, waiting for transfers between devices: 46.1 us -> 44 us  [along_z(): lax.ppermute(x, 'expert', [(i, (i + 2 * by) % col_count) for i in range(c...]
  transfers between devices with their start and end apart: 20 -> 20, of which waited for: 13 -> 13; matrix products, arithmetic and copies ran while one was open for 0% -> 0% of each run, Pallas kernels for 12% -> 11%
where the time goes in v5:
time: 155 us
  waiting for transfers between devices  61.7 us (40%)
  starting transfers between devices  38.8 us (25%)
  Pallas kernels  27.1 us (17%)
  blocking collectives  25.3 us (16%)
    ppermute x14, waiting for transfers between devices, along_z(): lax.ppermute(x, 'expert', [(i, (i + 2 * by) % col_count) for i in range(c...  44 us
    pallas_call x9, Pallas kernels, kernel_call(): pl.pallas_call(body, out_shape=[where(*out) for where, out in zip(keep, o...  27.1 us
    all_to_all x1, blocking collectives, exchange(): return lax.all_to_all(x, 'dp', split_axis=0, concat_axis=0, tiled=True)  25.3 us
    ppermute x14, starting transfers between devices, along_z(): lax.ppermute(x, 'expert', [(i, (i + 2 * by) % col_count) for i in range(c...  23.3 us
    all_to_all x3, waiting for transfers between devices, exchange(): return lax.all_to_all(x, 'dp', split_axis=0, concat_axis=0, tiled=True)  17.7 us
    all_to_all x3, starting transfers between devices, exchange(): return lax.all_to_all(x, 'dp', split_axis=0, concat_axis=0, tiled=True)  14.9 us
  transfers between devices with their start and end apart: 20, of which 13 were waited for; matrix products, arithmetic and copies ran while one was open for 0% of the time, Pallas kernels for 11%

profile of v5, /device:TPU:96, one launch (start us, length us, event | category | flops | bytes accessed | tf_op | source)
XLA Modules:
  0.0 154.8 jit_solution(12883408379367230315)
XLA Ops:
  1.1 3.2 %collective-permute-start = (bf16[64,2176]{1,0:T(8,128)(2,1)S(1)}, bf16[64,2176]{1,0:T(8,128)(2,1)S(1)}, u32[]{:S(2)}, u32[]{:S(2)}) collective-permute-start(bf16[64,2176]{1,0:T(8,128)(2,1)S(1)} %pack.1.refs_0_), channel_id=1, source_target_pairs={{0,2},{1,3},{2,4},{3,5},{4,6},{5,7},{6,8},{7,9},{8,10},{9,11},{10,... | collective-permute-start | bytes 835592 | tf_op jit(solution)/shard_map/ppermute | solution.py:187
  4.3 5.9 %collective-permute-done.refs_1_ = bf16[64,2176]{1,0:T(8,128)(2,1)S(1)} collective-permute-done((bf16[64,2176]{1,0:T(8,128)(2,1)S(1)}, bf16[64,2176]{1,0:T(8,128)(2,1)S(1)}, u32[]{:S(2)}, u32[]{:S(2)}) %collective-permute-start) | collective-permute-done | bytes 278560 | tf_op jit(solution)/shard_map/ppermute | solution.py:187
  10.2 3.7 %collective-permute-start.2 = (bf16[64,2176]{1,0:T(8,128)(2,1)S(1)}, bf16[64,2176]{1,0:T(8,128)(2,1)S(1)}, u32[]{:S(2)}, u32[]{:S(2)}) collective-permute-start(bf16[64,2176]{1,0:T(8,128)(2,1)S(1)} %collective-permute-done.refs_1_), channel_id=1, source_target_pairs={{0,2},{1,3},{2,4},{3,5},{4,6},{5,7},{6,8},{7,9},{8,10},{9,11},{10,... | collective-permute-start | bytes 835592 | tf_op jit(solution)/shard_map/ppermute | solution.py:187
  13.9 5.0 %collective-permute-done.2.refs_3_ = bf16[64,2176]{1,0:T(8,128)(2,1)S(1)} collective-permute-done((bf16[64,2176]{1,0:T(8,128)(2,1)S(1)}, bf16[64,2176]{1,0:T(8,128)(2,1)S(1)}, u32[]{:S(2)}, u32[]{:S(2)}) %collective-permute-start.2) | collective-permute-done | bytes 278560 | tf_op jit(solution)/shard_map/ppermute | solution.py:187
  22.3 7.2 %all-to-all-start = ((bf16[16,24,2048]{2,1,0:T(8,128)(2,1)}), bf16[16,24,2048]{2,1,0:T(8,128)(2,1)}, u32[]{:S(2)}, u32[]{:S(2)}) async-start(bf16[16,24,2048]{2,1,0:T(8,128)(2,1)} %bitcast.28), calls=%async_computation | async-start | bytes 3145728 | tf_op jit(solution)/shard_map/all_to_all | solution.py:195
  29.6 2.8 %collective-permute-start.4 = (bf16[64,2176]{1,0:T(8,128)(2,1)S(1)}, bf16[64,2176]{1,0:T(8,128)(2,1)S(1)}, u32[]{:S(2)}, u32[]{:S(2)}) collective-permute-start(bf16[64,2176]{1,0:T(8,128)(2,1)S(1)} %collective-permute-done.2.refs_3_), channel_id=1, source_target_pairs={{0,2},{1,3},{2,4},{3,5},{4,6},{5,7},{6,8},{7,9},{8,10},{9,11},{10,... | collective-permute-start | bytes 835592 | tf_op jit(solution)/shard_map/ppermute | solution.py:187
  32.4 4.1 %collective-permute-done.4.refs_1_ = bf16[64,2176]{1,0:T(8,128)(2,1)S(1)} collective-permute-done((bf16[64,2176]{1,0:T(8,128)(2,1)S(1)}, bf16[64,2176]{1,0:T(8,128)(2,1)S(1)}, u32[]{:S(2)}, u32[]{:S(2)}) %collective-permute-start.4) | collective-permute-done | bytes 278560 | tf_op jit(solution)/shard_map/ppermute | solution.py:187
  36.5 3.7 %collective-permute-start.6 = (bf16[64,2176]{1,0:T(8,128)(2,1)S(1)}, bf16[64,2176]{1,0:T(8,128)(2,1)S(1)}, u32[]{:S(2)}, u32[]{:S(2)}) collective-permute-start(bf16[64,2176]{1,0:T(8,128)(2,1)S(1)} %collective-permute-done.4.refs_1_), channel_id=1, source_target_pairs={{0,2},{1,3},{2,4},{3,5},{4,6},{5,7},{6,8},{7,9},{8,10},{9,11},{10,... | collective-permute-start | bytes 835592 | tf_op jit(solution)/shard_map/ppermute | solution.py:187
  40.7 3.5 %collective-permute-done.6.refs_3_ = bf16[64,2176]{1,0:T(8,128)(2,1)S(1)} collective-permute-done((bf16[64,2176]{1,0:T(8,128)(2,1)S(1)}, bf16[64,2176]{1,0:T(8,128)(2,1)S(1)}, u32[]{:S(2)}, u32[]{:S(2)}) %collective-permute-start.6) | collective-permute-done | bytes 278560 | tf_op jit(solution)/shard_map/ppermute | solution.py:187
  46.1 5.2 %all-to-all-done = bf16[16,24,2048]{2,1,0:T(8,128)(2,1)} async-done(((bf16[16,24,2048]{2,1,0:T(8,128)(2,1)}), bf16[16,24,2048]{2,1,0:T(8,128)(2,1)}, u32[]{:S(2)}, u32[]{:S(2)}) %all-to-all-start) | async-done | bytes 1572896 | tf_op jit(solution)/shard_map/all_to_all | solution.py:195
  51.3 3.9 %all-to-all-start.1 = ((bf16[16,24,2048]{2,1,0:T(8,128)(2,1)}), bf16[16,24,2048]{2,1,0:T(8,128)(2,1)S(1)}, u32[]{:S(2)}, u32[]{:S(2)}) async-start(bf16[16,24,2048]{2,1,0:T(8,128)(2,1)} %bitcast.29), calls=%async_computation.1 | async-start | bytes 3145728 | tf_op jit(solution)/shard_map/all_to_all | solution.py:195
  57.1 9.2 %expert.2 = bf16[384,2048]{1,0:T(8,128)(2,1)} custom-call(bf16[384,2048]{1,0:T(8,128)(2,1)} %bitcast.4.x_ref, bf16[2048,384]{1,0:T(8,128)(2,1)} %bitcast.17, bf16[2048,384]{1,0:T(8,128)(2,1)} %bitcast.21, bf16[2048,384]{1,0:T(8,128)(2,1)} %collective-permute-done.7.g1, bf16[2048,384]{1,0:T(8,128)(2,1)} %collective-permute-done.8.u1, ...), custom_call_target="tpu_custom_call" | custom-call | tf_op jit(solution)/shard_map/expert/pallas_call | solution.py:36
  66.2 10.6 %all-to-all-done.1 = bf16[16,24,2048]{2,1,0:T(8,128)(2,1)S(1)} async-done(((bf16[16,24,2048]{2,1,0:T(8,128)(2,1)}), bf16[16,24,2048]{2,1,0:T(8,128)(2,1)S(1)}, u32[]{:S(2)}, u32[]{:S(2)}) %all-to-all-start.1) | async-done | bytes 1572896 | tf_op jit(solution)/shard_map/all_to_all | solution.py:195
  76.8 7.8 %expert.3 = bf16[384,2048]{1,0:T(8,128)(2,1)} custom-call(bf16[384,2048]{1,0:T(8,128)(2,1)S(1)} %bitcast.14, bf16[2048,384]{1,0:T(8,128)(2,1)} %bitcast.18, bf16[2048,384]{1,0:T(8,128)(2,1)} %bitcast.22, bf16[2048,384]{1,0:T(8,128)(2,1)} %collective-permute-done.7.g1, bf16[2048,384]{1,0:T(8,128)(2,1)} %collective-permute-done.8.u1, ...), custom_call_target="tpu_custom_call" | custom-call | tf_op jit(solution)/shard_map/expert/pallas_call | solution.py:36
  84.6 25.3 %all_to_all.46 = bf16[16,24,2048]{2,1,0:T(8,128)(2,1)S(1)} all-to-all(bf16[16,24,2048]{2,1,0:T(8,128)(2,1)} %bitcast.27), channel_id=1, replica_groups=mesh['dp'=16,'expert'=16] {'dp'}, dimensions={0} | all-to-all | bytes 3145728 | tf_op jit(solution)/shard_map/all_to_all | solution.py:195
  109.9 3.8 %all-to-all-start.3 = ((bf16[16,24,2048]{2,1,0:T(8,128)(2,1)}), bf16[16,24,2048]{2,1,0:T(8,128)(2,1)S(1)}, u32[]{:S(2)}, u32[]{:S(2)}) async-start(bf16[16,24,2048]{2,1,0:T(8,128)(2,1)} %bitcast.26), calls=%async_computation.3 | async-start | bytes 3145728 | tf_op jit(solution)/shard_map/all_to_all | solution.py:195
  115.0 2.8 %collective-permute-start.12 = (bf16[64,2048]{1,0:T(8,128)(2,1)S(1)}, bf16[64,2048]{1,0:T(8,128)(2,1)S(1)}, u32[]{:S(2)}, u32[]{:S(2)}) collective-permute-start(bf16[64,2048]{1,0:T(8,128)(2,1)S(1)} %get-tuple-element.34), channel_id=1, source_target_pairs={{0,2},{1,3},{2,4},{3,5},{4,6},{5,7},{6,8},{7,9},{8,10},{9,11},{10,... | collective-permute-start | bytes 786440 | tf_op jit(solution)/shard_map/ppermute | solution.py:187
  117.7 4.3 %collective-permute-done.12 = bf16[64,2048]{1,0:T(8,128)(2,1)S(1)} collective-permute-done((bf16[64,2048]{1,0:T(8,128)(2,1)S(1)}, bf16[64,2048]{1,0:T(8,128)(2,1)S(1)}, u32[]{:S(2)}, u32[]{:S(2)}) %collective-permute-start.12) | collective-permute-done | bytes 262176 | tf_op jit(solution)/shard_map/ppermute | solution.py:187
  122.1 3.6 %collective-permute-start.13 = (bf16[64,2048]{1,0:T(8,128)(2,1)S(1)}, bf16[64,2048]{1,0:T(8,128)(2,1)S(1)}, u32[]{:S(2)}, u32[]{:S(2)}) collective-permute-start(bf16[64,2048]{1,0:T(8,128)(2,1)S(1)} %add_convert_fusion.3), channel_id=1, source_target_pairs={{0,2},{1,3},{2,4},{3,5},{4,6},{5,7},{6,8},{7,9},{8,10},{9,11},{10,... | collective-permute-start | bytes 786440 | tf_op jit(solution)/shard_map/ppermute | solution.py:187
  126.9 2.7 %collective-permute-done.13 = bf16[64,2048]{1,0:T(8,128)(2,1)S(1)} collective-permute-done((bf16[64,2048]{1,0:T(8,128)(2,1)S(1)}, bf16[64,2048]{1,0:T(8,128)(2,1)S(1)}, u32[]{:S(2)}, u32[]{:S(2)}) %collective-permute-start.13) | collective-permute-done | bytes 262176 | tf_op jit(solution)/shard_map/ppermute | solution.py:187
  129.6 3.8 %collective-permute-done.11 = bf16[64,2048]{1,0:T(8,128)(2,1)S(1)} collective-permute-done((bf16[64,2048]{1,0:T(8,128)(2,1)S(1)}, bf16[64,2048]{1,0:T(8,128)(2,1)S(1)}, u32[]{:S(2)}, u32[]{:S(2)}) %collective-permute-start.11) | collective-permute-done | bytes 262176 | tf_op jit(solution)/shard_map/ppermute | solution.py:187
  136.8 3.3 %collective-permute-start.14 = (bf16[64,2048]{1,0:T(8,128)(2,1)S(1)}, bf16[64,2048]{1,0:T(8,128)(2,1)S(1)}, u32[]{:S(2)}, u32[]{:S(2)}) collective-permute-start(bf16[64,2048]{1,0:T(8,128)(2,1)S(1)} %add_convert_fusion.2), channel_id=1, source_target_pairs={{0,2},{1,3},{2,4},{3,5},{4,6},{5,7},{6,8},{7,9},{8,10},{9,11},{10,... | collective-permute-start | bytes 786440 | tf_op jit(solution)/shard_map/ppermute | solution.py:187
  140.1 6.1 %collective-permute-done.15 = bf16[64,2048]{1,0:T(8,128)(2,1)S(1)} collective-permute-done((bf16[64,2048]{1,0:T(8,128)(2,1)S(1)}, bf16[64,2048]{1,0:T(8,128)(2,1)S(1)}, u32[]{:S(2)}, u32[]{:S(2)}) %collective-permute-start.15) | collective-permute-done | bytes 262176 | tf_op jit(solution)/shard_map/ppermute | solution.py:187
  146.4 7.6 %collective-permute-done.16 = bf16[64,2048]{1,0:T(8,128)(2,1)S(1)} collective-permute-done((bf16[64,2048]{1,0:T(8,128)(2,1)S(1)}, bf16[64,2048]{1,0:T(8,128)(2,1)S(1)}, u32[]{:S(2)}, u32[]{:S(2)}) %collective-permute-start.16) | collective-permute-done | bytes 262176 | tf_op jit(solution)/shard_map/ppermute | solution.py:187
  (40 shorter events, 15.6 us)
Async XLA Ops:
  1.1 9.1 %collective-permute-start = (bf16[64,2176]{1,0:T(8,128)(2,1)S(1)}, bf16[64,2176]{1,0:T(8,128)(2,1)S(1)}, u32[]{:S(2)}, u32[]{:S(2)}) collective-permute-start(bf16[64,2176]{1,0:T(8,128)(2,1)S(1)} %pack.1.refs_0_), channel_id=1, source_target_pairs={{0,2},{1,3},{2,4},{3,5},{4,6},{5,7},{6,8},{7,9},{8,10},{9,11},{10,... | collective-permute-start | bytes 835592 | tf_op jit(solution)/shard_map/ppermute | solution.py:187
  4.3 9.6 %collective-permute-start.1 = (bf16[64,2176]{1,0:T(8,128)(2,1)S(1)}, bf16[64,2176]{1,0:T(8,128)(2,1)S(1)}, u32[]{:S(2)}, u32[]{:S(2)}) collective-permute-start(bf16[64,2176]{1,0:T(8,128)(2,1)S(1)} %pack.1.refs_0_), channel_id=1, source_target_pairs={{0,14},{1,15},{2,0},{3,1},{4,2},{5,3},{6,4},{7,5},{8,6},{9,7},{10,... | collective-permute-start | bytes 835592 | tf_op jit(solution)/shard_map/ppermute | solution.py:187
  10.2 8.7 %collective-permute-start.2 = (bf16[64,2176]{1,0:T(8,128)(2,1)S(1)}, bf16[64,2176]{1,0:T(8,128)(2,1)S(1)}, u32[]{:S(2)}, u32[]{:S(2)}) collective-permute-start(bf16[64,2176]{1,0:T(8,128)(2,1)S(1)} %collective-permute-done.refs_1_), channel_id=1, source_target_pairs={{0,2},{1,3},{2,4},{3,5},{4,6},{5,7},{6,8},{7,9},{8,10},{9,11},{10,... | collective-permute-start | bytes 835592 | tf_op jit(solution)/shard_map/ppermute | solution.py:187
  13.9 8.5 %collective-permute-start.3 = (bf16[64,2176]{1,0:T(8,128)(2,1)S(1)}, bf16[64,2176]{1,0:T(8,128)(2,1)S(1)}, u32[]{:S(2)}, u32[]{:S(2)}) collective-permute-start(bf16[64,2176]{1,0:T(8,128)(2,1)S(1)} %collective-permute-done.1.refs_2_), channel_id=1, source_target_pairs={{0,14},{1,15},{2,0},{3,1},{4,2},{5,3},{6,4},{7,5},{8,6},{9,7},{10,... | collective-permute-start | bytes 835592 | tf_op jit(solution)/shard_map/ppermute | solution.py:187
  20.8 0.6 copy-start.1
  22.3 17.8 %copy-start.3 = (bf16[1,2048,384]{2,1,0:T(8,128)(2,1)S(1)}, bf16[1,2048,384]{2,1,0:T(8,128)(2,1)}, u32[]{:S(2)}) copy-start(bf16[1,2048,384]{2,1,0:T(8,128)(2,1)} %param.9) | copy-start | bytes 4718596
  22.3 29.0 %all-to-all-start = ((bf16[16,24,2048]{2,1,0:T(8,128)(2,1)}), bf16[16,24,2048]{2,1,0:T(8,128)(2,1)}, u32[]{:S(2)}, u32[]{:S(2)}) async-start(bf16[16,24,2048]{2,1,0:T(8,128)(2,1)} %bitcast.28), calls=%async_computation | async-start | bytes 3145728 | tf_op jit(solution)/shard_map/all_to_all | solution.py:195
  29.6 6.9 %collective-permute-start.4 = (bf16[64,2176]{1,0:T(8,128)(2,1)S(1)}, bf16[64,2176]{1,0:T(8,128)(2,1)S(1)}, u32[]{:S(2)}, u32[]{:S(2)}) collective-permute-start(bf16[64,2176]{1,0:T(8,128)(2,1)S(1)} %collective-permute-done.2.refs_3_), channel_id=1, source_target_pairs={{0,2},{1,3},{2,4},{3,5},{4,6},{5,7},{6,8},{7,9},{8,10},{9,11},{10,... | collective-permute-start | bytes 835592 | tf_op jit(solution)/shard_map/ppermute | solution.py:187
  32.4 8.3 %collective-permute-start.5 = (bf16[64,2176]{1,0:T(8,128)(2,1)S(1)}, bf16[64,2176]{1,0:T(8,128)(2,1)S(1)}, u32[]{:S(2)}, u32[]{:S(2)}) collective-permute-start(bf16[64,2176]{1,0:T(8,128)(2,1)S(1)} %collective-permute-done.3.refs_0_), channel_id=1, source_target_pairs={{0,14},{1,15},{2,0},{3,1},{4,2},{5,3},{6,4},{7,5},{8,6},{9,7},{10,... | collective-permute-start | bytes 835592 | tf_op jit(solution)/shard_map/ppermute | solution.py:187
  36.5 7.8 %collective-permute-start.6 = (bf16[64,2176]{1,0:T(8,128)(2,1)S(1)}, bf16[64,2176]{1,0:T(8,128)(2,1)S(1)}, u32[]{:S(2)}, u32[]{:S(2)}) collective-permute-start(bf16[64,2176]{1,0:T(8,128)(2,1)S(1)} %collective-permute-done.4.refs_1_), channel_id=1, source_target_pairs={{0,2},{1,3},{2,4},{3,5},{4,6},{5,7},{6,8},{7,9},{8,10},{9,11},{10,... | collective-permute-start | bytes 835592 | tf_op jit(solution)/shard_map/ppermute | solution.py:187
  40.2 16.9 %collective-permute-start.7 = (bf16[2048,384]{1,0:T(8,128)(2,1)S(1)}, bf16[2048,384]{1,0:T(8,128)(2,1)}, u32[]{:S(2)}, u32[]{:S(2)}) collective-permute-start(bf16[2048,384]{1,0:T(8,128)(2,1)S(1)} %bitcast.19), channel_id=1, source_target_pairs={{0,1},{1,0},{2,3},{3,2},{4,5},{5,4},{6,7},{7,6},{8,9},{9,8},{10,11... | collective-permute-start | bytes 4718600 | tf_op jit(solution)/shard_map/ppermute | solution.py:192
  40.2 16.9 %collective-permute-start.8 = (bf16[2048,384]{1,0:T(8,128)(2,1)}, bf16[2048,384]{1,0:T(8,128)(2,1)}, u32[]{:S(2)}, u32[]{:S(2)}) collective-permute-start(bf16[2048,384]{1,0:T(8,128)(2,1)} %bitcast.20), channel_id=1, source_target_pairs={{0,1},{1,0},{2,3},{3,2},{4,5},{5,4},{6,7},{7,6},{8,9},{9,8},{10,11... | collective-permute-start | bytes 4718600 | tf_op jit(solution)/shard_map/ppermute | solution.py:192
  40.7 16.4 %collective-permute-start.9 = (bf16[384,2048]{1,0:T(8,128)(2,1)}, bf16[384,2048]{1,0:T(8,128)(2,1)}, u32[]{:S(2)}, u32[]{:S(2)}) collective-permute-start(bf16[384,2048]{1,0:T(8,128)(2,1)} %bitcast.23), channel_id=1, source_target_pairs={{0,1},{1,0},{2,3},{3,2},{4,5},{5,4},{6,7},{7,6},{8,9},{9,8},{10,11... | collective-permute-start | bytes 4718600 | tf_op jit(solution)/shard_map/ppermute | solution.py:192
  51.3 25.5 %all-to-all-start.1 = ((bf16[16,24,2048]{2,1,0:T(8,128)(2,1)}), bf16[16,24,2048]{2,1,0:T(8,128)(2,1)S(1)}, u32[]{:S(2)}, u32[]{:S(2)}) async-start(bf16[16,24,2048]{2,1,0:T(8,128)(2,1)} %bitcast.29), calls=%async_computation.1 | async-start | bytes 3145728 | tf_op jit(solution)/shard_map/all_to_all | solution.py:195
  109.9 3.9 %copy-start = (bf16[512,384]{1,0:T(8,128)(2,1)S(1)}, bf16[512,384]{1,0:T(8,128)(2,1)}, u32[]{:S(2)}) copy-start(bf16[512,384]{1,0:T(8,128)(2,1)} %mixing.2.mix_ref) | copy-start | bytes 1179652
  109.9 25.5 %all-to-all-start.3 = ((bf16[16,24,2048]{2,1,0:T(8,128)(2,1)}), bf16[16,24,2048]{2,1,0:T(8,128)(2,1)S(1)}, u32[]{:S(2)}, u32[]{:S(2)}) async-start(bf16[16,24,2048]{2,1,0:T(8,128)(2,1)} %bitcast.26), calls=%async_computation.3 | async-start | bytes 3145728 | tf_op jit(solution)/shard_map/all_to_all | solution.py:195
  113.7 12.1 %copy-start.2 = (bf16[256,128]{1,0:T(8,128)(2,1)S(1)}, bf16[256,128]{1,0:T(8,128)(2,1)}, u32[]{:S(2)}) copy-start(bf16[256,128]{1,0:T(8,128)(2,1)} %copy-done.1) | copy-start | bytes 196612
  115.0 7.1 %collective-permute-start.12 = (bf16[64,2048]{1,0:T(8,128)(2,1)S(1)}, bf16[64,2048]{1,0:T(8,128)(2,1)S(1)}, u32[]{:S(2)}, u32[]{:S(2)}) collective-permute-start(bf16[64,2048]{1,0:T(8,128)(2,1)S(1)} %get-tuple-element.34), channel_id=1, source_target_pairs={{0,2},{1,3},{2,4},{3,5},{4,6},{5,7},{6,8},{7,9},{8,10},{9,11},{10,... | collective-permute-start | bytes 786440 | tf_op jit(solution)/shard_map/ppermute | solution.py:187
  117.7 7.9 %collective-permute-start.10 = (bf16[64,2048]{1,0:T(8,128)(2,1)S(1)}, bf16[64,2048]{1,0:T(8,128)(2,1)S(1)}, u32[]{:S(2)}, u32[]{:S(2)}) collective-permute-start(bf16[64,2048]{1,0:T(8,128)(2,1)S(1)} %get-tuple-element.32), channel_id=1, source_target_pairs={{0,14},{1,15},{2,0},{3,1},{4,2},{5,3},{6,4},{7,5},{8,6},{9,7},{10,... | collective-permute-start | bytes 786440 | tf_op jit(solution)/shard_map/ppermute | solution.py:187
  122.1 7.5 %collective-permute-start.13 = (bf16[64,2048]{1,0:T(8,128)(2,1)S(1)}, bf16[64,2048]{1,0:T(8,128)(2,1)S(1)}, u32[]{:S(2)}, u32[]{:S(2)}) collective-permute-start(bf16[64,2048]{1,0:T(8,128)(2,1)S(1)} %add_convert_fusion.3), channel_id=1, source_target_pairs={{0,2},{1,3},{2,4},{3,5},{4,6},{5,7},{6,8},{7,9},{8,10},{9,11},{10,... | collective-permute-start | bytes 786440 | tf_op jit(solution)/shard_map/ppermute | solution.py:187
  125.7 7.7 %collective-permute-start.11 = (bf16[64,2048]{1,0:T(8,128)(2,1)S(1)}, bf16[64,2048]{1,0:T(8,128)(2,1)S(1)}, u32[]{:S(2)}, u32[]{:S(2)}) collective-permute-start(bf16[64,2048]{1,0:T(8,128)(2,1)S(1)} %add_convert_fusion.4), channel_id=1, source_target_pairs={{0,14},{1,15},{2,0},{3,1},{4,2},{5,3},{6,4},{7,5},{8,6},{9,7},{10,... | collective-permute-start | bytes 786440 | tf_op jit(solution)/shard_map/ppermute | solution.py:187
  136.6 9.6 %collective-permute-start.15 = (bf16[64,2048]{1,0:T(8,128)(2,1)S(1)}, bf16[64,2048]{1,0:T(8,128)(2,1)S(1)}, u32[]{:S(2)}, u32[]{:S(2)}) collective-permute-start(bf16[64,2048]{1,0:T(8,128)(2,1)S(1)} %add_convert_fusion.1), channel_id=1, source_target_pairs={{0,14},{1,15},{2,0},{3,1},{4,2},{5,3},{6,4},{7,5},{8,6},{9,7},{10,... | collective-permute-start | bytes 786440 | tf_op jit(solution)/shard_map/ppermute | solution.py:187
  136.8 9.6 %collective-permute-start.14 = (bf16[64,2048]{1,0:T(8,128)(2,1)S(1)}, bf16[64,2048]{1,0:T(8,128)(2,1)S(1)}, u32[]{:S(2)}, u32[]{:S(2)}) collective-permute-start(bf16[64,2048]{1,0:T(8,128)(2,1)S(1)} %add_convert_fusion.2), channel_id=1, source_target_pairs={{0,2},{1,3},{2,4},{3,5},{4,6},{5,7},{6,8},{7,9},{8,10},{9,11},{10,... | collective-permute-start | bytes 786440 | tf_op jit(solution)/shard_map/ppermute | solution.py:187
  146.3 7.7 %collective-permute-start.16 = (bf16[64,2048]{1,0:T(8,128)(2,1)S(1)}, bf16[64,2048]{1,0:T(8,128)(2,1)S(1)}, u32[]{:S(2)}, u32[]{:S(2)}) collective-permute-start(bf16[64,2048]{1,0:T(8,128)(2,1)S(1)} %add_convert_fusion), channel_id=1, source_target_pairs={{0,14},{1,15},{2,0},{3,1},{4,2},{5,3},{6,4},{7,5},{8,6},{9,7},{10,... | collective-permute-start | bytes 786440 | tf_op jit(solution)/shard_map/ppermute | solution.py:187
